TPU v7x, 32 devices: a whole 2x2x4 slice. The times are simulated.
32 devices in a mesh: dp: 4 (over x, core), row: 4 (over z), col: 2 (over y).
Axes of the slice: x: 2, y: 2, z: 4, core: 2. Of those that a mesh axis runs over, the one named last changes fastest.
Arguments:
- hidden: bfloat16 [16384, 1024], P(('dp', 'col'), 'row')
- memory: bfloat16 [8192, 1024], P(('dp', 'col'), 'row')
- compressed: bfloat16 [8192, 1024], P(('dp', 'col'), 'row')
- seg_ids: int32 [16384], P(('dp', 'row')), may hold values from -1 to 32767, as said below
- positions: int32 [16384], P(('dp', 'row')), may hold values from 0 to 1022, as said below
- keep_mask: int32 [16384], P(('dp', 'row')), may hold values from 0 to 1
- mem_seg: int32 [16384], P(('dp', 'row')), may hold values from 0 to 32767, as said below
- cotangent: bfloat16 [16384, 1024], P(('dp', 'col'), 'row'), may hold values from -6 to 6
- w_qkv: float32 [1024, 3, 8, 128], P('row', None, 'col', 'dp'), may hold values from -0.1875 to 0.1875
- w_out: float32 [8, 128, 1024], P('col', 'dp', 'row'), may hold values from -1 to 1
- w_up: float32 [1024, 4096], P('row', ('dp', 'col')), may hold values from -0.1875 to 0.1875
- w_down: float32 [4096, 1024], P(('dp', 'col'), 'row'), may hold values from -0.09375 to 0.09375
- norm_attn: float32 [1024], P('row'), may hold values from 0.5 to 1.5
- norm_ffn: float32 [1024], P('row'), may hold values from 0.5 to 1.5
- conv_w: float32 [3, 1024], P(None, 'row'), may hold values from -3.5 to 3.5
Outputs:
- out: bfloat16 [16384, 1024], P(('dp', 'col'), 'row')
- d_hidden: bfloat16 [16384, 1024], P(('dp', 'col'), 'row')
- grad_w_qkv: float32 [1024, 3, 8, 128], P('row', None, 'col', 'dp')
- grad_w_out: float32 [8, 128, 1024], P('col', 'dp', 'row')
- grad_w_up: float32 [1024, 4096], P('row', ('dp', 'col'))
- grad_w_down: float32 [4096, 1024], P(('dp', 'col'), 'row')
- grad_norm_attn: float32 [1024], P('row')
- grad_norm_ffn: float32 [1024], P('row')
- grad_conv_w: float32 [3, 1024], P(None, 'row')
Inputs may be any that keep to these rules, and one draw needn't show every extreme that they name: `seg_ids`: -1 marks padding, which stands at the end of a sequence; other equal ids mark one document, and a sequence's first document may continue in memory rows with the same id. `positions`: offset from the document's first token in the sequence; 0 for padding. `mem_seg`: for each sequence its 512 compressed rows, then its 512 memory rows, oldest first.
All inputs are finite; a program needn't handle non-finite values.
Results may differ from a plain program's by a relative error of at most 0.018.
Values may be sent and summed in bfloat16 or wider, within the bound.
No kernel may reach another device: no remote copies, remote signals or barrier semaphores. Data moves between devices by JAX's collectives and lax.ppermute only.
A program may use at most 256 MiB of HBM per device.

v0:
```python
import jax
import jax.numpy as jnp
from jax import lax
from jax.sharding import PartitionSpec as P

D = 1024
DH = 128
MEM = 512
CMEM = 512
RATE = 3
NEWC = 128
SEQ_LEN = 1024


EPSILON = 1e-05
MASKED = -1e30


def shortened(array):
    return jax.tree.map(lambda a: a.astype(jnp.bfloat16) if a.dtype == jnp.float32 else a, array)


def col_rows(block_in):
    return lax.all_gather(block_in, "col", axis=0, tiled=True)


def row_rows(block_in):
    return lax.all_gather(shortened(block_in), "row", axis=0, tiled=True).astype(block_in.dtype)


def row_sums(term_in):
    return lax.psum_scatter(term_in, "row", scatter_dimension=0, tiled=True)


def col_sums(term_in):
    return lax.psum_scatter(
        term_in.astype(jnp.bfloat16), "col", scatter_dimension=0, tiled=True
    ).astype(jnp.float32)


def share_rows(block_in):
    return lax.all_to_all(block_in, "row", split_axis=0, concat_axis=1, tiled=True)


def return_rows(block_in):
    return lax.all_to_all(
        block_in.astype(jnp.bfloat16), "row", split_axis=1, concat_axis=0, tiled=True
    ).astype(block_in.dtype)


def feature_totals(first_sum, second_sum):
    return lax.psum(jnp.stack([first_sum, second_sum], axis=0), "row")


def matmul(left_side, right_side):
    return jnp.dot(left_side, right_side, preferred_element_type=jnp.float32)


def matmul_tn(left_side, right_side):
    return lax.dot_general(
        left_side, right_side, (((0,), (0,)), ((), ())), preferred_element_type=jnp.float32
    )


def matmul_nt(left_side, right_side):
    return lax.dot_general(
        left_side, right_side, (((1,), (1,)), ((), ())), preferred_element_type=jnp.float32
    )


def smooth_gate(values):
    return jax.nn.gelu(values, approximate=True)


def normalize(rows_in, gain_row):
    totals = feature_totals(jnp.sum(rows_in, axis=1), jnp.sum(rows_in * rows_in, axis=1))
    average = totals[0] / D
    spread = totals[1] / D - average * average
    factor = lax.rsqrt(spread + EPSILON)
    unit_rows = (rows_in - average[:, None]) * factor[:, None]
    return (unit_rows, factor, unit_rows * gain_row[None, :])


def normalize_back(grad_rows, gain_row, unit_rows, factor):
    scaled = grad_rows * gain_row[None, :]
    totals = feature_totals(jnp.sum(scaled, axis=1), jnp.sum(scaled * unit_rows, axis=1))
    return factor[:, None] * (scaled - totals[0][:, None] / D - unit_rows * totals[1][:, None] / D)


def key_mask(seg_query, pos_query, index_query, seg_tok, pos_tok, keep_tok, seg_mem):
    mem_ok = seg_mem[None, :] == seg_query[:, None]
    index_key = jnp.arange(SEQ_LEN, dtype=jnp.int32)
    tok_ok = (seg_tok[None, :] == seg_query[:, None]) & (pos_tok[None, :] <= pos_query[:, None]) & (
        keep_tok[None, :] == 1
    ) | (index_key[None, :] == index_query[:, None])
    return jnp.concatenate([mem_ok, tok_ok], axis=1)


def masked_scores(queries, key_rows, allowed):
    scores = jnp.einsum(
        "qhd,khd->hqk", queries, key_rows, preferred_element_type=jnp.float32
    ) * DH ** (-0.5)
    if allowed is not None:
        scores = jnp.where(allowed[None], scores, MASKED)
    return scores


def attend_forward(queries, key_rows, value_rows, allowed):
    scores = masked_scores(queries, key_rows, allowed)
    highest = jnp.max(scores, axis=-1, keepdims=True)
    expo_scores = jnp.exp(scores - highest)
    summed = jnp.sum(expo_scores, axis=-1, keepdims=True)
    probs_low = (expo_scores / summed).astype(jnp.bfloat16)
    result = jnp.einsum("hqk,khd->qhd", probs_low, value_rows, preferred_element_type=jnp.float32)
    return (result, highest[..., 0] + jnp.log(summed[..., 0]))


def attend_back(queries, key_rows, value_rows, allowed, log_total, grad_low):
    scores = masked_scores(queries, key_rows, allowed)
    soft_probs = jnp.exp(scores - log_total[..., None])
    probs_low = soft_probs.astype(jnp.bfloat16)
    grad_probs = jnp.einsum(
        "qhd,khd->hqk", grad_low, value_rows, preferred_element_type=jnp.float32
    )
    grad_values = jnp.einsum(
        "hqk,qhd->khd", probs_low, grad_low, preferred_element_type=jnp.float32
    )
    grad_scores = (
        soft_probs * (grad_probs - jnp.sum(soft_probs * grad_probs, axis=-1, keepdims=True))
    ).astype(jnp.bfloat16)
    grad_query = jnp.einsum(
        "hqk,khd->qhd", grad_scores, key_rows, preferred_element_type=jnp.float32
    ) * DH ** (-0.5)
    grad_keys = jnp.einsum(
        "hqk,qhd->khd", grad_scores, queries, preferred_element_type=jnp.float32
    ) * DH ** (-0.5)
    return (grad_query, grad_keys, grad_values)


def sequence_forward(entries):
    tok_proj, mem_proj, seg_tok, pos_tok, keep_tok, seg_mem = entries
    queries = tok_proj[:, 0]
    key_rows = jnp.concatenate([mem_proj[: CMEM + MEM, 0], tok_proj[:, 1]], axis=0)
    value_rows = jnp.concatenate([mem_proj[: CMEM + MEM, 1], tok_proj[:, 2]], axis=0)
    index_all = jnp.arange(SEQ_LEN, dtype=jnp.int32)
    block_len = min(512, SEQ_LEN)
    outputs = []
    log_parts = []
    for block_start in range(0, SEQ_LEN, block_len):
        block_end = block_start + block_len
        allowed = key_mask(
            seg_tok[block_start:block_end],
            pos_tok[block_start:block_end],
            index_all[block_start:block_end],
            seg_tok,
            pos_tok,
            keep_tok,
            seg_mem,
        )
        result, log_total = attend_forward(
            queries[block_start:block_end], key_rows, value_rows, allowed
        )
        outputs.append(result.astype(jnp.bfloat16))
        log_parts.append(log_total)
    return (jnp.concatenate(outputs, axis=0), jnp.concatenate(log_parts, axis=1))


def sequence_backward(entries):
    tok_proj, mem_proj, grad_out, log_totals, seg_tok, pos_tok, keep_tok, seg_mem = entries
    mem_len = CMEM + MEM
    old_end = CMEM + RATE * NEWC
    queries = tok_proj[:, 0]
    key_rows = jnp.concatenate([mem_proj[:mem_len, 0], tok_proj[:, 1]], axis=0)
    value_rows = jnp.concatenate([mem_proj[:mem_len, 1], tok_proj[:, 2]], axis=0)
    old_keys = mem_proj[CMEM:old_end, 0]
    old_values = mem_proj[CMEM:old_end, 1]
    new_keys = mem_proj[mem_len:, 0]
    new_values = mem_proj[mem_len:, 1]
    index_all = jnp.arange(SEQ_LEN, dtype=jnp.int32)
    block_len = min(512, SEQ_LEN)
    grad_keys = jnp.zeros(key_rows.shape, jnp.float32)
    grad_values = jnp.zeros(value_rows.shape, jnp.float32)
    old_gk = jnp.zeros(old_keys.shape, jnp.float32)
    old_gv = jnp.zeros(old_values.shape, jnp.float32)
    new_gk = jnp.zeros(new_keys.shape, jnp.float32)
    new_gv = jnp.zeros(new_values.shape, jnp.float32)
    grad_queries = []
    for block_start in range(0, SEQ_LEN, block_len):
        block_end = block_start + block_len
        part_q = queries[block_start:block_end]
        allowed = key_mask(
            seg_tok[block_start:block_end],
            pos_tok[block_start:block_end],
            index_all[block_start:block_end],
            seg_tok,
            pos_tok,
            keep_tok,
            seg_mem,
        )
        main_q, main_k, main_v = attend_back(
            part_q,
            key_rows,
            value_rows,
            allowed,
            log_totals[:, block_start:block_end],
            grad_out[block_start:block_end],
        )
        old_result, old_total = attend_forward(part_q, old_keys, old_values, None)
        new_result, new_total = attend_forward(part_q, new_keys, new_values, None)
        recon_gap = (old_result - new_result).astype(jnp.bfloat16)
        old_q, old_k, old_v = attend_back(part_q, old_keys, old_values, None, old_total, recon_gap)
        new_q, new_k, new_v = attend_back(part_q, new_keys, new_values, None, new_total, -recon_gap)
        grad_queries.append((main_q + old_q + new_q).astype(jnp.bfloat16))
        grad_keys = grad_keys + main_k
        grad_values = grad_values + main_v
        old_gk = old_gk + old_k
        old_gv = old_gv + old_v
        new_gk = new_gk + new_k
        new_gv = new_gv + new_v
    grad_keys = grad_keys.at[CMEM:old_end].add(old_gk)
    grad_values = grad_values.at[CMEM:old_end].add(old_gv)
    tok_grad = jnp.stack(
        [
            jnp.concatenate(grad_queries, axis=0),
            grad_keys[mem_len:].astype(jnp.bfloat16),
            grad_values[mem_len:].astype(jnp.bfloat16),
        ],
        axis=1,
    )
    mem_keys = jnp.concatenate([grad_keys[:mem_len], new_gk], axis=0).astype(jnp.bfloat16)
    mem_values = jnp.concatenate([grad_values[:mem_len], new_gv], axis=0).astype(jnp.bfloat16)
    return (tok_grad, jnp.stack([mem_keys, mem_values], axis=1))


def per_device(
    hidden,
    memory,
    compressed,
    seg_ids,
    positions,
    keep_mask,
    mem_seg,
    cotangent,
    w_qkv,
    w_out,
    w_up,
    w_down,
    norm_attn,
    norm_ffn,
    conv_w,
):
    local_tokens, feat_part = hidden.shape
    heads_part = w_qkv.shape[2]
    head_width = heads_part * DH
    col_seqs = local_tokens // SEQ_LEN
    row_seqs = seg_ids.shape[0] // SEQ_LEN
    group_seqs = col_seqs * lax.axis_size("col")
    extra_rows = CMEM + MEM + NEWC
    seq_span = SEQ_LEN + extra_rows
    proj_span = 3 * SEQ_LEN + 2 * extra_rows
    qkv_b, out_b, up_b, down_b = (
        lax.all_gather(w_qkv.astype(jnp.bfloat16), "dp", axis=3, tiled=True),
        lax.all_gather(w_out.astype(jnp.bfloat16), "dp", axis=1, tiled=True),
        lax.all_gather(w_up.astype(jnp.bfloat16), "dp", axis=1, tiled=True),
        lax.all_gather(w_down.astype(jnp.bfloat16), "dp", axis=0, tiled=True),
    )
    w_proj = qkv_b.reshape(feat_part, 3 * head_width)
    w_mem = qkv_b[:, 1:].reshape(feat_part, 2 * head_width)
    w_back = out_b.reshape(head_width, feat_part)
    x_in = hidden.astype(jnp.float32)
    first_rows = jnp.concatenate(
        [x_in, compressed.astype(jnp.float32), memory.astype(jnp.float32)], axis=0
    )
    unit_first, factor_first, normed = normalize(first_rows, norm_attn)
    cm_count = col_seqs * CMEM
    x_norm = normed[:local_tokens]
    cm_norm = normed[local_tokens : local_tokens + cm_count]
    m_norm = normed[local_tokens + cm_count :]
    oldest = m_norm.reshape(col_seqs, MEM, feat_part)[:, : RATE * NEWC].reshape(
        col_seqs, NEWC, RATE, feat_part
    )
    packed = jnp.sum(oldest * conv_w[None, None], axis=2)
    seq_rows = jnp.concatenate(
        [
            x_norm.reshape(col_seqs, SEQ_LEN, feat_part),
            cm_norm.reshape(col_seqs, CMEM, feat_part),
            m_norm.reshape(col_seqs, MEM, feat_part),
            packed,
        ],
        axis=1,
    )
    seq_low = seq_rows.astype(jnp.bfloat16).reshape(col_seqs * seq_span, feat_part)
    rows_all = col_rows(seq_low).reshape(group_seqs, seq_span, feat_part)
    tok_rows = rows_all[:, :SEQ_LEN].reshape(group_seqs * SEQ_LEN, feat_part)
    mem_rows = rows_all[:, SEQ_LEN:].reshape(group_seqs * extra_rows, feat_part)
    proj_term = jnp.concatenate(
        [
            matmul(tok_rows, w_proj).reshape(group_seqs, 3 * SEQ_LEN, head_width),
            matmul(mem_rows, w_mem).reshape(group_seqs, 2 * extra_rows, head_width),
        ],
        axis=1,
    )
    projected = (
        row_sums(proj_term.reshape(group_seqs * proj_span, head_width))
        .astype(jnp.bfloat16)
        .reshape(row_seqs, proj_span, head_width)
    )
    tok_p = projected[:, : 3 * SEQ_LEN].reshape(row_seqs, SEQ_LEN, 3, heads_part, DH)
    mem_p = projected[:, 3 * SEQ_LEN :].reshape(row_seqs, extra_rows, 2, heads_part, DH)
    seg_q = seg_ids.reshape(row_seqs, SEQ_LEN)
    pos_q = positions.reshape(row_seqs, SEQ_LEN)
    keep_q = keep_mask.reshape(row_seqs, SEQ_LEN)
    seg_m = mem_seg.reshape(row_seqs, CMEM + MEM)
    heads_out, log_totals = lax.map(sequence_forward, (tok_p, mem_p, seg_q, pos_q, keep_q, seg_m))
    heads_all = row_rows(heads_out.reshape(row_seqs * SEQ_LEN, head_width))
    mid_state = x_in + col_sums(matmul(heads_all, w_back))
    unit_mid, factor_mid, normed_mid = normalize(mid_state, norm_ffn)
    x2_low = normed_mid.astype(jnp.bfloat16)
    x2_share = share_rows(x2_low)
    up_rows, down_rows = (
        lax.all_gather(up_b, "row", axis=0, tiled=True),
        lax.all_gather(down_b, "row", axis=1, tiled=True),
    )
    up_full, down_full = (
        lax.all_gather(up_rows, "col", axis=1, tiled=True),
        lax.all_gather(down_rows, "col", axis=0, tiled=True),
    )
    pre_act = matmul(x2_share, up_full)
    act_low = smooth_gate(pre_act).astype(jnp.bfloat16)
    branch_out = return_rows(matmul(act_low, down_full))
    out = (mid_state + branch_out).astype(jnp.bfloat16)
    cot_full = cotangent.astype(jnp.float32)
    gate_value, gate_pull = jax.vjp(smooth_gate, pre_act)
    cot_share = share_rows(cotangent)
    full_down = matmul_tn(act_low, cot_share)
    grad_act = matmul_nt(cot_share, down_full)
    grad_pre = gate_pull(grad_act)[0].astype(jnp.bfloat16)
    full_up = matmul_tn(x2_share, grad_pre)
    grad_x2 = return_rows(matmul_nt(grad_pre, up_full))
    up_cols, down_cols = (
        lax.psum_scatter(
            full_up.astype(jnp.bfloat16), "col", scatter_dimension=1, tiled=True
        ).astype(jnp.float32),
        lax.psum_scatter(
            full_down.astype(jnp.bfloat16), "col", scatter_dimension=0, tiled=True
        ).astype(jnp.float32),
    )
    grad_up, grad_down = (
        lax.psum_scatter(
            up_cols.astype(jnp.bfloat16), "row", scatter_dimension=0, tiled=True
        ).astype(jnp.float32),
        lax.psum_scatter(
            down_cols.astype(jnp.bfloat16), "row", scatter_dimension=1, tiled=True
        ).astype(jnp.float32),
    )
    grad_norm2 = jnp.sum(grad_x2 * unit_mid, axis=0)
    grad_mid = cot_full + normalize_back(grad_x2, norm_ffn, unit_mid, factor_mid)
    grad_mid_low = grad_mid.astype(jnp.bfloat16)
    grad_attn_all = col_rows(grad_mid_low)
    grad_wout = matmul_tn(heads_all, grad_attn_all).reshape(heads_part, DH, feat_part)
    grad_heads = (
        row_sums(matmul_nt(grad_attn_all, w_back))
        .astype(jnp.bfloat16)
        .reshape(row_seqs, SEQ_LEN, heads_part, DH)
    )
    tok_grad, mem_grad = lax.map(
        sequence_backward, (tok_p, mem_p, grad_heads, log_totals, seg_q, pos_q, keep_q, seg_m)
    )
    grad_proj = jnp.concatenate(
        [
            tok_grad.reshape(row_seqs, 3 * SEQ_LEN, head_width),
            mem_grad.reshape(row_seqs, 2 * extra_rows, head_width),
        ],
        axis=1,
    )
    grad_all = row_rows(grad_proj.reshape(row_seqs * proj_span, head_width)).reshape(
        group_seqs, proj_span, head_width
    )
    grad_tok = grad_all[:, : 3 * SEQ_LEN].reshape(group_seqs * SEQ_LEN, 3 * head_width)
    grad_memrows = grad_all[:, 3 * SEQ_LEN :].reshape(group_seqs * extra_rows, 2 * head_width)
    tok_weight = matmul_tn(tok_rows, grad_tok)
    mem_weight = matmul_tn(mem_rows, grad_memrows)
    grad_qkv = jnp.concatenate(
        [tok_weight[:, :head_width], tok_weight[:, head_width:] + mem_weight], axis=1
    ).reshape(feat_part, 3, heads_part, DH)
    back_term = jnp.concatenate(
        [
            matmul_nt(grad_tok, w_proj).reshape(group_seqs, SEQ_LEN, feat_part),
            matmul_nt(grad_memrows, w_mem).reshape(group_seqs, extra_rows, feat_part),
        ],
        axis=1,
    )
    grad_rows = col_sums(back_term.reshape(group_seqs * seq_span, feat_part)).reshape(
        col_seqs, seq_span, feat_part
    )
    grad_x = grad_rows[:, :SEQ_LEN].reshape(local_tokens, feat_part)
    grad_cm = grad_rows[:, SEQ_LEN : SEQ_LEN + CMEM].reshape(cm_count, feat_part)
    grad_m = grad_rows[:, SEQ_LEN + CMEM : SEQ_LEN + CMEM + MEM]
    grad_packed = grad_rows[:, SEQ_LEN + CMEM + MEM :]
    grad_conv = jnp.sum(grad_packed[:, :, None, :] * oldest, axis=(0, 1))
    grad_oldest = grad_packed[:, :, None, :] * conv_w[None, None]
    grad_m = grad_m.at[:, : RATE * NEWC].add(grad_oldest.reshape(col_seqs, RATE * NEWC, feat_part))
    grad_first = jnp.concatenate(
        [grad_x, grad_cm, grad_m.reshape(col_seqs * MEM, feat_part)], axis=0
    )
    grad_norm1 = jnp.sum(grad_first * unit_first, axis=0)
    d_input = grad_mid + normalize_back(
        grad_x, norm_attn, unit_first[:local_tokens], factor_first[:local_tokens]
    )
    sum_qkv, sum_out, sum_up, sum_down = (
        lax.psum_scatter(
            grad_qkv.astype(jnp.bfloat16), "dp", scatter_dimension=3, tiled=True
        ).astype(jnp.float32),
        lax.psum_scatter(
            grad_wout.astype(jnp.bfloat16), "dp", scatter_dimension=1, tiled=True
        ).astype(jnp.float32),
        lax.psum_scatter(
            grad_up.astype(jnp.bfloat16), "dp", scatter_dimension=1, tiled=True
        ).astype(jnp.float32),
        lax.psum_scatter(
            grad_down.astype(jnp.bfloat16), "dp", scatter_dimension=0, tiled=True
        ).astype(jnp.float32),
    )
    sum_norm1, sum_norm2, sum_conv = lax.psum((grad_norm1, grad_norm2, grad_conv), ("dp", "col"))
    return (
        out,
        d_input.astype(jnp.bfloat16),
        sum_qkv,
        sum_out,
        sum_up,
        sum_down,
        sum_norm1,
        sum_norm2,
        sum_conv,
    )


def solution(mesh):
    placed = (
        P(("dp", "col"), "row"),
        P(("dp", "col"), "row"),
        P(("dp", "col"), "row"),
        P(("dp", "row")),
        P(("dp", "row")),
        P(("dp", "row")),
        P(("dp", "row")),
        P(("dp", "col"), "row"),
        P("row", None, "col", "dp"),
        P("col", "dp", "row"),
        P("row", ("dp", "col")),
        P(("dp", "col"), "row"),
        P("row"),
        P("row"),
        P(None, "row"),
    )
    return jax.shard_map(
        per_device,
        mesh=mesh,
        in_specs=placed,
        out_specs=(
            P(("dp", "col"), "row"),
            P(("dp", "col"), "row"),
            P("row", None, "col", "dp"),
            P("col", "dp", "row"),
            P("row", ("dp", "col")),
            P(("dp", "col"), "row"),
            P("row"),
            P("row"),
            P(None, "row"),
        ),
        check_vma=False,
    )
```

profile of v0, /device:TPU:0, one launch (start us, length us, event | category | flops | bytes accessed | tf_op | source)
XLA Modules:
  0.0 2682.0 jit_solution(2016870551485448600)
XLA Ops:
  12.9 20.8 psum.49
  52.0 49.3 %all-gather.12.cloned.1.call-done = bf16[8704,256]{1,0:T(8,128)(2,1)} async-done(((bf16[4352,256]{1,0:T(8,128)(2,1)}), bf16[8704,256]{1,0:T(8,128)(2,1)}) %all-gather.12.cloned.1.call-update) | async-done | bytes 4456464 | tf_op jit(solution)/shard_map/all_gather | solution.py:24
  113.6 20.4 reshape.488
  144.4 27.8 %reshape.485 = f32[4,3072,512]{2,1,0:T(8,128)} reshape(f32[4096,1536]{1,0:T(8,128)} %fusion.144) | data formatting | bytes 50331648 | tf_op jit(solution)/shard_map/reshape | solution.py:298
  172.2 29.7 %pad_maximum_fusion = f32[4,5376,512]{2,1,0:T(8,128)} fusion(f32[4,2304,512]{2,1,0:T(8,128)} %reshape.488, f32[4,3072,512]{2,1,0:T(8,128)} %reshape.485), kind=kLoop, calls=%fused_computation | loop fusion | flops 11010048 | bytes 88080384 | tf_op jit(solution)/shard_map/concatenate | solution.py:296
  209.3 712.8 %reduce-scatter.13.cloned.1.call-done = f32[5376,512]{1,0:T(8,128)} async-done(((f32[21504,512]{1,0:T(8,128)}), f32[5376,512]{1,0:T(8,128)}) %reduce-scatter.13.cloned.1.call-update) | async-done | bytes 11010064 | tf_op jit(solution)/shard_map/reduce_scatter | solution.py:32
  1013.3 74.8 %all-gather.14.cloned.1.call-done = bf16[4096,512]{0,1:T(8,128)(2,1)} async-done(((bf16[1024,512]{0,1:T(8,128)(2,1)}), bf16[4096,512]{0,1:T(8,128)(2,1)}) %all-gather.14.cloned.1.call-update) | async-done | bytes 4194320 | tf_op jit(solution)/shard_map/all_gather | solution.py:28
  1093.1 75.6 %all-gather.24.cloned.1.call-done = bf16[2048,1024]{1,0:T(8,128)(2,1)} async-done(((bf16[2048,256]{1,0:T(8,128)(2,1)}), bf16[2048,1024]{1,0:T(8,128)(2,1)}) %all-gather.24.cloned.1.call-update) | async-done | bytes 4194320 | tf_op jit(solution)/shard_map/all_gather | solution.py:322
  1168.8 80.3 %all-gather.18.cloned.1.call-done = bf16[1024,2048]{1,0:T(8,128)(2,1)} async-done(((bf16[256,2048]{1,0:T(8,128)(2,1)}), bf16[1024,2048]{1,0:T(8,128)(2,1)}) %all-gather.18.cloned.1.call-update) | async-done | bytes 4194320 | tf_op jit(solution)/shard_map/all_gather | solution.py:321
  1254.6 32.4 %psum.50 = f32[2,2048]{1,0:T(2,128)S(1)} all-reduce(f32[2,2048]{1,0:T(2,128)S(1)} %pad_maximum_fusion.11), channel_id=1, replica_groups=mesh['dp'=4,'row'=4,'col'=2] {'row'}, use_global_device_ids=true, to_apply=%region_12.13 | all-reduce | flops 4096 | bytes 32768 | tf_op jit(solution)/shard_map/psum | solution.py:52
  1295.4 57.7 %all-gather.26.cloned.1.call-done = bf16[4096,1024]{1,0:T(8,128)(2,1)} async-done(((bf16[2048,1024]{1,0:T(8,128)(2,1)}), bf16[4096,1024]{1,0:T(8,128)(2,1)}) %all-gather.26.cloned.1.call-update) | async-done | bytes 8388624 | tf_op jit(solution)/shard_map/all_gather | solution.py:326
  1363.6 94.7 %all-gather.20.cloned.1.call-done = bf16[1024,4096]{1,0:T(8,128)(2,1)} async-done(((bf16[1024,2048]{1,0:T(8,128)(2,1)}), bf16[1024,4096]{1,0:T(8,128)(2,1)}) %all-gather.20.cloned.1.call-update) | async-done | bytes 8388624 | tf_op jit(solution)/shard_map/all_gather | solution.py:325
  1458.3 15.7 fusion.10
  1484.4 10.9 convolution_convert_fusion.6
  1496.3 13.5 all-to-all-done.3
  1516.5 31.4 %psum.51 = f32[2,2048]{1,0:T(2,128)S(1)} all-reduce(f32[2,2048]{1,0:T(2,128)S(1)} %pad_maximum_fusion.12), channel_id=1, replica_groups=mesh['dp'=4,'row'=4,'col'=2] {'row'}, use_global_device_ids=true, to_apply=%region_15.16 | all-reduce | flops 4096 | bytes 32768 | tf_op jit(solution)/shard_map/psum | solution.py:52
  1593.4 90.2 %reduce-scatter.25.cloned.1.call-done = bf16[1024,2048]{1,0:T(8,128)(2,1)} async-done(((bf16[1024,4096]{1,0:T(8,128)(2,1)}), bf16[1024,2048]{1,0:T(8,128)(2,1)}) %reduce-scatter.25.cloned.1.call-update) | async-done | bytes 4194320 | tf_op jit(solution)/shard_map/reduce_scatter | solution.py:341
  1705.4 79.8 %reduce-scatter.31.cloned.1.call-done = bf16[2048,1024]{1,0:T(8,128)(2,1)} async-done(((bf16[4096,1024]{1,0:T(8,128)(2,1)}), bf16[2048,1024]{1,0:T(8,128)(2,1)}) %reduce-scatter.31.cloned.1.call-update) | async-done | bytes 4194320 | tf_op jit(solution)/shard_map/reduce_scatter | solution.py:344
  1785.5 146.6 %reduce-scatter.17.cloned.1.call-done = f32[1024,512]{1,0:T(8,128)} async-done(((f32[4096,512]{1,0:T(8,128)}), f32[1024,512]{1,0:T(8,128)}) %reduce-scatter.17.cloned.1.call-update) | async-done | bytes 2097168 | tf_op jit(solution)/shard_map/reduce_scatter | solution.py:32
  1939.0 12.7 multiply_reduce_fusion.1
  1951.7 16.0 multiply_convert_fusion.1
  1967.7 11.2 multiply_reduce_fusion
  1978.9 12.0 multiply_convert_fusion
  2067.3 24.3 reduce-scatter.33.cloned.1.call-done
  2091.6 353.8 %all-gather.30.cloned.1.call-done = bf16[1,21504,512]{2,1,0:T(8,128)(2,1)} async-done(((bf16[1,5376,512]{2,1,0:T(8,128)(2,1)}), bf16[1,21504,512]{2,1,0:T(8,128)(2,1)}) %all-gather.30.cloned.1.call-update) | async-done | bytes 22020112 | tf_op jit(solution)/shard_map/all_gather | solution.py:28
  2464.2 14.4 dot_general.247
  2478.6 14.4 reshape.501
  2492.9 19.7 reshape.500
  2530.9 19.9 dot_general.245
  2569.8 48.3 %reduce-scatter.19.cloned.1.call-done = bf16[4352,256]{1,0:T(8,128)(2,1)} async-done(((bf16[8704,256]{1,0:T(8,128)(2,1)}), bf16[4352,256]{1,0:T(8,128)(2,1)}) %reduce-scatter.19.cloned.1.call-update) | async-done | bytes 2228240 | tf_op jit(solution)/shard_map/reduce_scatter | solution.py:36
  2632.2 18.7 psum.52
  2657.7 13.4 all-reduce
  (444 shorter events, 421.0 us)
Async XLA Ops:
  8.0 93.3 %all-gather.12.cloned.1.call-start = ((), (), s32[]{:S(2)}) async-start(), calls=%async_computation.16 | async-start | bytes 6684672 | tf_op jit(solution)/shard_map/all_gather | solution.py:24
  43.2 878.9 %reduce-scatter.13.cloned.1.call-start = ((), (), s32[]{:S(2)}) async-start(), calls=%async_computation.17 | async-start | bytes 55050240 | tf_op jit(solution)/shard_map/reduce_scatter | solution.py:32
  51.9 82.1 %copy-start.44 = (bf16[256,3,4,128]{0,3,2,1:T(8,128)(2,1)}, bf16[256,3,4,128]{0,3,2,1:T(8,128)(2,1)S(1)}, u32[]{:S(2)}) copy-start(bf16[256,3,4,128]{0,3,2,1:T(8,128)(2,1)S(1)} %all_gather.37) | copy-start | bytes 2359300
  52.0 53.8 %copy-start.56 = (bf16[256,2,4,128]{0,3,2,1:T(8,128)(2,1)}, bf16[256,2,4,128]{0,3,2,1:T(8,128)(2,1)S(1)}, u32[]{:S(2)}) copy-start(bf16[256,2,4,128]{0,3,2,1:T(8,128)(2,1)S(1)} %slice.379) | copy-start | bytes 1572868
  202.0 804.1 %all-gather.22.cloned.1.call-start = ((), (), s32[]{:S(2)}) async-start(), calls=%async_computation.23 | async-start | bytes 1310720 | tf_op jit(solution)/shard_map/all_gather | solution.py:265
  203.7 803.1 %all-gather.16.cloned.1.call-start = ((), (), s32[]{:S(2)}) async-start(), calls=%async_computation.20 | async-start | bytes 1310720 | tf_op jit(solution)/shard_map/all_gather | solution.py:264
  204.5 883.7 %all-gather.14.cloned.1.call-start = ((), (), s32[]{:S(2)}) async-start(), calls=%async_computation.18 | async-start | bytes 5242880 | tf_op jit(solution)/shard_map/all_gather | solution.py:28
  1006.0 162.7 %all-gather.24.cloned.1.call-start = ((), (), s32[]{:S(2)}) async-start(), calls=%async_computation.24 | async-start | bytes 5242880 | tf_op jit(solution)/shard_map/all_gather | solution.py:322
  1006.7 242.4 %all-gather.18.cloned.1.call-start = ((), (), s32[]{:S(2)}) async-start(), calls=%async_computation.21 | async-start | bytes 5242880 | tf_op jit(solution)/shard_map/all_gather | solution.py:321
  1007.5 245.2 %reduce-scatter.15.cloned.1.call-start = ((), (), s32[]{:S(2)}) async-start(), calls=%async_computation.19 | async-start | bytes 3145728 | tf_op jit(solution)/shard_map/reduce_scatter | solution.py:36
  1093.0 260.0 %all-gather.26.cloned.1.call-start = ((), (), s32[]{:S(2)}) async-start(), calls=%async_computation.25 | async-start | bytes 12582912 | tf_op jit(solution)/shard_map/all_gather | solution.py:326
  1168.7 84.0 %copy-start.7 = (bf16[2048,256]{1,0:T(8,128)(2,1)S(1)}, bf16[2048,256]{1,0:T(8,128)(2,1)}, u32[]{:S(2)}) copy-start(bf16[2048,256]{1,0:T(8,128)(2,1)} %param.21) | copy-start | bytes 3145732
  1168.7 289.6 %all-gather.20.cloned.1.call-start = ((), (), s32[]{:S(2)}) async-start(), calls=%async_computation.22 | async-start | bytes 12582912 | tf_op jit(solution)/shard_map/all_gather | solution.py:325
  1249.1 41.0 %all-to-all-start.2 = ((bf16[4,512,256]{2,1,0:T(8,128)(2,1)}), bf16[4,512,256]{2,1,0:T(8,128)(2,1)S(1)}, u32[]{:S(2)}, u32[]{:S(2)}) async-start(bf16[4,512,256]{2,1,0:T(8,128)(2,1)} %bitcast.35), calls=%async_computation.4 | async-start | bytes 2097152 | tf_op jit(solution)/shard_map/all_to_all | solution.py:42
  1290.1 168.2 %all-to-all-start = ((bf16[4,512,256]{1,2,0:T(8,128)(2,1)}), bf16[4,512,256]{1,2,0:T(8,128)(2,1)}, u32[]{:S(2)}, u32[]{:S(2)}) async-start(bf16[4,512,256]{1,2,0:T(8,128)(2,1)} %copy.209), calls=%async_computation.2 | async-start | bytes 2097152 | tf_op jit(solution)/shard_map/all_to_all | solution.py:42
  1295.4 68.2 %copy-start.58 = (bf16[512,4,256]{0,2,1:T(8,128)(2,1)}, bf16[512,4,256]{0,2,1:T(8,128)(2,1)S(1)}, u32[]{:S(2)}) copy-start(bf16[512,4,256]{0,2,1:T(8,128)(2,1)S(1)} %copy.211) | copy-start | bytes 3145732
  1479.6 30.3 %all-to-all-start.3 = ((bf16[512,4,256]{2,0,1:T(8,128)(2,1)}), bf16[512,4,256]{2,0,1:T(8,128)(2,1)S(1)}, u32[]{:S(2)}, u32[]{:S(2)}) async-start(bf16[512,4,256]{2,0,1:T(8,128)(2,1)} %bitcast.270), calls=%async_computation.5 | async-start | bytes 2097152 | tf_op jit(solution)/shard_map/all_to_all | solution.py:46
  1509.9 38.0 %all-to-all-start.1 = ((bf16[512,4,256]{2,0,1:T(8,128)(2,1)}), bf16[512,4,256]{2,0,1:T(8,128)(2,1)}, u32[]{:S(2)}, u32[]{:S(2)}) async-start(bf16[512,4,256]{2,0,1:T(8,128)(2,1)} %bitcast.313), calls=%async_computation.3 | async-start | bytes 2097152 | tf_op jit(solution)/shard_map/all_to_all | solution.py:46
  1514.1 68.0 %all-gather.28.cloned.1.call-start = ((), (), s32[]{:S(2)}) async-start(), calls=%async_computation.26 | async-start | bytes 3145728 | tf_op jit(solution)/shard_map/all_gather | solution.py:24
  1551.9 131.8 %reduce-scatter.25.cloned.1.call-start = ((), (), s32[]{:S(2)}) async-start(), calls=%async_computation.31 | async-start | bytes 12582912 | tf_op jit(solution)/shard_map/reduce_scatter | solution.py:341
  1562.3 222.9 %reduce-scatter.31.cloned.1.call-start = ((), (), s32[]{:S(2)}) async-start(), calls=%async_computation.34 | async-start | bytes 12582912 | tf_op jit(solution)/shard_map/reduce_scatter | solution.py:344
  1573.7 358.4 %reduce-scatter.17.cloned.1.call-start = ((), (), s32[]{:S(2)}) async-start(), calls=%async_computation.27 | async-start | bytes 10485760 | tf_op jit(solution)/shard_map/reduce_scatter | solution.py:32
  1588.4 478.1 %reduce-scatter.27.cloned.1.call-start = ((), (), s32[]{:S(2)}) async-start(), calls=%async_computation.32 | async-start | bytes 5242880 | tf_op jit(solution)/shard_map/reduce_scatter | solution.py:349
  1589.6 94.1 %copy-start.52 = (bf16[128,1,4,128]{3,2,1,0:T(4,128)(2,1)}, bf16[128,1,4,128]{3,2,1,0:T(4,128)(2,1)S(1)}, u32[]{:S(2)}) copy-start(bf16[128,1,4,128]{3,2,1,0:T(4,128)(2,1)S(1)} %get-tuple-element.134) | copy-start | bytes 393220
  1593.4 92.7 %copy-start.10 = (f32[4,512,128]{1,2,0:T(8,128)}, f32[4,512,128]{1,2,0:T(8,128)S(1)}, u32[]{:S(2)}) copy-start(f32[4,512,128]{1,2,0:T(8,128)S(1)} %get-tuple-element.177) | copy-start | bytes 3145732
  1683.6 407.9 %reduce-scatter.33.cloned.1.call-start = ((), (), s32[]{:S(2)}) async-start(), calls=%async_computation.35 | async-start | bytes 5242880 | tf_op jit(solution)/shard_map/reduce_scatter | solution.py:352
  1785.2 660.2 %all-gather.30.cloned.1.call-start = ((), (), s32[]{:S(2)}) async-start(), calls=%async_computation.37 | async-start | bytes 27525120 | tf_op jit(solution)/shard_map/all_gather | solution.py:28
  2060.7 502.2 %reduce-scatter.23.cloned.1.call-start = ((), (), s32[]{:S(2)}) async-start(), calls=%async_computation.30 | async-start | bytes 327680 | tf_op jit(solution)/shard_map/reduce_scatter | solution.py:414
  2066.5 498.0 %reduce-scatter.29.cloned.1.call-start = ((), (), s32[]{:S(2)}) async-start(), calls=%async_computation.33 | async-start | bytes 1310720 | tf_op jit(solution)/shard_map/reduce_scatter | solution.py:417
  2067.2 499.0 %reduce-scatter.35.cloned.1.call-start = ((), (), s32[]{:S(2)}) async-start(), calls=%async_computation.36 | async-start | bytes 1310720 | tf_op jit(solution)/shard_map/reduce_scatter | solution.py:420
  2091.5 476.5 %reduce-scatter.21.cloned.1.call-start = ((), (), s32[]{:S(2)}) async-start(), calls=%async_computation.29 | async-start | bytes 983040 | tf_op jit(solution)/shard_map/reduce_scatter | solution.py:411
  2524.5 93.7 %reduce-scatter.19.cloned.1.call-start = ((), (), s32[]{:S(2)}) async-start(), calls=%async_computation.28 | async-start | bytes 6684672 | tf_op jit(solution)/shard_map/reduce_scatter | solution.py:36
  (98 other events, 689.2 us)
Sparse Core Ops, SparseCore 0:
  43.4 57.9 all-gather.11
  202.1 720.0 reduce-scatter.12
  1093.1 30.3 reduce-scatter.14
  2060.8 384.5 all-gather.29
Sparse Core Ops, SparseCore 1:
  204.6 16.5 all-gather.21
  222.6 16.5 all-gather.15
  1006.1 82.1 all-gather.13
  1089.8 78.9 all-gather.23
  1170.3 78.8 all-gather.17
  1250.7 102.3 all-gather.25
  1354.4 103.8 all-gather.19
  1551.9 30.2 all-gather.27
  1584.3 99.2 reduce-scatter.24
  1685.9 99.2 reduce-scatter.30
  1787.4 144.6 reduce-scatter.16
  1934.4 77.3 reduce-scatter.26
  2013.9 77.6 reduce-scatter.32
  2094.6 31.8 reduce-scatter.22
  2129.0 24.7 reduce-scatter.28
  2156.3 24.7 reduce-scatter.34
  2524.5 22.7 reduce-scatter.20
  2561.3 56.8 reduce-scatter.18
where the time goes:
time: 2700 us; the launch traced here: 2680 us
  waiting for transfers between devices  1910 us (71%)
  matrix products  226 us (8%)
  local copies, waits for them, and re-layouts  222 us (8%)
  other arithmetic  154 us (6%)
  blocking collectives  131 us (5%)
    reduce_scatter x2, waiting for transfers between devices, row_sums(): return lax.psum_scatter(term_in, 'row', scatter_dimension=0, tiled=True)  859 us
    all_gather x2, waiting for transfers between devices, row_rows(): lax.all_gather(shortened(block_in), 'row', axis=0, tiled=True)  429 us
    psum x4, blocking collectives, feature_totals(): return lax.psum(jnp.stack([first_sum, second_sum], axis=0), 'row')  103 us
    all_gather x1, waiting for transfers between devices, per_device(): lax.all_gather(up_rows, 'col', axis=1, tiled=True)  94.7 us
    reduce_scatter x1, waiting for transfers between devices, per_device(): lax.psum_scatter(full_up.astype(jnp.bfloat16), 'col', scatter_dimension=1...  90.2 us
    all_gather x1, waiting for transfers between devices, per_device(): lax.all_gather(up_b, 'row', axis=0, tiled=True)  80.3 us
    reduce_scatter x1, waiting for transfers between devices, per_device(): lax.psum_scatter(full_down.astype(jnp.bfloat16), 'col', scatter_dimension...  79.8 us
    all_gather x1, waiting for transfers between devices, per_device(): lax.all_gather(down_b, 'row', axis=1, tiled=True)  75.6 us
  transfers between devices with their start and end apart: 26, of which 15 were waited for; matrix products, arithmetic and copies ran while one was open for 16% of the time, Pallas kernels for 0%

commit v1 on v0

v1 whole, which is shorter than its diff:
```python
import functools

import jax
import jax.numpy as jnp
from jax import lax
from jax.experimental import pallas as pl
from jax.experimental.pallas import tpu as pltpu
from jax.sharding import PartitionSpec as P

D = 1024
DH = 128
MEM = 512
CMEM = 512
RATE = 3
NEWC = 128
SEQ_LEN = 1024
HALF = SEQ_LEN // 2
HEADS = 4
OLD = RATE * NEWC
MROWS = CMEM + MEM
KM = MROWS + NEWC
QUARTER = D // 4
CHUNK = 256

EPSILON = 1e-05
MASKED = -1e30
LOG2E = 1.4426950408889634
SCALE = DH**-0.5
SCALE2 = SCALE * LOG2E
F32 = jnp.float32
BF = jnp.bfloat16


def nn(a, b):
    return lax.dot_general(a, b, (((1,), (0,)), ((), ())), preferred_element_type=F32)


def nt(a, b):
    return lax.dot_general(a, b, (((1,), (1,)), ((), ())), preferred_element_type=F32)


def tn(a, b):
    return lax.dot_general(a, b, (((0,), (0,)), ((), ())), preferred_element_type=F32)


def swap(x, axis, distance):
    n = lax.axis_size(axis)
    return lax.ppermute(x, axis, [(i, i ^ distance) for i in range(n)])


def add_low(a, b):
    return (a.astype(F32) + b.astype(F32)).astype(BF)


def params(limit_mb, dims=1):
    return pltpu.CompilerParams(
        dimension_semantics=("arbitrary",) * dims, vmem_limit_bytes=limit_mb << 20
    )


def shape(dims, kind):
    return jax.ShapeDtypeStruct(dims, kind)


def whole(dims):
    zeros = (0,) * len(dims)
    return pl.BlockSpec(dims, lambda *_: zeros)


def norm_block(pieces, gain_ref, row_id):
    columns, values, total = [], [], 0.0
    for k in range(4):
        start = pl.multiple_of((row_id ^ k) * QUARTER, QUARTER)
        columns.append(pl.ds(start, QUARTER))
        v = pieces[k].astype(F32)
        values.append(v)
        total = total + jnp.sum(v, axis=1, keepdims=True)
    mean = total / D
    square = 0.0
    for k in range(4):
        values[k] = values[k] - mean
        square = square + jnp.sum(values[k] * values[k], axis=1, keepdims=True)
    factor = lax.rsqrt(square / D + EPSILON)
    return columns, [values[k] * factor * gain_ref[:, columns[k]] for k in range(4)]


def tok_norm_kernel(where, p0, p1, p2, p3, gain_ref, low_ref, raw_ref):
    pieces = [p[...] for p in (p0, p1, p2, p3)]
    columns, normed = norm_block(pieces, gain_ref, where[0])
    for k in range(4):
        low_ref[:, columns[k]] = normed[k].astype(BF)
        raw_ref[:, columns[k]] = pieces[k]


def tok_norm(where, pieces, gain):
    block = 256
    count = SEQ_LEN // block
    piece = pl.BlockSpec((block, QUARTER), lambda i, w: ((i + w[1] * (count // 2)) % count, 0))
    out = pl.BlockSpec((block, D), lambda i, w: (i, 0))
    return pl.pallas_call(
        tok_norm_kernel,
        out_shape=(shape((SEQ_LEN, D), BF), shape((SEQ_LEN, D), BF)),
        grid_spec=pltpu.PrefetchScalarGridSpec(
            num_scalar_prefetch=1,
            grid=(count,),
            in_specs=[piece] * 4 + [whole((1, D))],
            out_specs=[out, out],
        ),
        compiler_params=params(24),
        name="tok_norm",
    )(where, *pieces, gain)


def mem_norm_kernel(where, p0, p1, p2, p3, gain_ref, conv_ref, low_ref, raw_ref, keep_ref):
    for block in range(MROWS // 256):
        rows = slice(block * 256, block * 256 + 256)
        pieces = [p[rows, :] for p in (p0, p1, p2, p3)]
        columns, normed = norm_block(pieces, gain_ref, where[0])
        for k in range(4):
            low_ref[rows, columns[k]] = normed[k].astype(BF)
            raw_ref[rows, columns[k]] = pieces[k]
            if block * 256 >= CMEM:
                start = block * 256 - CMEM
                for j in range(2):
                    lanes = (where[0] ^ k) * 2 + j
                    keep_ref[lanes, start : start + 256, :] = normed[k][:, j * DH : j * DH + DH]
    for j in range(D // DH):
        lanes = slice(j * DH, j * DH + DH)
        packed = 0.0
        for t in range(RATE):
            picked = keep_ref[j, pl.ds(t, NEWC, stride=RATE), :]
            packed = packed + conv_ref[t : t + 1, lanes] * picked
        low_ref[MROWS:, lanes] = packed.astype(BF)


def mem_norm(where, pieces, gain, conv):
    return pl.pallas_call(
        mem_norm_kernel,
        out_shape=(shape((KM, D), BF), shape((MROWS, D), BF)),
        grid_spec=pltpu.PrefetchScalarGridSpec(
            num_scalar_prefetch=1,
            grid=(1,),
            in_specs=[whole((MROWS, QUARTER))] * 4 + [whole((1, D)), whole((RATE, D))],
            out_specs=[whole((KM, D)), whole((MROWS, D))],
            scratch_shapes=[pltpu.VMEM((D // DH, MEM, DH), F32)],
        ),
        compiler_params=params(32),
        name="mem_norm",
    )(where, *pieces, gain, conv)


def fill_bias(bias_ref, row_ref, col_ref):
    seg_q, pos_q = row_ref[0:1, :], row_ref[1:2, :]

    def memory_chunk(c, carry):
        rows = pl.ds(pl.multiple_of(c * CHUNK, CHUNK), CHUNK)
        bias_ref[rows, :] = jnp.where(col_ref[rows, 2:3] == seg_q, 0.0, MASKED)
        return carry

    def token_chunk(c, carry):
        start = pl.multiple_of(c * CHUNK, CHUNK)
        rows = pl.ds(start, CHUNK)
        same = (col_ref[rows, 0:1] == seg_q) & (col_ref[rows, 1:2] <= pos_q)
        key_id = lax.broadcasted_iota(jnp.int32, (CHUNK, SEQ_LEN), 0) + start
        query_id = lax.broadcasted_iota(jnp.int32, (CHUNK, SEQ_LEN), 1)
        target = pl.ds(pl.multiple_of(MROWS + c * CHUNK, CHUNK), CHUNK)
        bias_ref[target, :] = jnp.where(same | (key_id == query_id), 0.0, MASKED)
        return carry

    lax.fori_loop(0, MROWS // CHUNK, memory_chunk, 0)
    lax.fori_loop(0, SEQ_LEN // CHUNK, token_chunk, 0)


def forward_kernel(tok_ref, mem_ref, row_ref, col_ref, o_ref, log_ref, bias_ref, s_ref, acc_ref):
    @pl.when(pl.program_id(0) == 0)
    def _():
        fill_bias(bias_ref, row_ref, col_ref)

    queries = tok_ref[:, :DH]

    def scores(key_ref, columns, offset):
        def step(c, top):
            rows = pl.ds(pl.multiple_of(c * CHUNK, CHUNK), CHUNK)
            target = pl.ds(pl.multiple_of(offset + c * CHUNK, CHUNK), CHUNK)
            s = nt(key_ref[rows, columns], queries) * SCALE2 + bias_ref[target, :]
            s_ref[target, :] = s
            return jnp.maximum(top, jnp.max(s.reshape(CHUNK // 8, 8, SEQ_LEN), axis=0))

        return step

    top = jnp.full((8, SEQ_LEN), -3.0e38, F32)
    top = lax.fori_loop(0, MROWS // CHUNK, scores(mem_ref, slice(0, DH), 0), top)
    top = lax.fori_loop(0, SEQ_LEN // CHUNK, scores(tok_ref, slice(DH, 2 * DH), MROWS), top)
    top = jnp.max(top, axis=0, keepdims=True)
    acc_ref[...] = jnp.zeros_like(acc_ref)

    def values(value_ref, columns, offset):
        def step(c, total):
            rows = pl.ds(pl.multiple_of(c * CHUNK, CHUNK), CHUNK)
            target = pl.ds(pl.multiple_of(offset + c * CHUNK, CHUNK), CHUNK)
            p = jnp.exp2(s_ref[target, :] - top)
            acc_ref[...] += nn(value_ref[rows, columns].T, p.astype(BF))
            return total + jnp.sum(p.reshape(CHUNK // 8, 8, SEQ_LEN), axis=0)

        return step

    total = jnp.zeros((8, SEQ_LEN), F32)
    total = lax.fori_loop(0, MROWS // CHUNK, values(mem_ref, slice(DH, 2 * DH), 0), total)
    total = lax.fori_loop(
        0, SEQ_LEN // CHUNK, values(tok_ref, slice(2 * DH, 3 * DH), MROWS), total
    )
    total = jnp.sum(total, axis=0, keepdims=True)
    o_ref[...] = (acc_ref[...] / total).T.astype(BF)
    log_ref[...] = (top + jnp.log2(total)).reshape(1, 1, SEQ_LEN)


def attention_forward(tok_p, mem_p, row_attr, col_attr):
    return pl.pallas_call(
        forward_kernel,
        out_shape=(shape((SEQ_LEN, HEADS * DH), BF), shape((HEADS, 1, SEQ_LEN), F32)),
        grid=(HEADS,),
        in_specs=[
            pl.BlockSpec((SEQ_LEN, 3 * DH), lambda h: (0, h)),
            pl.BlockSpec((KM, 2 * DH), lambda h: (0, h)),
            whole(row_attr.shape),
            whole(col_attr.shape),
        ],
        out_specs=[
            pl.BlockSpec((SEQ_LEN, DH), lambda h: (0, h)),
            pl.BlockSpec((1, 1, SEQ_LEN), lambda h: (h, 0, 0)),
        ],
        scratch_shapes=[
            pltpu.VMEM((MROWS + SEQ_LEN, SEQ_LEN), F32),
            pltpu.VMEM((MROWS + SEQ_LEN, SEQ_LEN), F32),
            pltpu.VMEM((DH, SEQ_LEN), F32),
        ],
        compiler_params=params(40),
        name="attention_forward",
    )(tok_p, mem_p, row_attr, col_attr)


def recon_kernel(tok_ref, mem_ref, gq_ref, gm_ref):
    q = tok_ref[:, :DH]
    old, new = slice(CMEM, CMEM + OLD), slice(MROWS, KM)
    keys, values = slice(0, DH), slice(DH, 2 * DH)

    def softmax_rows(key_rows):
        s = nt(key_rows, q) * SCALE2
        p = jnp.exp2(s - jnp.max(s, axis=0, keepdims=True))
        return p / jnp.sum(p, axis=0, keepdims=True)

    ko, vo, kn, vn = mem_ref[old, keys], mem_ref[old, values], mem_ref[new, keys], mem_ref[new, values]
    po, pn = softmax_rows(ko), softmax_rows(kn)
    po_low, pn_low = po.astype(BF), pn.astype(BF)
    out_o, out_n = nn(vo.T, po_low), nn(vn.T, pn_low)
    gap = (out_o - out_n).astype(BF)
    gap32 = gap.astype(F32)
    do = (po * (nn(vo, gap) - jnp.sum(gap32 * out_o, axis=0, keepdims=True))).astype(BF)
    dn = (pn * (jnp.sum(gap32 * out_n, axis=0, keepdims=True) - nn(vn, gap))).astype(BF)
    gq_ref[...] = ((nn(ko.T, do) + nn(kn.T, dn)) * SCALE).reshape(1, DH, SEQ_LEN)
    gap_t = gap32.T.astype(BF)
    gm_ref[:OLD, keys] = nn(do, q) * SCALE
    gm_ref[:OLD, values] = nn(po_low, gap_t)
    gm_ref[OLD:MEM, :] = jnp.zeros((MEM - OLD, 2 * DH), F32)
    gm_ref[MEM:, keys] = nn(dn, q) * SCALE
    gm_ref[MEM:, values] = -nn(pn_low, gap_t)


def reconstruction(tok_p, mem_p):
    return pl.pallas_call(
        recon_kernel,
        out_shape=(
            shape((HEADS, DH, SEQ_LEN), F32),
            shape((MEM + NEWC, HEADS * 2 * DH), F32),
        ),
        grid=(HEADS,),
        in_specs=[
            pl.BlockSpec((SEQ_LEN, 3 * DH), lambda h: (0, h)),
            pl.BlockSpec((KM, 2 * DH), lambda h: (0, h)),
        ],
        out_specs=[
            pl.BlockSpec((1, DH, SEQ_LEN), lambda h: (h, 0, 0)),
            pl.BlockSpec((MEM + NEWC, 2 * DH), lambda h: (0, h)),
        ],
        compiler_params=params(40),
        name="reconstruction",
    )(tok_p, mem_p)


def backward_kernel(
    tok_ref, mem_ref, own_ref, got_ref, o_ref, log_ref, rq_ref, rm_ref, row_ref, col_ref,
    gt_ref, gm_ref, bias_ref, acc_ref,
):
    @pl.when(pl.program_id(0) == 0)
    def _():
        fill_bias(bias_ref, row_ref, col_ref)

    q = tok_ref[:, :DH]
    go = jnp.concatenate([own_ref[...], got_ref[...]], axis=0)
    product = go.astype(F32) * o_ref[...].astype(F32)
    delta = jnp.sum(product.T, axis=0, keepdims=True)
    log_total = log_ref[...].reshape(1, SEQ_LEN)
    acc_ref[...] = rq_ref[...].reshape(DH, SEQ_LEN)

    def piece(k, v, offset):
        s = nt(k, q) * SCALE2 + bias_ref[offset, :]
        p = jnp.exp2(s - log_total)
        d = (p * (nt(v, go) - delta)).astype(BF)
        acc_ref[...] += nn(k.T, d) * SCALE
        return nn(d, q) * SCALE, nn(p.astype(BF), go)

    def memory_chunk(c, carry):
        rows = pl.ds(pl.multiple_of(c * CHUNK, CHUNK), CHUNK)
        gk, gv = piece(mem_ref[rows, :DH], mem_ref[rows, DH:], rows)
        gm_ref[rows, :DH] = gk.astype(BF)
        gm_ref[rows, DH:] = gv.astype(BF)
        return carry

    def shared_chunk(c, carry):
        rows = pl.ds(pl.multiple_of(c * CHUNK, CHUNK), CHUNK)
        extra = pl.ds(pl.multiple_of(c * CHUNK - CMEM, CHUNK), CHUNK)
        gk, gv = piece(mem_ref[rows, :DH], mem_ref[rows, DH:], rows)
        gm_ref[rows, :DH] = (gk + rm_ref[extra, :DH]).astype(BF)
        gm_ref[rows, DH:] = (gv + rm_ref[extra, DH:]).astype(BF)
        return carry

    def token_chunk(c, carry):
        rows = pl.ds(pl.multiple_of(c * CHUNK, CHUNK), CHUNK)
        target = pl.ds(pl.multiple_of(MROWS + c * CHUNK, CHUNK), CHUNK)
        gk, gv = piece(tok_ref[rows, DH : 2 * DH], tok_ref[rows, 2 * DH :], target)
        gt_ref[rows, DH : 2 * DH] = gk.astype(BF)
        gt_ref[rows, 2 * DH :] = gv.astype(BF)
        return carry

    lax.fori_loop(0, CMEM // CHUNK, memory_chunk, 0)
    lax.fori_loop(CMEM // CHUNK, MROWS // CHUNK, shared_chunk, 0)
    lax.fori_loop(0, SEQ_LEN // CHUNK, token_chunk, 0)
    gm_ref[MROWS:, :] = rm_ref[MEM:, :].astype(BF)
    gt_ref[:, :DH] = acc_ref[...].T.astype(BF)


def attention_backward(tok_p, mem_p, go_own, go_got, o, logs, rec_q, rec_m, row_attr, col_attr):
    half = pl.BlockSpec((HALF, DH), lambda h: (0, h))
    return pl.pallas_call(
        backward_kernel,
        out_shape=(
            shape((SEQ_LEN, HEADS * 3 * DH), BF),
            shape((KM, HEADS * 2 * DH), BF),
        ),
        grid=(HEADS,),
        in_specs=[
            pl.BlockSpec((SEQ_LEN, 3 * DH), lambda h: (0, h)),
            pl.BlockSpec((KM, 2 * DH), lambda h: (0, h)),
            half,
            half,
            pl.BlockSpec((SEQ_LEN, DH), lambda h: (0, h)),
            pl.BlockSpec((1, 1, SEQ_LEN), lambda h: (h, 0, 0)),
            pl.BlockSpec((1, DH, SEQ_LEN), lambda h: (h, 0, 0)),
            pl.BlockSpec((MEM + NEWC, 2 * DH), lambda h: (0, h)),
            whole(row_attr.shape),
            whole(col_attr.shape),
        ],
        out_specs=[
            pl.BlockSpec((SEQ_LEN, 3 * DH), lambda h: (0, h)),
            pl.BlockSpec((KM, 2 * DH), lambda h: (0, h)),
        ],
        scratch_shapes=[
            pltpu.VMEM((MROWS + SEQ_LEN, SEQ_LEN), F32),
            pltpu.VMEM((DH, SEQ_LEN), F32),
        ],
        compiler_params=params(40),
        name="attention_backward",
    )(tok_p, mem_p, go_own, go_got, o, logs, rec_q, rec_m, row_attr, col_attr)


def center_rows(rows):
    centered = rows - jnp.mean(rows, axis=1, keepdims=True)
    factor = lax.rsqrt(jnp.mean(centered * centered, axis=1, keepdims=True) + EPSILON)
    return centered * factor, factor


def mid_kernel(raw_ref, own_ref, got_ref, w_ref, gain_ref, mid_ref, x2_ref, x2t_ref):
    width = own_ref.shape[1]
    mid = raw_ref[...].astype(F32) + (
        nn(own_ref[...], w_ref[:width, :]) + nn(got_ref[...], w_ref[width:, :])
    )
    unit, _ = center_rows(mid)
    normed = unit * gain_ref[...]
    mid_ref[...] = mid
    x2_ref[...] = normed.astype(BF)
    x2t_ref[...] = normed.T.astype(BF)


def residual_mid(raw, o, o_got, w_out, gain):
    block = 256
    rows = lambda width: pl.BlockSpec((block, width), lambda i: (i, 0))
    return pl.pallas_call(
        mid_kernel,
        out_shape=(shape((HALF, D), F32), shape((HALF, D), BF), shape((D, HALF), BF)),
        grid=(HALF // block,),
        in_specs=[rows(D), rows(HEADS * DH), rows(HEADS * DH), whole((D, D)), whole((1, D))],
        out_specs=[rows(D), rows(D), pl.BlockSpec((D, block), lambda i: (0, i))],
        compiler_params=params(32),
        name="residual_mid",
    )(raw, o, o_got, w_out, gain)


def ffn_kernel(first, order, x2_ref, x2t_ref, cot_ref, cott_ref, w_ref, *rest):
    if first:
        up_ref, down_ref, out_ref, gx_ref = rest
    else:
        out0_ref, gx0_ref, up_ref, down_ref, out_ref, gx_ref = rest

    @pl.when(pl.program_id(0) == 0)
    def _():
        if first:
            out_ref[...] = jnp.zeros_like(out_ref)
            gx_ref[...] = jnp.zeros_like(gx_ref)
        else:
            out_ref[...] = out0_ref[...]
            gx_ref[...] = gx0_ref[...]

    width = w_ref.shape[-1]
    w_up = w_ref[0, :, 0].reshape(D, width)
    w_down = w_ref[0, :, 1].reshape(D, width)
    v = nn(x2_ref[...], w_up)
    g_act = nn(cot_ref[...], w_down)
    c0, c1 = 0.7978845608028654, 0.044715
    v2 = v * v
    t = jnp.tanh(c0 * v * (1.0 + c1 * v2))
    half = 0.5 * (1.0 + t)
    act = (v * half).astype(BF)
    slope = half + (0.5 * c0) * v * (1.0 - t * t) * (1.0 + (3.0 * c1) * v2)
    g_pre = (g_act * slope).astype(BF)
    out_ref[...] += nt(act, w_down)
    gx_ref[...] += nt(g_pre, w_up)
    up_ref[0] = nn(x2t_ref[...], g_pre).astype(BF).reshape(4, QUARTER, width)
    down_ref[0] = nn(cott_ref[...], act).astype(BF).reshape(4, QUARTER, width)


def feed_forward(order, x2, x2t, cot, cott, weights, sums=None):
    count = order.shape[0]
    width = weights.shape[-1]
    grads = shape((count, 4, QUARTER, width), BF)
    grad_spec = pl.BlockSpec((1, 4, QUARTER, width), lambda i, f: (i, 0, 0, 0))
    rows, cols = whole((HALF, D)), whole((D, HALF))
    extra = () if sums is None else sums
    return pl.pallas_call(
        functools.partial(ffn_kernel, sums is None),
        out_shape=(grads, grads, shape((HALF, D), F32), shape((HALF, D), F32)),
        grid_spec=pltpu.PrefetchScalarGridSpec(
            num_scalar_prefetch=1,
            grid=(count,),
            in_specs=[rows, cols, rows, cols]
            + [pl.BlockSpec((1, 4, 2, QUARTER, width), lambda i, f: (f[i], 0, 0, 0, 0))]
            + [rows] * len(extra),
            out_specs=[grad_spec, grad_spec, rows, rows],
        ),
        compiler_params=params(56),
        name="feed_forward",
    )(order, x2, x2t, cot, cott, weights, *extra)


def mid_back_kernel(gx_ref, mid_ref, cot_ref, gain_ref, w_ref, gm_ref, ga_ref, keep_ref, send_ref, gn_ref):
    @pl.when(pl.program_id(0) == 0)
    def _():
        gn_ref[...] = jnp.zeros_like(gn_ref)

    unit, factor = center_rows(mid_ref[...])
    gx = gx_ref[...]
    gn_ref[...] += jnp.sum(gx * unit, axis=0, keepdims=True)
    s = gx * gain_ref[...]
    g_mid = cot_ref[...].astype(F32) + factor * (
        s - jnp.mean(s, axis=1, keepdims=True) - unit * jnp.mean(s * unit, axis=1, keepdims=True)
    )
    gm_ref[...] = g_mid
    low = g_mid.astype(BF)
    ga_ref[...] = low
    width = keep_ref.shape[1]
    send_ref[...] = nt(low, w_ref[width:, :]).astype(BF)
    keep_ref[...] = nt(low, w_ref[:width, :]).astype(BF)


def mid_back(gx, mid, cot, gain, w_out):
    block = 256
    rows = lambda width: pl.BlockSpec((block, width), lambda i: (i, 0))
    half = shape((HALF, HEADS * DH), BF)
    return pl.pallas_call(
        mid_back_kernel,
        out_shape=(shape((HALF, D), F32), shape((HALF, D), BF), half, half, shape((1, D), F32)),
        grid=(HALF // block,),
        in_specs=[rows(D), rows(D), rows(D), whole((1, D)), whole((D, D))],
        out_specs=[rows(D), rows(D), rows(HEADS * DH), rows(HEADS * DH), whole((1, D))],
        compiler_params=params(32),
        name="mid_back",
    )(gx, mid, cot, gain, w_out)


def input_grad_kernel(keep_ref, got_ref, raw_ref, gm_ref, gain_ref, out_ref, gn_ref):
    @pl.when(pl.program_id(0) == 0)
    def _():
        gn_ref[...] = jnp.zeros_like(gn_ref)

    unit, factor = center_rows(raw_ref[...].astype(F32))
    gx = keep_ref[...] + got_ref[...].astype(F32)
    gn_ref[...] += jnp.sum(gx * unit, axis=0, keepdims=True)
    s = gx * gain_ref[...]
    g = gm_ref[...] + factor * (
        s - jnp.mean(s, axis=1, keepdims=True) - unit * jnp.mean(s * unit, axis=1, keepdims=True)
    )
    for k in range(4):
        out_ref[k] = g[:, k * QUARTER : (k + 1) * QUARTER].astype(BF)


def input_grad(keep, got, raw, g_mid, gain):
    block = 256
    rows = pl.BlockSpec((block, D), lambda i: (i, 0))
    return pl.pallas_call(
        input_grad_kernel,
        out_shape=(shape((4, HALF, QUARTER), BF), shape((1, D), F32)),
        grid=(HALF // block,),
        in_specs=[rows, rows, rows, rows, whole((1, D))],
        out_specs=[pl.BlockSpec((4, block, QUARTER), lambda i: (0, i, 0)), whole((1, D))],
        compiler_params=params(32),
        name="input_grad",
    )(keep, got, raw, g_mid, gain)


def mem_grad_kernel(g_ref, w_ref, raw_ref, gain_ref, conv_ref, gn_ref, gc_ref, unit_ref):
    total = jnp.zeros((1, D), F32)
    for block in range(MROWS // 256):
        rows = slice(block * 256, block * 256 + 256)
        unit, _ = center_rows(raw_ref[rows, :].astype(F32))
        total = total + jnp.sum(nn(g_ref[rows, :], w_ref[...]) * unit, axis=0, keepdims=True)
        if block * 256 >= CMEM:
            start = block * 256 - CMEM
            for j in range(D // DH):
                unit_ref[j, start : start + 256, :] = unit[:, j * DH : j * DH + DH]
    gn_ref[...] = total
    packed = nn(g_ref[MROWS:, :], w_ref[...])
    for j in range(D // DH):
        lanes = slice(j * DH, j * DH + DH)
        for t in range(RATE):
            picked = unit_ref[j, pl.ds(t, NEWC, stride=RATE), :]
            term = jnp.sum(packed[:, lanes] * picked, axis=0, keepdims=True)
            gc_ref[t : t + 1, lanes] = term * gain_ref[:, lanes]
            gn_ref[:, lanes] += conv_ref[t : t + 1, lanes] * term


def mem_grad(g_mem, w_mem, raw, gain, conv):
    return pl.pallas_call(
        mem_grad_kernel,
        out_shape=(shape((1, D), F32), shape((RATE, D), F32)),
        grid=(1,),
        in_specs=[
            whole((KM, D)), whole((D, D)), whole((MROWS, D)), whole((1, D)), whole((RATE, D)),
        ],
        out_specs=[whole((1, D)), whole((RATE, D))],
        scratch_shapes=[pltpu.VMEM((D // DH, MEM, DH), F32)],
        compiler_params=params(40),
        name="mem_grad",
    )(g_mem, w_mem, raw, gain, conv)


def halve_x(g):
    return add_low(g[0], swap(g[1], "dp", 2))


def halve_col(g):
    while g.shape[0] > 1:
        n = g.shape[0] // 2
        g = add_low(g[:n], swap(g[n:], "col", n))
    return g[0]


def pick(g, index, axis=0):
    return lax.dynamic_index_in_dim(g, index, axis, keepdims=False)


def halve_row(g, z_high, z_low):
    g = g.reshape((2, 2) + g.shape[1:])
    g = add_low(pick(g, z_high), swap(pick(g, 1 - z_high), "row", 2))
    got = swap(pick(g, 1 - z_low), "row", 1)
    return pick(g, z_low).astype(F32) + got.astype(F32)


def split_axis_of(g, axis, index):
    return pick(g, index, axis), pick(g, 1 - index, axis)


def sum_all(v):
    for axis, distances in (("dp", (1, 2)), ("row", (1, 2)), ("col", None)):
        if distances is None:
            distances, n = [], 1
            while n < lax.axis_size(axis):
                distances.append(n)
                n *= 2
        for distance in distances:
            v = v + swap(v, axis, distance)
    return v


def per_device(
    hidden, memory, compressed, seg_ids, positions, keep_mask, mem_seg, cotangent,
    w_qkv, w_out, w_up, w_down, norm_attn, norm_ffn, conv_w,
):
    n_col = lax.axis_size("col")
    heads_part = w_qkv.shape[2]
    dp, row, col = lax.axis_index("dp"), lax.axis_index("row"), lax.axis_index("col")
    z_high, z_low = row // 2, row % 2
    everything = ("dp", "col", "row")
    where = jnp.stack([row, z_low]).astype(jnp.int32)

    def gather_rows(rows):
        mine, other = pick(rows, z_high), pick(rows, 1 - z_high)
        far = swap(other, "row", 2)
        near = swap(mine, "row", 1)
        return [mine, near, far, swap(far, "row", 1)]

    tok_pieces = gather_rows(hidden.reshape(2, SEQ_LEN, QUARTER))
    mem_rows = jnp.concatenate(
        [compressed.reshape(2, CMEM, QUARTER), memory.reshape(2, MEM, QUARTER)], axis=1
    )
    mem_pieces = gather_rows(mem_rows)

    small = jnp.concatenate(
        [norm_attn, norm_ffn, conv_w.reshape(-1)]
        + [a.astype(F32) for a in (seg_ids, positions, keep_mask, mem_seg)]
    )
    shared = jnp.stack([small] + [swap(small, "row", k) for k in (1, 2, 3)])
    gains = jnp.stack([pick(shared, row ^ k) for k in range(4)])[:, : 5 * QUARTER]
    gains = gains.reshape(4, 5, QUARTER).transpose(1, 0, 2).reshape(5, D)
    gain1, gain2, conv = gains[0:1], gains[1:2], gains[2:5]
    spans = seg_ids.shape[0] // SEQ_LEN
    sequence = 2 * col + z_high
    ids = pick(shared, row ^ (sequence // spans))[5 * QUARTER :]
    ids = pick(ids.reshape(4, spans, SEQ_LEN), sequence % spans, 1)
    rolled = jnp.concatenate([ids[:3, HALF:], ids[:3, :HALF]], axis=1)
    seg, pos, keep = jnp.where(z_low == 0, ids[:3], rolled)
    row_attr = jnp.stack([seg, pos])
    col_attr = jnp.stack([jnp.where(keep == 1, seg, -2.0), pos, ids[3]], axis=1)

    qkv_t = w_qkv.astype(BF).transpose(1, 2, 3, 0)
    qkv_all = lax.all_gather(qkv_t, everything, axis=0, tiled=False)
    qkv_all = qkv_all.reshape(4, n_col, 4, 3, heads_part, DH // 4, QUARTER)
    out_all = lax.all_gather(w_out.astype(BF), everything, axis=0, tiled=False)
    out_all = out_all.reshape(4, n_col, 4, heads_part, DH // 4, QUARTER)
    if heads_part % 2 == 0:
        part = heads_part // 2
        w_tok = lax.dynamic_slice_in_dim(qkv_all, z_low * part, part, 4)
        outs = [lax.dynamic_slice_in_dim(out_all, z * part, part, 3) for z in (z_low, 1 - z_low)]
    else:
        part = n_col // 2
        w_tok = lax.dynamic_slice_in_dim(qkv_all, z_low * part, part, 1)
        outs = [lax.dynamic_slice_in_dim(out_all, z * part, part, 1) for z in (z_low, 1 - z_low)]
    w_tok = w_tok.transpose(1, 4, 3, 0, 5, 2, 6).reshape(HEADS * 3 * DH, D)
    w_mem = w_tok.reshape(HEADS, 3, DH, D)[:, 1:].reshape(HEADS * 2 * DH, D)
    w_back = jnp.concatenate(
        [w.transpose(1, 3, 0, 4, 2, 5).reshape(HEADS * DH, D) for w in outs], axis=0
    )
    ffn_part = jnp.stack([w_up.astype(BF), w_down.astype(BF).T])
    ffn_all = lax.all_gather(ffn_part, everything, axis=0, tiled=False)
    ffn_all = ffn_all.reshape(4 * n_col, 4, 2, QUARTER, w_up.shape[1])

    x_tok, raw_tok = tok_norm(where, tok_pieces, gain1)
    x_mem, raw_mem = mem_norm(where, mem_pieces, gain1, conv)
    tok_p = nt(x_tok, w_tok).astype(BF)
    mem_p = nt(x_mem, w_mem).astype(BF)
    o, logs = attention_forward(tok_p, mem_p, row_attr, col_attr)
    o_got = swap(o[HALF:], "row", 1)
    rec_q, rec_m = reconstruction(tok_p, mem_p)

    cotangent, _ = lax.optimization_barrier((cotangent, mem_pieces[3]))
    cot = lax.all_to_all(cotangent, "row", split_axis=0, concat_axis=0, tiled=True)
    cot = cot.reshape(4, HALF, QUARTER).transpose(1, 0, 2).reshape(HALF, D)
    cott = cot.T

    mid, x2, x2t = residual_mid(raw_tok, o, o_got, w_back, gain2)

    steps = jnp.arange(2 * n_col, dtype=jnp.int32)
    x_rel, col_rel = steps // n_col, steps % n_col
    order = lambda core: (dp ^ (2 * x_rel + core)) * n_col + (col ^ col_rel)
    up_send, down_send, out_sum, gx_sum = feed_forward(order(1), x2, x2t, cot, cott, ffn_all)
    up_got, down_got = swap(up_send, "dp", 1), swap(down_send, "dp", 1)
    up_keep, down_keep, out_sum, gx_sum = feed_forward(
        order(0), x2, x2t, cot, cott, ffn_all, (out_sum, gx_sum)
    )
    g_mid, g_attn, go_keep, go_send, gain2_sum = mid_back(gx_sum, mid, cot, gain2, w_back)
    go_got = swap(go_send, "row", 1)
    blocks = (2, n_col) + up_keep.shape[1:]
    grad_up = halve_x(add_low(up_keep, up_got).reshape(blocks))
    grad_up = halve_row(halve_col(grad_up), z_high, z_low)
    grad_down = add_low(down_keep, down_got).reshape(blocks).swapaxes(0, 1)
    grad_down = halve_x(halve_col(grad_down[:, None])[0])
    grad_down = halve_row(grad_down, z_high, z_low).T

    g_tok, g_mem = attention_backward(
        tok_p, mem_p, go_keep, go_got, o, logs, rec_q, rec_m, row_attr, col_attr
    )
    gx = nn(g_tok, w_tok)
    gx_got = swap(gx[HALF:].astype(BF), "row", 1)

    out = (mid + out_sum).astype(BF).reshape(HALF, 4, QUARTER).transpose(1, 0, 2)
    out = lax.all_to_all(
        out.reshape(4 * HALF, QUARTER), "row", split_axis=0, concat_axis=0, tiled=True
    )

    g_tok_w = tn(g_tok, x_tok).reshape(HEADS, 3, DH, D)
    g_mem_w = tn(g_mem, x_mem).reshape(HEADS, 2, DH, D)
    g_qkv = jnp.concatenate([g_tok_w[:, :1], g_tok_w[:, 1:] + g_mem_w], axis=1).astype(BF)
    g_out = jnp.concatenate([tn(o[:HALF], g_attn), tn(o_got, g_attn)], axis=0).astype(BF)
    grad_qkv, grad_out = reduce_heads(g_qkv, g_out, n_col, heads_part, dp, z_high, z_low)

    d_rows, gain1_tok = input_grad(gx, gx_got, raw_tok, g_mid, gain1)
    d_input = lax.all_to_all(
        d_rows.reshape(4 * HALF, QUARTER), "row", split_axis=0, concat_axis=0, tiled=True
    )
    gain1_mem, conv_sum = mem_grad(g_mem, w_mem, raw_mem, gain1, conv)
    sums = sum_all(jnp.concatenate([gain1_tok + gain1_mem, gain2_sum, conv_sum], axis=0))
    sums = pick(sums.reshape(5, 4, QUARTER), row, 1)
    return (out, d_input, grad_qkv, grad_out, grad_up, grad_down, sums[0], sums[1], sums[2:])


def reduce_heads(g_qkv, g_out, n_col, heads_part, dp, z_high, z_low):
    core, x_id = dp % 2, dp // 2
    quarter = DH // 4
    g_qkv = g_qkv.reshape(HEADS, 3, 2, 2, quarter, 4, QUARTER)
    g_out = g_out.reshape(2, HEADS, 2, 2, quarter, 4, QUARTER)
    g_out = jnp.stack([pick(g_out, z_low), pick(g_out, 1 - z_low)])

    def over_dp(g, axis):
        mine, other = split_axis_of(g, axis + 1, core)
        g = add_low(mine, swap(other, "dp", 1))
        mine, other = split_axis_of(g, axis, x_id)
        return add_low(mine, swap(other, "dp", 2))

    g_qkv = over_dp(g_qkv, 2)
    g_out = over_dp(g_out, 2)
    if n_col == 2:
        c = lax.axis_index("col")
        part = heads_part // 2
        mine, other = split_axis_of(g_qkv.reshape(2, part, 3, quarter, 4, QUARTER), 0, c)
        g_qkv = add_low(mine, swap(other, "col", 1))
        mine, other = split_axis_of(g_out.reshape(2, 2, part, quarter, 4, QUARTER), 1, c)
        g_out = add_low(mine, swap(other, "col", 1))
        g_qkv = g_qkv.transpose(3, 0, 1, 2, 4).reshape(4, part * 3 * quarter, QUARTER)
        g_qkv = lax.all_to_all(g_qkv, "row", split_axis=0, concat_axis=0, tiled=True)
        g_qkv = g_qkv.astype(F32).reshape(2, 2, part, 3, quarter, QUARTER).sum(axis=0)
        g_qkv = g_qkv.reshape(heads_part, 3, quarter, QUARTER)
        g_out = g_out.transpose(3, 0, 1, 2, 4).reshape(4, heads_part, quarter, QUARTER)
        g_out = halve_row(g_out, z_high, z_low)
    else:
        zeros = jnp.zeros_like(g_qkv)
        g_qkv = jnp.where(
            z_low == 0, jnp.concatenate([g_qkv, zeros]), jnp.concatenate([zeros, g_qkv])
        )
        scatter = lambda g, axis, name: lax.psum_scatter(
            g, name, scatter_dimension=axis, tiled=True
        )
        g_qkv = scatter(scatter(g_qkv, 0, "col"), 3, "row")[:, :, :, 0].astype(F32)
        g_out = g_out.reshape((2 * HEADS,) + g_out.shape[2:])
        g_out = scatter(scatter(g_out, 0, "col"), 2, "row")[:, :, 0].astype(F32)
    return g_qkv.transpose(3, 1, 0, 2), g_out


def solution(mesh):
    tokens, features = ("dp", "col"), "row"
    placed = (
        P(tokens, features),
        P(tokens, features),
        P(tokens, features),
        P(("dp", "row")),
        P(("dp", "row")),
        P(("dp", "row")),
        P(("dp", "row")),
        P(tokens, features),
        P("row", None, "col", "dp"),
        P("col", "dp", "row"),
        P("row", tokens),
        P(tokens, "row"),
        P("row"),
        P("row"),
        P(None, "row"),
    )
    return jax.shard_map(
        per_device,
        mesh=mesh,
        in_specs=placed,
        out_specs=(
            P(tokens, features),
            P(tokens, features),
            P("row", None, "col", "dp"),
            P("col", "dp", "row"),
            P("row", tokens),
            P(tokens, "row"),
            P("row"),
            P("row"),
            P(None, "row"),
        ),
        check_vma=False,
    )
```

time: 2700 us -> 656 us (0.24)
  waiting for transfers between devices: 1910 us -> 294 us
  matrix products: 226 us -> 21 us
  local copies, waits for them, and re-layouts: 222 us -> 84.4 us
  Pallas kernels: 0 us -> 132 us
  blocking collectives: 131 us -> 0 us
  other arithmetic: 154 us -> 44 us
  starting transfers between devices: 19.2 us -> 61.1 us
    reduce_scatter x12 -> x0, waiting for transfers between devices: 1100 us -> none  [the longest x2 859 us: row_sums(): return lax.psum_scatter(term_in, 'row', scatter_dimension=0, tiled=True)]
    all_gather x10 -> x3, waiting for transfers between devices: 795 us -> 87.2 us  [the longest x1 87.2 us: per_device(): ffn_all = lax.all_gather(ffn_part, everything, axis=0, tiled=False)]
    dot_general x51 -> x7, matrix products: 226 us -> 21 us  [the longest x4 8.95 us: tn(): lax.dot_general(a, b, (((0,), (0,)), ((), ())), preferred_element_type=F32)]
    ppermute x0 -> x35, waiting for transfers between devices: none -> 204 us  [swap(): return lax.ppermute(x, axis, [(i, i ^ distance) for i in range(n)])]
    pallas_call x0 -> x11, Pallas kernels: none -> 132 us  [the longest x2 40.9 us: feed_forward(): pl.pallas_call(functools.partial(ffn_kernel, sums is None), out_shape=(gr...]
    psum x5 -> x0, blocking collectives: 117 us -> none  [the longest x4 103 us: feature_totals(): return lax.psum(jnp.stack([first_sum, second_sum], axis=0), 'row')]
    reshape x6 -> x4, local copies, waits for them, and re-layouts: 91.5 us -> 3.46 us  [the longest x1 2.4 us: per_device(): cot = cot.reshape(4, HALF, QUARTER).transpose(1, 0, 2).reshape(HALF, D)]
    ppermute x0 -> x35, starting transfers between devices: none -> 44.2 us  [swap(): return lax.ppermute(x, axis, [(i, i ^ distance) for i in range(n)])]
  transfers between devices with their start and end apart: 26 -> 42, of which waited for: 15 -> 19; matrix products, arithmetic and copies ran while one was open for 16% -> 17% of each run, Pallas kernels for 0% -> 14%
where the time goes in v1:
time: 656 us; the launch traced here: 652 us
  waiting for transfers between devices  294 us (45%)
  Pallas kernels  132 us (20%)
  local copies, waits for them, and re-layouts  84.4 us (13%)
  starting transfers between devices  61.1 us (9%)
  other arithmetic  44 us (7%)
  matrix products  21 us (3%)
  between operations  15.4 us (2%)
    ppermute x35, waiting for transfers between devices, swap(): return lax.ppermute(x, axis, [(i, i ^ distance) for i in range(n)])  204 us
    all_gather x1, waiting for transfers between devices, per_device(): ffn_all = lax.all_gather(ffn_part, everything, axis=0, tiled=False)  87.2 us
    ppermute x35, starting transfers between devices, swap(): return lax.ppermute(x, axis, [(i, i ^ distance) for i in range(n)])  44.2 us
    pallas_call x2, Pallas kernels, feed_forward(): pl.pallas_call(functools.partial(ffn_kernel, sums is None), out_shape=(gr...  40.9 us
    unnamed x152, local copies, waits for them, and re-layouts  36.9 us
    pallas_call x1, Pallas kernels, attention_backward(): pl.pallas_call(backward_kernel, out_shape=(shape((SEQ_LEN, HEADS * 3 * DH...  36.1 us
    convert_element_type x14, other arithmetic, add_low(): return (a.astype(F32) + b.astype(F32)).astype(BF)  24.5 us
    pallas_call x1, Pallas kernels, attention_forward(): pl.pallas_call(forward_kernel, out_shape=(shape((SEQ_LEN, HEADS * DH), BF...  24.1 us
  transfers between devices with their start and end apart: 42, of which 19 were waited for; matrix products, arithmetic and copies ran while one was open for 17% of the time, Pallas kernels for 14%

profile of v1, /device:TPU:0, one launch (start us, length us, event | category | flops | bytes accessed | tf_op | source)
XLA Modules:
  0.0 651.6 jit_solution(13460537110093049481)
XLA Ops:
  13.2 5.1 collective-permute-start.5
  26.7 26.0 %collective-permute-done.1.p2 = bf16[1024,256]{1,0:T(8,128)(2,1)S(1)} collective-permute-done((bf16[1024,256]{1,0:T(8,128)(2,1)}, bf16[1024,256]{1,0:T(8,128)(2,1)S(1)}, u32[]{:S(2)}, u32[]{:S(2)}) %collective-permute-start.1) | collective-permute-done | bytes 524320 | tf_op jit(solution)/shard_map/ppermute | solution.py:48
  52.7 27.8 %collective-permute-done.7.p2 = bf16[1024,256]{1,0:T(8,128)(2,1)S(1)} collective-permute-done((bf16[1024,256]{1,0:T(8,128)(2,1)}, bf16[1024,256]{1,0:T(8,128)(2,1)S(1)}, u32[]{:S(2)}, u32[]{:S(2)}) %collective-permute-start.7) | collective-permute-done | bytes 524320 | tf_op jit(solution)/shard_map/ppermute | solution.py:48
  84.4 34.8 %collective-permute-done.8.p3 = bf16[1024,256]{1,0:T(8,128)(2,1)} collective-permute-done((bf16[1024,256]{1,0:T(8,128)(2,1)S(1)}, bf16[1024,256]{1,0:T(8,128)(2,1)}, u32[]{:S(2)}, u32[]{:S(2)}) %collective-permute-start.8) | collective-permute-done | bytes 524320 | tf_op jit(solution)/shard_map/ppermute | solution.py:48
  119.3 4.4 all-to-all-start
  123.7 4.2 tok_norm.1
  130.5 4.0 mem_norm.1
  145.0 3.9 reshape_reshape.6
  154.2 3.7 convolution_convert_fusion.1.tok_ref
  157.9 24.1 %attention_forward.1 = (bf16[1024,512]{1,0:T(8,128)(2,1)S(1)}, f32[4,1,1024]{2,1,0:T(1,128)S(1)}) custom-call(bf16[1024,1536]{1,0:T(8,128)(2,1)S(1)} %convolution_convert_fusion.1.tok_ref, bf16[1152,1024]{1,0:T(8,128)(2,1)S(1)} %convolution_convert_fusion.mem_ref, f32[2,1024]{1,0:T(2,128)S(1)} %stack.67.row_ref, f32[1024,3]{1,0:T(8,128)S(1)} %copy-done.20), custom_call_target="tpu_custom_call" | custom-call | tf_op jit(solution)/shard_map/attention_forward/pallas_call | solution.py:218
  196.8 10.5 %reconstruction.1 = (f32[4,128,1024]{2,1,0:T(8,128)S(1)}, f32[640,1024]{1,0:T(8,128)S(1)}) custom-call(bf16[1024,1536]{1,0:T(8,128)(2,1)S(1)} %convolution_convert_fusion.1.tok_ref, bf16[1152,1024]{1,0:T(8,128)(2,1)S(1)} %copy-done.3), custom_call_target="tpu_custom_call" | custom-call | tf_op jit(solution)/shard_map/reconstruction/pallas_call | solution.py:270
  215.5 87.2 %all-gather.11.cloned.1.call-done = bf16[64,256,512]{2,1,0:T(8,128)(2,1)} async-done(((bf16[2,256,512]{2,1,0:T(8,128)(2,1)}), bf16[64,256,512]{2,1,0:T(8,128)(2,1)}) %all-gather.11.cloned.1.call-update) | async-done | bytes 16777232 | tf_op jit(solution)/shard_map/all_gather | solution.py:662
  302.7 19.3 %feed_forward.2 = (bf16[4,4,256,512]{3,2,1,0:T(8,128)(2,1)}, bf16[4,4,256,512]{3,2,1,0:T(8,128)(2,1)}, f32[512,1024]{1,0:T(8,128)}, f32[512,1024]{1,0:T(8,128)}) custom-call(s32[4]{0:T(128)} %get-tuple-element.113.order, bf16[512,1024]{1,0:T(8,128)(2,1)} %copy-done.22, bf16[1024,512]{1,0:T(8,128)(2,1)} %copy-done.23, bf16[512,1024]{1,0:T(8,128)(2,1)} %bitcast.194, ...), custom_call_target="tpu_custom_call" | custom-call | tf_op jit(solution)/shard_map/feed_forward/pallas_call | solution.py:448
  322.0 21.6 %feed_forward.3 = (bf16[4,4,256,512]{3,2,1,0:T(8,128)(2,1)}, bf16[4,4,256,512]{3,2,1,0:T(8,128)(2,1)}, f32[512,1024]{1,0:T(8,128)}, f32[512,1024]{1,0:T(8,128)}) custom-call(s32[4]{0:T(128)} %get-tuple-element.114.order, bf16[512,1024]{1,0:T(8,128)(2,1)} %copy-done.22, bf16[1024,512]{1,0:T(8,128)(2,1)} %copy-done.23, bf16[512,1024]{1,0:T(8,128)(2,1)} %bitcast.195, ...), custom_call_target="tpu_custom_call" | custom-call | tf_op jit(solution)/shard_map/feed_forward/pallas_call | solution.py:448
  346.5 4.4 all-to-all-start.1
  369.1 12.9 %collective-permute-done.10.got_ref = bf16[512,512]{1,0:T(8,128)(2,1)S(1)} collective-permute-done((bf16[512,512]{1,0:T(8,128)(2,1)}, bf16[512,512]{1,0:T(8,128)(2,1)S(1)}, u32[]{:S(2)}, u32[]{:S(2)}) %collective-permute-start.10) | collective-permute-done | bytes 524320 | tf_op jit(solution)/shard_map/ppermute | solution.py:48
  383.6 36.1 %attention_backward.1 = (bf16[1024,1536]{1,0:T(8,128)(2,1)}, bf16[1152,1024]{1,0:T(8,128)(2,1)S(1)}) custom-call(bf16[1024,1536]{1,0:T(8,128)(2,1)} %copy-done, bf16[1152,1024]{1,0:T(8,128)(2,1)S(1)} %copy-done.4, bf16[512,512]{1,0:T(8,128)(2,1)S(1)} %copy-done.34, bf16[512,512]{1,0:T(8,128)(2,1)S(1)} %collective-permute-done.10.got_ref, ...), custom_call_target="tpu_custom_call" | custom-call | tf_op jit(solution)/shard_map/attention_backward/pallas_call | solution.py:344
  419.8 5.4 fusion.34.keep_ref
  431.8 3.5 fusion.35
  442.9 4.5 concatenate.33
  450.2 3.7 fusion.6
  463.3 3.6 add_convert_fusion.1
  471.4 3.5 add_convert_fusion
  480.8 37.8 %collective-permute-done.31 = f32[5,1024]{1,0:T(8,128)S(1)} collective-permute-done((f32[5,1024]{1,0:T(8,128)S(1)}, f32[5,1024]{1,0:T(8,128)S(1)}, u32[]{:S(2)}, u32[]{:S(2)}) %collective-permute-start.31) | collective-permute-done | bytes 20512 | tf_op jit(solution)/shard_map/ppermute | solution.py:48
  535.4 4.5 all-to-all-start.2
  558.0 9.1 %collective-permute-done.13 = bf16[4,3,32,4,256]{4,3,2,1,0:T(4,128)(2,1)S(1)} collective-permute-done((bf16[4,3,32,4,256]{4,3,2,1,0:T(4,128)(2,1)S(1)}, bf16[4,3,32,4,256]{4,3,2,1,0:T(4,128)(2,1)S(1)}, u32[]{:S(2)}, u32[]{:S(2)}) %collective-permute-start.13) | collective-permute-done | bytes 786464 | tf_op jit(solution)/shard_map/ppermute | solution.py:48
  570.1 6.0 collective-permute-done.22
  581.8 5.1 collective-permute-done.27
  594.4 3.5 all-to-all-start.3
  597.8 17.8 %collective-permute-done.23 = bf16[2,256,512]{2,1,0:T(8,128)(2,1)} collective-permute-done((bf16[2,256,512]{2,1,0:T(8,128)(2,1)}, bf16[2,256,512]{2,1,0:T(8,128)(2,1)}, u32[]{:S(2)}, u32[]{:S(2)}) %collective-permute-start.23) | collective-permute-done | bytes 524320 | tf_op jit(solution)/shard_map/ppermute | solution.py:48
  617.0 9.9 %collective-permute-done.28 = bf16[2,256,512]{1,2,0:T(8,128)(2,1)} collective-permute-done((bf16[2,256,512]{1,2,0:T(8,128)(2,1)S(1)}, bf16[2,256,512]{1,2,0:T(8,128)(2,1)}, u32[]{:S(2)}, u32[]{:S(2)}) %collective-permute-start.28) | collective-permute-done | bytes 524320 | tf_op jit(solution)/shard_map/ppermute | solution.py:48
  634.7 4.7 collective-permute-done.29
  (327 shorter events, 183.7 us)
Async XLA Ops:
  7.3 130.0 %all-gather.7.cloned.1.call-start = ((), (), s32[]{:S(2)}) async-start(), calls=%async_computation.4 | async-start | bytes 6488064 | tf_op jit(solution)/shard_map/all_gather | solution.py:644
  9.2 181.8 %all-gather.9.cloned.1.call-start = ((), (), s32[]{:S(2)}) async-start(), calls=%async_computation.5 | async-start | bytes 2162688 | tf_op jit(solution)/shard_map/all_gather | solution.py:646
  10.8 291.9 %all-gather.11.cloned.1.call-start = ((), (), s32[]{:S(2)}) async-start(), calls=%async_computation.6 | async-start | bytes 17301504 | tf_op jit(solution)/shard_map/all_gather | solution.py:662
  19.9 103.9 %collective-permute-start = (bf16[1024,256]{1,0:T(8,128)(2,1)S(1)}, bf16[1024,256]{1,0:T(8,128)(2,1)S(1)}, u32[]{:S(2)}, u32[]{:S(2)}) collective-permute-start(bf16[1024,256]{1,0:T(8,128)(2,1)S(1)} %get-tuple-element.98.p0), channel_id=1, source_target_pairs={{0,2},{2,0},{4,6},{6,4},{1,3},{3,1},{5,7},{7,5},{8,10},{10,8},{12,... | collective-permute-start | bytes 1572872 | tf_op jit(solution)/shard_map/ppermute | solution.py:48
  21.3 31.5 %collective-permute-start.1 = (bf16[1024,256]{1,0:T(8,128)(2,1)}, bf16[1024,256]{1,0:T(8,128)(2,1)S(1)}, u32[]{:S(2)}, u32[]{:S(2)}) collective-permute-start(bf16[1024,256]{1,0:T(8,128)(2,1)} %get-tuple-element.97), channel_id=1, source_target_pairs={{0,4},{2,6},{4,0},{6,2},{1,5},{3,7},{5,1},{7,3},{8,12},{10,14},{12... | collective-permute-start | bytes 1572872 | tf_op jit(solution)/shard_map/ppermute | solution.py:48
  25.2 105.3 %collective-permute-start.6 = (bf16[1024,256]{1,0:T(8,128)(2,1)S(1)}, bf16[1024,256]{1,0:T(8,128)(2,1)S(1)}, u32[]{:S(2)}, u32[]{:S(2)}) collective-permute-start(bf16[1024,256]{1,0:T(8,128)(2,1)S(1)} %get-tuple-element.96.p0), channel_id=1, source_target_pairs={{0,2},{2,0},{4,6},{6,4},{1,3},{3,1},{5,7},{7,5},{8,10},{10,8},{12,... | collective-permute-start | bytes 1572872 | tf_op jit(solution)/shard_map/ppermute | solution.py:48
  25.4 55.1 %collective-permute-start.7 = (bf16[1024,256]{1,0:T(8,128)(2,1)}, bf16[1024,256]{1,0:T(8,128)(2,1)S(1)}, u32[]{:S(2)}, u32[]{:S(2)}) collective-permute-start(bf16[1024,256]{1,0:T(8,128)(2,1)} %get-tuple-element.95), channel_id=1, source_target_pairs={{0,4},{2,6},{4,0},{6,2},{1,5},{3,7},{5,1},{7,3},{8,12},{10,14},{12... | collective-permute-start | bytes 1572872 | tf_op jit(solution)/shard_map/ppermute | solution.py:48
  52.7 71.0 %collective-permute-start.2 = (bf16[1024,256]{1,0:T(8,128)(2,1)S(1)}, bf16[1024,256]{1,0:T(8,128)(2,1)}, u32[]{:S(2)}, u32[]{:S(2)}) collective-permute-start(bf16[1024,256]{1,0:T(8,128)(2,1)S(1)} %collective-permute-done.1.p2), channel_id=1, source_target_pairs={{0,2},{2,0},{4,6},{6,4},{1,3},{3,1},{5,7},{7,5},{8,10},{10,8},{12,... | collective-permute-start | bytes 1572872 | tf_op jit(solution)/shard_map/ppermute | solution.py:48
  80.5 38.8 %collective-permute-start.8 = (bf16[1024,256]{1,0:T(8,128)(2,1)S(1)}, bf16[1024,256]{1,0:T(8,128)(2,1)}, u32[]{:S(2)}, u32[]{:S(2)}) collective-permute-start(bf16[1024,256]{1,0:T(8,128)(2,1)S(1)} %collective-permute-done.7.p2), channel_id=1, source_target_pairs={{0,2},{2,0},{4,6},{6,4},{1,3},{3,1},{5,7},{7,5},{8,10},{10,8},{12,... | collective-permute-start | bytes 1572872 | tf_op jit(solution)/shard_map/ppermute | solution.py:48
  119.3 67.1 %all-to-all-start = ((bf16[4,512,256]{2,1,0:T(8,128)(2,1)}), bf16[4,512,256]{2,1,0:T(8,128)(2,1)}, u32[]{:S(2)}, u32[]{:S(2)}) async-start(bf16[4,512,256]{2,1,0:T(8,128)(2,1)} %bitcast.238), calls=%async_computation | async-start | bytes 2097152 | tf_op jit(solution)/shard_map/all_to_all | solution.py:674
  183.8 26.4 %collective-permute-start.9 = (bf16[512,512]{1,0:T(8,128)(2,1)}, bf16[512,512]{1,0:T(8,128)(2,1)}, u32[]{:S(2)}, u32[]{:S(2)}) collective-permute-start(bf16[512,512]{1,0:T(8,128)(2,1)} %slice.122), channel_id=1, source_target_pairs={{0,2},{2,0},{4,6},{6,4},{1,3},{3,1},{5,7},{7,5},{8,10},{10,8},{12,... | collective-permute-start | bytes 1572872 | tf_op jit(solution)/shard_map/ppermute | solution.py:48
  346.5 188.9 %all-to-all-start.1 = ((bf16[4,512,256]{2,1,0:T(8,128)(2,1)}), bf16[4,512,256]{2,1,0:T(8,128)(2,1)}, u32[]{:S(2)}, u32[]{:S(2)}) async-start(bf16[4,512,256]{2,1,0:T(8,128)(2,1)} %bitcast.221), calls=%async_computation.1 | async-start | bytes 2097152 | tf_op jit(solution)/shard_map/all_to_all | solution.py:704
  357.4 24.6 %collective-permute-start.10 = (bf16[512,512]{1,0:T(8,128)(2,1)}, bf16[512,512]{1,0:T(8,128)(2,1)S(1)}, u32[]{:S(2)}, u32[]{:S(2)}) collective-permute-start(bf16[512,512]{1,0:T(8,128)(2,1)} %get-tuple-element.53), channel_id=1, source_target_pairs={{0,2},{2,0},{4,6},{6,4},{1,3},{3,1},{5,7},{7,5},{8,10},{10,8},{12,... | collective-permute-start | bytes 1572872 | tf_op jit(solution)/shard_map/ppermute | solution.py:48
  360.1 103.2 %collective-permute-start.20 = (bf16[4,4,256,512]{3,2,1,0:T(8,128)(2,1)}, bf16[4,4,256,512]{3,2,1,0:T(8,128)(2,1)}, u32[]{:S(2)}, u32[]{:S(2)}) collective-permute-start(bf16[4,4,256,512]{3,2,1,0:T(8,128)(2,1)} %get-tuple-element.63), channel_id=1, source_target_pairs={{0,8},{8,0},{16,24},{24,16},{1,9},{9,1},{17,25},{25,17},{2,10},{10... | collective-permute-start | bytes 12582920 | tf_op jit(solution)/shard_map/ppermute | solution.py:48
  368.5 66.8 %collective-permute-start.15 = (bf16[2,4,2,32,4,256]{5,4,3,2,1,0:T(4,128)(2,1)S(1)}, bf16[2,4,2,32,4,256]{5,4,3,2,1,0:T(4,128)(2,1)}, u32[]{:S(2)}, u32[]{:S(2)}) collective-permute-start(bf16[2,4,2,32,4,256]{5,4,3,2,1,0:T(4,128)(2,1)S(1)} %fusion.11), channel_id=1, source_target_pairs={{0,8},{8,0},{16,24},{24,16},{1,9},{9,1},{17,25},{25,17},{2,10},{10... | collective-permute-start | bytes 3145736 | tf_op jit(solution)/shard_map/ppermute | solution.py:48
  369.0 101.8 %collective-permute-start.25 = (bf16[4,4,256,512]{3,2,1,0:T(8,128)(2,1)}, bf16[4,4,256,512]{3,2,1,0:T(8,128)(2,1)}, u32[]{:S(2)}, u32[]{:S(2)}) collective-permute-start(bf16[4,4,256,512]{3,2,1,0:T(8,128)(2,1)} %get-tuple-element.65), channel_id=1, source_target_pairs={{0,8},{8,0},{16,24},{24,16},{1,9},{9,1},{17,25},{25,17},{2,10},{10... | collective-permute-start | bytes 12582920 | tf_op jit(solution)/shard_map/ppermute | solution.py:48
  428.4 28.8 %collective-permute-start.11 = (bf16[512,1024]{1,0:T(8,128)(2,1)}, bf16[512,1024]{1,0:T(8,128)(2,1)S(1)}, u32[]{:S(2)}, u32[]{:S(2)}) collective-permute-start(bf16[512,1024]{1,0:T(8,128)(2,1)} %slice.177), channel_id=1, source_target_pairs={{0,2},{2,0},{4,6},{6,4},{1,3},{3,1},{5,7},{7,5},{8,10},{10,8},{12,... | collective-permute-start | bytes 3145736 | tf_op jit(solution)/shard_map/ppermute | solution.py:48
  438.4 23.6 %collective-permute-start.16 = (bf16[2,4,32,4,256]{4,3,2,1,0:T(4,128)(2,1)}, bf16[2,4,32,4,256]{4,3,2,1,0:T(4,128)(2,1)}, u32[]{:S(2)}, u32[]{:S(2)}) collective-permute-start(bf16[2,4,32,4,256]{4,3,2,1,0:T(4,128)(2,1)} %dynamic-slice_bitcast_fusion.3), channel_id=1, source_target_pairs={{0,16},{8,24},{16,0},{24,8},{1,17},{9,25},{17,1},{25,9},{2,18},{10... | collective-permute-start | bytes 1572872 | tf_op jit(solution)/shard_map/ppermute | solution.py:48
  453.9 89.6 %collective-permute-start.12 = (bf16[4,3,2,32,4,256]{5,4,3,2,1,0:T(4,128)(2,1)}, bf16[4,3,2,32,4,256]{5,4,3,2,1,0:T(4,128)(2,1)}, u32[]{:S(2)}, u32[]{:S(2)}) collective-permute-start(bf16[4,3,2,32,4,256]{5,4,3,2,1,0:T(4,128)(2,1)} %fusion.6), channel_id=1, source_target_pairs={{0,8},{8,0},{16,24},{24,16},{1,9},{9,1},{17,25},{25,17},{2,10},{10... | collective-permute-start | bytes 4718600 | tf_op jit(solution)/shard_map/ppermute | solution.py:48
  461.4 18.5 %collective-permute-start.30 = (f32[5,1024]{1,0:T(8,128)S(1)}, f32[5,1024]{1,0:T(8,128)S(1)}, u32[]{:S(2)}, u32[]{:S(2)}) collective-permute-start(f32[5,1024]{1,0:T(8,128)S(1)} %pad_maximum_fusion.3), channel_id=1, source_target_pairs={{0,8},{8,0},{16,24},{24,16},{1,9},{9,1},{17,25},{25,17},{2,10},{10... | collective-permute-start | bytes 61448 | tf_op jit(solution)/shard_map/ppermute | solution.py:48
  470.1 77.3 %collective-permute-start.21 = (bf16[2,4,256,512]{3,2,1,0:T(8,128)(2,1)}, bf16[2,4,256,512]{3,2,1,0:T(8,128)(2,1)}, u32[]{:S(2)}, u32[]{:S(2)}) collective-permute-start(bf16[2,4,256,512]{3,2,1,0:T(8,128)(2,1)} %slice.152), channel_id=1, source_target_pairs={{0,16},{8,24},{16,0},{24,8},{1,17},{9,25},{17,1},{25,9},{2,18},{10... | collective-permute-start | bytes 6291464 | tf_op jit(solution)/shard_map/ppermute | solution.py:48
  477.6 73.8 %collective-permute-start.26 = (bf16[1,1,2,4,256,512]{5,4,3,2,1,0:T(8,128)(2,1)}, bf16[1,1,2,4,256,512]{5,4,3,2,1,0:T(8,128)(2,1)}, u32[]{:S(2)}, u32[]{:S(2)}) collective-permute-start(bf16[1,1,2,4,256,512]{5,4,3,2,1,0:T(8,128)(2,1)} %slice_bitcast_fusion), channel_id=1, source_target_pairs={{0,1},{1,0},{2,3},{3,2},{4,5},{5,4},{6,7},{7,6},{8,9},{9,8},{10,11... | collective-permute-start | bytes 6291464 | tf_op jit(solution)/shard_map/ppermute | solution.py:48
  478.8 52.5 %collective-permute-start.17 = (bf16[2,2,32,4,256]{4,2,1,0,3:T(8,128)(2,1)S(1)}, bf16[2,2,32,4,256]{4,2,1,0,3:T(8,128)(2,1)S(1)}, u32[]{:S(2)}, u32[]{:S(2)}) collective-permute-start(bf16[2,2,32,4,256]{4,2,1,0,3:T(8,128)(2,1)S(1)} %bitcast.244), channel_id=1, source_target_pairs={{0,1},{1,0},{2,3},{3,2},{4,5},{5,4},{6,7},{7,6},{8,9},{9,8},{10,11... | collective-permute-start | bytes 786440 | tf_op jit(solution)/shard_map/ppermute | solution.py:48
  480.0 38.6 %collective-permute-start.31 = (f32[5,1024]{1,0:T(8,128)S(1)}, f32[5,1024]{1,0:T(8,128)S(1)}, u32[]{:S(2)}, u32[]{:S(2)}) collective-permute-start(f32[5,1024]{1,0:T(8,128)S(1)} %fusion.31), channel_id=1, source_target_pairs={{0,16},{8,24},{16,0},{24,8},{1,17},{9,25},{17,1},{25,9},{2,18},{10... | collective-permute-start | bytes 61448 | tf_op jit(solution)/shard_map/ppermute | solution.py:48
  535.4 34.7 %all-to-all-start.2 = ((bf16[4,512,256]{2,1,0:T(8,128)(2,1)}), bf16[4,512,256]{2,1,0:T(8,128)(2,1)}, u32[]{:S(2)}, u32[]{:S(2)}) async-start(bf16[4,512,256]{2,1,0:T(8,128)(2,1)} %get-tuple-element.59), calls=%async_computation.2 | async-start | bytes 2097152 | tf_op jit(solution)/shard_map/all_to_all | solution.py:715
  546.6 20.5 %collective-permute-start.13 = (bf16[4,3,32,4,256]{4,3,2,1,0:T(4,128)(2,1)S(1)}, bf16[4,3,32,4,256]{4,3,2,1,0:T(4,128)(2,1)S(1)}, u32[]{:S(2)}, u32[]{:S(2)}) collective-permute-start(bf16[4,3,32,4,256]{4,3,2,1,0:T(4,128)(2,1)S(1)} %dynamic-slice_bitcast_fusion), channel_id=1, source_target_pairs={{0,16},{8,24},{16,0},{24,8},{1,17},{9,25},{17,1},{25,9},{2,18},{10... | collective-permute-start | bytes 2359304 | tf_op jit(solution)/shard_map/ppermute | solution.py:48
  549.9 26.2 %collective-permute-start.22 = (bf16[1,4,256,512]{3,2,1,0:T(8,128)(2,1)S(1)}, bf16[1,4,256,512]{3,2,1,0:T(8,128)(2,1)}, u32[]{:S(2)}, u32[]{:S(2)}) collective-permute-start(bf16[1,4,256,512]{3,2,1,0:T(8,128)(2,1)S(1)} %slice.154), channel_id=1, source_target_pairs={{0,1},{1,0},{2,3},{3,2},{4,5},{5,4},{6,7},{7,6},{8,9},{9,8},{10,11... | collective-permute-start | bytes 3145736 | tf_op jit(solution)/shard_map/ppermute | solution.py:48
  554.8 32.1 %collective-permute-start.27 = (bf16[4,256,512]{2,1,0:T(8,128)(2,1)}, bf16[4,256,512]{2,1,0:T(8,128)(2,1)}, u32[]{:S(2)}, u32[]{:S(2)}) collective-permute-start(bf16[4,256,512]{2,1,0:T(8,128)(2,1)} %slice_bitcast_fusion.2), channel_id=1, source_target_pairs={{0,16},{8,24},{16,0},{24,8},{1,17},{9,25},{17,1},{25,9},{2,18},{10... | collective-permute-start | bytes 3145736 | tf_op jit(solution)/shard_map/ppermute | solution.py:48
  569.3 23.1 %collective-permute-start.14 = (bf16[2,3,32,4,256]{4,2,3,1,0:T(8,128)(2,1)}, bf16[2,3,32,4,256]{4,2,3,1,0:T(8,128)(2,1)S(1)}, u32[]{:S(2)}, u32[]{:S(2)}) collective-permute-start(bf16[2,3,32,4,256]{4,2,3,1,0:T(8,128)(2,1)} %dynamic-slice_bitcast_fusion.6), channel_id=1, source_target_pairs={{0,1},{1,0},{2,3},{3,2},{4,5},{5,4},{6,7},{7,6},{8,9},{9,8},{10,11... | collective-permute-start | bytes 1179656 | tf_op jit(solution)/shard_map/ppermute | solution.py:48
  578.4 37.2 %collective-permute-start.23 = (bf16[2,256,512]{2,1,0:T(8,128)(2,1)}, bf16[2,256,512]{2,1,0:T(8,128)(2,1)}, u32[]{:S(2)}, u32[]{:S(2)}) collective-permute-start(bf16[2,256,512]{2,1,0:T(8,128)(2,1)} %dynamic-slice_bitcast_fusion.2), channel_id=1, source_target_pairs={{0,4},{2,6},{4,0},{6,2},{1,5},{3,7},{5,1},{7,3},{8,12},{10,14},{12... | collective-permute-start | bytes 1572872 | tf_op jit(solution)/shard_map/ppermute | solution.py:48
  589.0 37.9 %collective-permute-start.28 = (bf16[2,256,512]{1,2,0:T(8,128)(2,1)S(1)}, bf16[2,256,512]{1,2,0:T(8,128)(2,1)}, u32[]{:S(2)}, u32[]{:S(2)}) collective-permute-start(bf16[2,256,512]{1,2,0:T(8,128)(2,1)S(1)} %dynamic-slice_bitcast_fusion.1), channel_id=1, source_target_pairs={{0,4},{2,6},{4,0},{6,2},{1,5},{3,7},{5,1},{7,3},{8,12},{10,14},{12... | collective-permute-start | bytes 1572872 | tf_op jit(solution)/shard_map/ppermute | solution.py:48
  594.4 36.1 %all-to-all-start.3 = ((bf16[4,192,256]{2,1,0:T(8,128)(2,1)}), bf16[4,192,256]{2,1,0:T(8,128)(2,1)S(1)}, u32[]{:S(2)}, u32[]{:S(2)}) async-start(bf16[4,192,256]{2,1,0:T(8,128)(2,1)} %bitcast.44), calls=%async_computation.3 | async-start | bytes 786432 | tf_op jit(solution)/shard_map/all_to_all | solution.py:747
  (80 other events, 793.0 us)
Sparse Core Ops, SparseCore 0:
  11.5 105.8 all-gather.6
  120.9 65.4 all-gather.8
  189.4 113.1 all-gather.10

commit v2 on v1

v2 whole, which is shorter than its diff:
```python
import functools

import jax
import jax.numpy as jnp
from jax import lax
from jax.experimental import pallas as pl
from jax.experimental.pallas import tpu as pltpu
from jax.sharding import PartitionSpec as P

D = 1024
DH = 128
MEM = 512
CMEM = 512
RATE = 3
NEWC = 128
SEQ_LEN = 1024
HALF = SEQ_LEN // 2
HEADS = 4
OLD = RATE * NEWC
MROWS = CMEM + MEM
KM = MROWS + NEWC
QUARTER = D // 4
CHUNK = 256
LIMIT = 60

EPSILON = 1e-05
MASKED = -1e30
LOG2E = 1.4426950408889634
SCALE = DH**-0.5
SCALE2 = SCALE * LOG2E
F32 = jnp.float32
BF = jnp.bfloat16


def nn(a, b):
    return lax.dot_general(a, b, (((1,), (0,)), ((), ())), preferred_element_type=F32)


def nt(a, b):
    return lax.dot_general(a, b, (((1,), (1,)), ((), ())), preferred_element_type=F32)


def tn(a, b):
    return lax.dot_general(a, b, (((0,), (0,)), ((), ())), preferred_element_type=F32)


def swap(x, axis, distance):
    n = lax.axis_size(axis)
    return lax.ppermute(x, axis, [(i, i ^ distance) for i in range(n)])


def add_low(a, b):
    return (a.astype(F32) + b.astype(F32)).astype(BF)


def params(limit_mb, dims=1):
    return pltpu.CompilerParams(
        dimension_semantics=("arbitrary",) * dims, vmem_limit_bytes=limit_mb << 20
    )


ANY = pl.BlockSpec(memory_space=pl.ANY)


def cost(flops):
    return pl.CostEstimate(flops=flops, transcendentals=0, bytes_accessed=flops // 1000)


def shape(dims, kind):
    return jax.ShapeDtypeStruct(dims, kind)


def whole(dims):
    zeros = (0,) * len(dims)
    return pl.BlockSpec(dims, lambda *_: zeros)


def norm_block(pieces, gain_ref):
    values = [p.astype(F32) for p in pieces]
    mean = sum(jnp.sum(v, axis=1, keepdims=True) for v in values) / D
    values = [v - mean for v in values]
    spread = sum(jnp.sum(v * v, axis=1, keepdims=True) for v in values) / D
    factor = lax.rsqrt(spread + EPSILON)
    return [values[k] * factor * gain_ref[:, block_of(k)] for k in range(4)]


def block_of(k):
    return slice(k * QUARTER, (k + 1) * QUARTER)


def tok_norm_kernel(where, p0, p1, p2, p3, gain_ref, low_ref, raw_ref):
    pieces = [p[...] for p in (p0, p1, p2, p3)]
    normed = norm_block(pieces, gain_ref)
    for k in range(4):
        low_ref[:, block_of(k)] = normed[k].astype(BF)
        raw_ref[:, block_of(k)] = pieces[k]


def tok_norm(where, pieces, gain):
    block = 256
    count = SEQ_LEN // block
    piece = pl.BlockSpec((block, QUARTER), lambda i, w: ((i + w[0] * (count // 2)) % count, 0))
    out = pl.BlockSpec((block, D), lambda i, w: (i, 0))
    return pl.pallas_call(
        tok_norm_kernel,
        out_shape=(shape((SEQ_LEN, D), BF), shape((SEQ_LEN, D), BF)),
        grid_spec=pltpu.PrefetchScalarGridSpec(
            num_scalar_prefetch=1,
            grid=(count,),
            in_specs=[piece] * 4 + [whole((1, D))],
            out_specs=[out, out],
        ),
        compiler_params=params(LIMIT),
        name="tok_norm",
    )(where, *pieces, gain)


def mem_norm_kernel(p0, p1, p2, p3, gain_ref, conv_ref, low_ref, raw_ref, keep_ref):
    for block in range(MROWS // 256):
        rows = slice(block * 256, block * 256 + 256)
        pieces = [p[rows, :] for p in (p0, p1, p2, p3)]
        normed = norm_block(pieces, gain_ref)
        for k in range(4):
            low_ref[rows, block_of(k)] = normed[k].astype(BF)
            raw_ref[rows, block_of(k)] = pieces[k]
            if block * 256 >= CMEM:
                start = block * 256 - CMEM
                for j in range(2):
                    keep_ref[k * 2 + j, start : start + 256, :] = normed[k][:, j * DH : j * DH + DH]
    for j in range(D // DH):
        lanes = slice(j * DH, j * DH + DH)
        packed = 0.0
        for t in range(RATE):
            picked = keep_ref[j, pl.ds(t, NEWC, stride=RATE), :]
            packed = packed + conv_ref[t : t + 1, lanes] * picked
        low_ref[MROWS:, lanes] = packed.astype(BF)


def mem_norm(pieces, gain, conv):
    return pl.pallas_call(
        mem_norm_kernel,
        out_shape=(shape((KM, D), BF), shape((MROWS, D), BF)),
        grid=(1,),
        in_specs=[whole((MROWS, QUARTER))] * 4 + [whole((1, D)), whole((RATE, D))],
        out_specs=[whole((KM, D)), whole((MROWS, D))],
        scratch_shapes=[pltpu.VMEM((D // DH, MEM, DH), F32)],
        compiler_params=params(LIMIT),
        name="mem_norm",
    )(*pieces, gain, conv)


def join_kernel(*refs):
    parts, (tok_ref, mem_ref, back_ref) = refs[:4], refs[4:]
    cols, _, part, _, span, _ = parts[0].shape
    for head in range(HEADS):
        c, i = head // part, head % part
        for kind in range(5):
            for dp, ref in enumerate(parts):
                low = dp * span
                for k in range(4):
                    value = ref[c, k, i, kind]
                    if kind < 3:
                        row = (head * 3 + kind) * DH + low
                        tok_ref[row : row + span, block_of(k)] = value
                    if 0 < kind < 3:
                        row = (head * 2 + kind - 1) * DH + low
                        mem_ref[row : row + span, block_of(k)] = value
                    if kind > 2:
                        row = ((kind - 3) * HEADS + head) * DH + low
                        back_ref[row : row + span, block_of(k)] = value


def join_weights(parts):
    dims = ((HEADS * 3 * DH, D), (HEADS * 2 * DH, D), (HEADS * 2 * DH, D))
    return pl.pallas_call(
        join_kernel,
        out_shape=tuple(shape(d, BF) for d in dims),
        grid=(1,),
        in_specs=[whole(p.shape) for p in parts],
        out_specs=[whole(d) for d in dims],
        compiler_params=params(LIMIT),
        name="join_weights",
    )(*parts)


def fill_bias(bias_ref, row_ref, col_ref):
    seg_q, pos_q = row_ref[0:1, :], row_ref[1:2, :]

    def memory_chunk(c, carry):
        rows = pl.ds(pl.multiple_of(c * CHUNK, CHUNK), CHUNK)
        bias_ref[rows, :] = jnp.where(col_ref[rows, 2:3] == seg_q, 0.0, MASKED)
        return carry

    def token_chunk(c, carry):
        start = pl.multiple_of(c * CHUNK, CHUNK)
        rows = pl.ds(start, CHUNK)
        same = (col_ref[rows, 0:1] == seg_q) & (col_ref[rows, 1:2] <= pos_q)
        key_id = lax.broadcasted_iota(jnp.int32, (CHUNK, SEQ_LEN), 0) + start
        query_id = lax.broadcasted_iota(jnp.int32, (CHUNK, SEQ_LEN), 1)
        target = pl.ds(pl.multiple_of(MROWS + c * CHUNK, CHUNK), CHUNK)
        bias_ref[target, :] = jnp.where(same | (key_id == query_id), 0.0, MASKED)
        return carry

    lax.fori_loop(0, MROWS // CHUNK, memory_chunk, 0)
    lax.fori_loop(0, SEQ_LEN // CHUNK, token_chunk, 0)


def forward_kernel(tok_ref, mem_ref, row_ref, col_ref, o_ref, log_ref, bias_ref, s_ref, acc_ref):
    @pl.when(pl.program_id(0) == 0)
    def _():
        fill_bias(bias_ref, row_ref, col_ref)

    queries = tok_ref[:, :DH]

    def scores(key_ref, columns, offset):
        def step(c, top):
            rows = pl.ds(pl.multiple_of(c * CHUNK, CHUNK), CHUNK)
            target = pl.ds(pl.multiple_of(offset + c * CHUNK, CHUNK), CHUNK)
            s = nt(key_ref[rows, columns], queries) * SCALE2 + bias_ref[target, :]
            s_ref[target, :] = s
            return jnp.maximum(top, jnp.max(s.reshape(CHUNK // 8, 8, SEQ_LEN), axis=0))

        return step

    top = jnp.full((8, SEQ_LEN), -3.0e38, F32)
    top = lax.fori_loop(0, MROWS // CHUNK, scores(mem_ref, slice(0, DH), 0), top)
    top = lax.fori_loop(0, SEQ_LEN // CHUNK, scores(tok_ref, slice(DH, 2 * DH), MROWS), top)
    top = jnp.max(top, axis=0, keepdims=True)
    acc_ref[...] = jnp.zeros_like(acc_ref)

    def values(value_ref, columns, offset):
        def step(c, total):
            rows = pl.ds(pl.multiple_of(c * CHUNK, CHUNK), CHUNK)
            target = pl.ds(pl.multiple_of(offset + c * CHUNK, CHUNK), CHUNK)
            p = jnp.exp2(s_ref[target, :] - top)
            acc_ref[...] += nn(value_ref[rows, columns].T, p.astype(BF))
            return total + jnp.sum(p.reshape(CHUNK // 8, 8, SEQ_LEN), axis=0)

        return step

    total = jnp.zeros((8, SEQ_LEN), F32)
    total = lax.fori_loop(0, MROWS // CHUNK, values(mem_ref, slice(DH, 2 * DH), 0), total)
    total = lax.fori_loop(
        0, SEQ_LEN // CHUNK, values(tok_ref, slice(2 * DH, 3 * DH), MROWS), total
    )
    total = jnp.sum(total, axis=0, keepdims=True)
    o_ref[...] = (acc_ref[...] / total).T.astype(BF)
    log_ref[...] = (top + jnp.log2(total)).reshape(1, 1, SEQ_LEN)


def attention_forward(tok_p, mem_p, row_attr, col_attr):
    return pl.pallas_call(
        forward_kernel,
        out_shape=(shape((SEQ_LEN, HEADS * DH), BF), shape((HEADS, 1, SEQ_LEN), F32)),
        grid=(HEADS,),
        in_specs=[
            pl.BlockSpec((SEQ_LEN, 3 * DH), lambda h: (0, h)),
            pl.BlockSpec((KM, 2 * DH), lambda h: (0, h)),
            whole(row_attr.shape),
            whole(col_attr.shape),
        ],
        out_specs=[
            pl.BlockSpec((SEQ_LEN, DH), lambda h: (0, h)),
            pl.BlockSpec((1, 1, SEQ_LEN), lambda h: (h, 0, 0)),
        ],
        scratch_shapes=[
            pltpu.VMEM((MROWS + SEQ_LEN, SEQ_LEN), F32),
            pltpu.VMEM((MROWS + SEQ_LEN, SEQ_LEN), F32),
            pltpu.VMEM((DH, SEQ_LEN), F32),
        ],
        compiler_params=params(LIMIT),
        cost_estimate=cost(25_000_000_000),
        name="attention_forward",
    )(tok_p, mem_p, row_attr, col_attr)


def recon_kernel(tok_ref, mem_ref, _, gq_ref, gm_ref):
    q = tok_ref[:, :DH]
    old, new = slice(CMEM, CMEM + OLD), slice(MROWS, KM)
    keys, values = slice(0, DH), slice(DH, 2 * DH)

    def softmax_rows(key_rows):
        s = nt(key_rows, q) * SCALE2
        p = jnp.exp2(s - jnp.max(s, axis=0, keepdims=True))
        return p / jnp.sum(p, axis=0, keepdims=True)

    ko, vo, kn, vn = mem_ref[old, keys], mem_ref[old, values], mem_ref[new, keys], mem_ref[new, values]
    po, pn = softmax_rows(ko), softmax_rows(kn)
    po_low, pn_low = po.astype(BF), pn.astype(BF)
    out_o, out_n = nn(vo.T, po_low), nn(vn.T, pn_low)
    gap = (out_o - out_n).astype(BF)
    gap32 = gap.astype(F32)
    do = (po * (nn(vo, gap) - jnp.sum(gap32 * out_o, axis=0, keepdims=True))).astype(BF)
    dn = (pn * (jnp.sum(gap32 * out_n, axis=0, keepdims=True) - nn(vn, gap))).astype(BF)
    gq_ref[...] = ((nn(ko.T, do) + nn(kn.T, dn)) * SCALE).reshape(1, DH, SEQ_LEN)
    gap_t = gap32.T.astype(BF)
    gm_ref[:OLD, keys] = nn(do, q) * SCALE
    gm_ref[:OLD, values] = nn(po_low, gap_t)
    gm_ref[OLD:MEM, :] = jnp.zeros((MEM - OLD, 2 * DH), F32)
    gm_ref[MEM:, keys] = nn(dn, q) * SCALE
    gm_ref[MEM:, values] = -nn(pn_low, gap_t)


def reconstruction(tok_p, mem_p, earlier):
    return pl.pallas_call(
        recon_kernel,
        out_shape=(
            shape((HEADS, DH, SEQ_LEN), F32),
            shape((MEM + NEWC, HEADS * 2 * DH), F32),
        ),
        grid=(HEADS,),
        in_specs=[
            pl.BlockSpec((SEQ_LEN, 3 * DH), lambda h: (0, h)),
            pl.BlockSpec((KM, 2 * DH), lambda h: (0, h)),
            ANY,
        ],
        out_specs=[
            pl.BlockSpec((1, DH, SEQ_LEN), lambda h: (h, 0, 0)),
            pl.BlockSpec((MEM + NEWC, 2 * DH), lambda h: (0, h)),
        ],
        compiler_params=params(LIMIT),
        cost_estimate=cost(10_000_000_000),
        name="reconstruction",
    )(tok_p, mem_p, earlier)


def backward_kernel(
    tok_ref, mem_ref, own_ref, got_ref, o_ref, log_ref, rq_ref, rm_ref, row_ref, col_ref,
    *refs,
):
    gt_ref, gm_ref, bias_ref, acc_ref = refs[-4:]

    @pl.when(pl.program_id(0) == 0)
    def _():
        fill_bias(bias_ref, row_ref, col_ref)

    q = tok_ref[:, :DH]
    go = jnp.concatenate([own_ref[...], got_ref[...]], axis=0)
    product = go.astype(F32) * o_ref[...].astype(F32)
    delta = jnp.sum(product.T, axis=0, keepdims=True)
    log_total = log_ref[...].reshape(1, SEQ_LEN)
    acc_ref[...] = rq_ref[...].reshape(DH, SEQ_LEN)

    def piece(k, v, offset):
        s = nt(k, q) * SCALE2 + bias_ref[offset, :]
        p = jnp.exp2(s - log_total)
        d = (p * (nt(v, go) - delta)).astype(BF)
        acc_ref[...] += nn(k.T, d) * SCALE
        return nn(d, q) * SCALE, nn(p.astype(BF), go)

    def memory_chunk(c, carry):
        rows = pl.ds(pl.multiple_of(c * CHUNK, CHUNK), CHUNK)
        gk, gv = piece(mem_ref[rows, :DH], mem_ref[rows, DH:], rows)
        gm_ref[rows, :DH] = gk.astype(BF)
        gm_ref[rows, DH:] = gv.astype(BF)
        return carry

    def shared_chunk(c, carry):
        rows = pl.ds(pl.multiple_of(c * CHUNK, CHUNK), CHUNK)
        extra = pl.ds(pl.multiple_of(c * CHUNK - CMEM, CHUNK), CHUNK)
        gk, gv = piece(mem_ref[rows, :DH], mem_ref[rows, DH:], rows)
        gm_ref[rows, :DH] = (gk + rm_ref[extra, :DH]).astype(BF)
        gm_ref[rows, DH:] = (gv + rm_ref[extra, DH:]).astype(BF)
        return carry

    def token_chunk(c, carry):
        rows = pl.ds(pl.multiple_of(c * CHUNK, CHUNK), CHUNK)
        target = pl.ds(pl.multiple_of(MROWS + c * CHUNK, CHUNK), CHUNK)
        gk, gv = piece(tok_ref[rows, DH : 2 * DH], tok_ref[rows, 2 * DH :], target)
        gt_ref[rows, DH : 2 * DH] = gk.astype(BF)
        gt_ref[rows, 2 * DH :] = gv.astype(BF)
        return carry

    lax.fori_loop(0, CMEM // CHUNK, memory_chunk, 0)
    lax.fori_loop(CMEM // CHUNK, MROWS // CHUNK, shared_chunk, 0)
    lax.fori_loop(0, SEQ_LEN // CHUNK, token_chunk, 0)
    gm_ref[MROWS:, :] = rm_ref[MEM:, :].astype(BF)
    gt_ref[:, :DH] = acc_ref[...].T.astype(BF)


def attention_backward(
    tok_p, mem_p, go_own, go_got, o, logs, rec_q, rec_m, row_attr, col_attr, *earlier
):
    half = pl.BlockSpec((HALF, DH), lambda h: (0, h))
    return pl.pallas_call(
        backward_kernel,
        out_shape=(
            shape((SEQ_LEN, HEADS * 3 * DH), BF),
            shape((KM, HEADS * 2 * DH), BF),
        ),
        grid=(HEADS,),
        in_specs=[
            pl.BlockSpec((SEQ_LEN, 3 * DH), lambda h: (0, h)),
            pl.BlockSpec((KM, 2 * DH), lambda h: (0, h)),
            half,
            half,
            pl.BlockSpec((SEQ_LEN, DH), lambda h: (0, h)),
            pl.BlockSpec((1, 1, SEQ_LEN), lambda h: (h, 0, 0)),
            pl.BlockSpec((1, DH, SEQ_LEN), lambda h: (h, 0, 0)),
            pl.BlockSpec((MEM + NEWC, 2 * DH), lambda h: (0, h)),
            whole(row_attr.shape),
            whole(col_attr.shape),
        ]
        + [ANY] * len(earlier),
        out_specs=[
            pl.BlockSpec((SEQ_LEN, 3 * DH), lambda h: (0, h)),
            pl.BlockSpec((KM, 2 * DH), lambda h: (0, h)),
        ],
        scratch_shapes=[
            pltpu.VMEM((MROWS + SEQ_LEN, SEQ_LEN), F32),
            pltpu.VMEM((DH, SEQ_LEN), F32),
        ],
        compiler_params=params(LIMIT),
        cost_estimate=cost(35_000_000_000),
        name="attention_backward",
    )(tok_p, mem_p, go_own, go_got, o, logs, rec_q, rec_m, row_attr, col_attr, *earlier)


def center_rows(rows):
    centered = rows - jnp.mean(rows, axis=1, keepdims=True)
    factor = lax.rsqrt(jnp.mean(centered * centered, axis=1, keepdims=True) + EPSILON)
    return centered * factor, factor


def mid_kernel(raw_ref, own_ref, got_ref, w_ref, gain_ref, _, mid_ref, x2_ref):
    width = own_ref.shape[1]
    mid = raw_ref[...].astype(F32) + (
        nn(own_ref[...], w_ref[:width, :]) + nn(got_ref[...], w_ref[width:, :])
    )
    unit, _ = center_rows(mid)
    mid_ref[...] = mid
    x2_ref[...] = (unit * gain_ref[...]).astype(BF)


def residual_mid(raw, o, o_got, w_out, gain, earlier):
    block = 256
    rows = lambda width: pl.BlockSpec((block, width), lambda i: (i, 0))
    return pl.pallas_call(
        mid_kernel,
        out_shape=(shape((HALF, D), F32), shape((HALF, D), BF)),
        grid=(HALF // block,),
        in_specs=[rows(D), rows(HEADS * DH), rows(HEADS * DH), whole((D, D)), whole((1, D)), ANY],
        out_specs=[rows(D), rows(D)],
        compiler_params=params(LIMIT),
        cost_estimate=cost(4 * HALF * D * D),
        name="residual_mid",
    )(raw, o, o_got, w_out, gain, earlier)


TILE = 256


def ffn_kernel(*refs):
    x_own, x_got, c_own, c_got = refs[:4]
    plain, far_up, far_down = refs[4:7], refs[7], refs[8]
    out_keep, out_send, gx_keep, gx_send = refs[9:13]
    grads = refs[13:18]
    x_ref, xt_ref, c_ref, ct_ref, out_ref, gx_ref, up_ref, down_ref = refs[18:]
    step, last = pl.program_id(0), pl.num_programs(0) - 1
    block = step // (pl.num_programs(0) // 4)

    @pl.when(step == 0)
    def _():
        out_ref[...] = jnp.zeros_like(out_ref)
        gx_ref[...] = jnp.zeros_like(gx_ref)
        for (own, got), full, turned in (
            ((x_own, x_got), x_ref, xt_ref),
            ((c_own, c_got), c_ref, ct_ref),
        ):
            for j, half in enumerate((own, got)):
                full[j * HALF : (j + 1) * HALF, :] = half[...]
                for i in range(0, HALF, 256):
                    turned[:, j * HALF + i : j * HALF + i + 256] = half[i : i + 256, :].T

    for k, ref in enumerate(plain):
        @pl.when(block == k)
        def _():
            up_ref[...] = ref[0].reshape(D, TILE)
            down_ref[...] = ref[1].reshape(D, TILE)

    @pl.when(block == 3)
    def _():
        up_ref[...] = far_up[...].reshape(D, TILE)
        down_ref[...] = far_down[...].reshape(D, TILE)

    w_up, w_down = up_ref[...], down_ref[...]
    v = nn(x_ref[...], w_up)
    g_act = nn(c_ref[...], w_down)
    c0, c1 = 0.7978845608028654, 0.044715
    v2 = v * v
    t = jnp.tanh(c0 * v * (1.0 + c1 * v2))
    half = 0.5 * (1.0 + t)
    act = (v * half).astype(BF)
    slope = half + (0.5 * c0) * v * (1.0 - t * t) * (1.0 + (3.0 * c1) * v2)
    g_pre = (g_act * slope).astype(BF)
    out_ref[...] += nt(act, w_down)
    gx_ref[...] += nt(g_pre, w_up)
    grad_up = nn(xt_ref[...], g_pre).astype(BF).reshape(4, QUARTER, TILE)
    grad_down = nn(ct_ref[...], act).astype(BF).reshape(4, QUARTER, TILE)

    for k in range(3):
        @pl.when(block == k)
        def _():
            grads[k][0] = grad_up
            grads[k][1] = grad_down

    @pl.when(block == 3)
    def _():
        grads[3][...] = grad_up
        grads[4][...] = grad_down

    @pl.when(step == last)
    def _():
        for total, keep, send in ((out_ref, out_keep, out_send), (gx_ref, gx_keep, gx_send)):
            keep[...] = total[:HALF, :]
            send[...] = total[HALF:, :].astype(BF)


def feed_forward(x2, x2_got, cot, cot_got, plain, far_up, far_down):
    width = far_up.shape[-1]
    tiles = width // TILE

    def tile(k, step):
        return jnp.clip(step - k * tiles, 0, tiles - 1)

    def pair(k):
        return pl.BlockSpec((2, 4, QUARTER, TILE), lambda i: (0, 0, 0, tile(k, i)))

    far = pl.BlockSpec((4, QUARTER, TILE), lambda i: (0, 0, tile(3, i)))
    blocks = [pair(0), pair(1), pair(2), far, far]
    once = pl.BlockSpec((HALF, D), lambda i: (0, 0), pipeline_mode=pl.Buffered(1))
    rows = whole((HALF, D))
    full, turned = pltpu.VMEM((SEQ_LEN, D), BF), pltpu.VMEM((D, SEQ_LEN), BF)
    total = pltpu.VMEM((SEQ_LEN, D), F32)
    return pl.pallas_call(
        ffn_kernel,
        out_shape=(
            shape((HALF, D), F32), shape((HALF, D), BF),
            shape((HALF, D), F32), shape((HALF, D), BF),
        )
        + (shape(plain[0].shape, BF),) * 3
        + (shape(far_up.shape, BF),) * 2,
        grid=(4 * tiles,),
        in_specs=[once] * 4 + blocks,
        out_specs=[rows] * 4 + blocks,
        scratch_shapes=[full, turned, full, turned, total, total] + [pltpu.VMEM((D, TILE), BF)] * 2,
        compiler_params=params(LIMIT),
        cost_estimate=cost(12 * SEQ_LEN * D * 4 * width),
        name="feed_forward",
    )(x2, x2_got, cot, cot_got, *plain, far_up, far_down)


def mid_back_kernel(gx_ref, got_ref, mid_ref, cot_ref, gain_ref, w_ref, gm_ref, ga_ref, keep_ref, send_ref, gn_ref):
    @pl.when(pl.program_id(0) == 0)
    def _():
        gn_ref[...] = jnp.zeros_like(gn_ref)

    unit, factor = center_rows(mid_ref[...])
    gx = gx_ref[...] + got_ref[...].astype(F32)
    gn_ref[...] += jnp.sum(gx * unit, axis=0, keepdims=True)
    s = gx * gain_ref[...]
    g_mid = cot_ref[...].astype(F32) + factor * (
        s - jnp.mean(s, axis=1, keepdims=True) - unit * jnp.mean(s * unit, axis=1, keepdims=True)
    )
    gm_ref[...] = g_mid
    low = g_mid.astype(BF)
    ga_ref[...] = low
    width = keep_ref.shape[1]
    send_ref[...] = nt(low, w_ref[width:, :]).astype(BF)
    keep_ref[...] = nt(low, w_ref[:width, :]).astype(BF)


def mid_back(gx, gx_got, mid, cot, gain, w_out):
    block = 256
    rows = lambda width: pl.BlockSpec((block, width), lambda i: (i, 0))
    half = shape((HALF, HEADS * DH), BF)
    return pl.pallas_call(
        mid_back_kernel,
        out_shape=(shape((HALF, D), F32), shape((HALF, D), BF), half, half, shape((1, D), F32)),
        grid=(HALF // block,),
        in_specs=[rows(D)] * 4 + [whole((1, D)), whole((D, D))],
        out_specs=[rows(D), rows(D), rows(HEADS * DH), rows(HEADS * DH), whole((1, D))],
        compiler_params=params(LIMIT),
        cost_estimate=cost(2 * HALF * D * D),
        name="mid_back",
    )(gx, gx_got, mid, cot, gain, w_out)


def tok_grad_kernel(g_ref, w_ref, raw_ref, *refs):
    keep_ref, send_ref, gn_ref = refs[-3:]
    step = pl.program_id(0)

    @pl.when(step == 0)
    def _():
        gn_ref[...] = jnp.zeros_like(gn_ref)

    gx = nn(g_ref[...], w_ref[...])
    unit, _ = center_rows(raw_ref[...].astype(F32))
    gn_ref[...] += jnp.sum(gx * unit, axis=0, keepdims=True)

    @pl.when(step < pl.num_programs(0) // 2)
    def _():
        send_ref[...] = gx.astype(BF)

    @pl.when(step >= pl.num_programs(0) // 2)
    def _():
        keep_ref[...] = gx


def tok_grad(g_tok, w_tok, raw, *earlier):
    block = 256
    steps, half = SEQ_LEN // block, HALF // block
    rows = lambda width: pl.BlockSpec((block, width), lambda i: ((i + half) % steps, 0))
    return pl.pallas_call(
        tok_grad_kernel,
        out_shape=(shape((HALF, D), F32), shape((HALF, D), BF), shape((1, D), F32)),
        grid=(steps,),
        in_specs=[rows(HEADS * 3 * DH), whole((HEADS * 3 * DH, D)), rows(D)]
        + [ANY] * len(earlier),
        out_specs=[
            pl.BlockSpec((block, D), lambda i: (jnp.maximum(i - half, 0), 0)),
            pl.BlockSpec((block, D), lambda i: (jnp.minimum(i, half - 1), 0)),
            whole((1, D)),
        ],
        compiler_params=params(LIMIT),
        cost_estimate=cost(2 * SEQ_LEN * HEADS * 3 * DH * D),
        name="tok_grad",
    )(g_tok, w_tok, raw, *earlier)


def input_grad_kernel(keep_ref, got_ref, raw_ref, gm_ref, gain_ref, *refs):
    out_ref = refs[-1]
    unit, factor = center_rows(raw_ref[...].astype(F32))
    got = [got_ref[:, block_of(k ^ 1)].astype(F32) for k in range(4)]
    s = (keep_ref[...] + jnp.concatenate(got, axis=1)) * gain_ref[...]
    g = gm_ref[...] + factor * (
        s - jnp.mean(s, axis=1, keepdims=True) - unit * jnp.mean(s * unit, axis=1, keepdims=True)
    )
    for k in range(4):
        out_ref[k] = g[:, k * QUARTER : (k + 1) * QUARTER].astype(BF)


def input_grad(keep, got, raw, g_mid, gain, *earlier):
    block = 256
    rows = pl.BlockSpec((block, D), lambda i: (i, 0))
    return pl.pallas_call(
        input_grad_kernel,
        out_shape=shape((4, HALF, QUARTER), BF),
        grid=(HALF // block,),
        in_specs=[rows, rows, rows, rows, whole((1, D))] + [ANY] * len(earlier),
        out_specs=pl.BlockSpec((4, block, QUARTER), lambda i: (0, i, 0)),
        compiler_params=params(LIMIT),
        cost_estimate=cost(2 * HALF * D * D),
        name="input_grad",
    )(keep, got, raw, g_mid, gain, *earlier)


def mem_grad_kernel(g_ref, w_ref, raw_ref, gain_ref, conv_ref, _, gn_ref, gc_ref, unit_ref):
    total = jnp.zeros((1, D), F32)
    for block in range(MROWS // 256):
        rows = slice(block * 256, block * 256 + 256)
        unit, _ = center_rows(raw_ref[rows, :].astype(F32))
        total = total + jnp.sum(nn(g_ref[rows, :], w_ref[...]) * unit, axis=0, keepdims=True)
        if block * 256 >= CMEM:
            start = block * 256 - CMEM
            for j in range(D // DH):
                unit_ref[j, start : start + 256, :] = unit[:, j * DH : j * DH + DH]
    gn_ref[...] = total
    packed = nn(g_ref[MROWS:, :], w_ref[...])
    for j in range(D // DH):
        lanes = slice(j * DH, j * DH + DH)
        for t in range(RATE):
            picked = unit_ref[j, pl.ds(t, NEWC, stride=RATE), :]
            term = jnp.sum(packed[:, lanes] * picked, axis=0, keepdims=True)
            gc_ref[t : t + 1, lanes] = term * gain_ref[:, lanes]
            gn_ref[:, lanes] += conv_ref[t : t + 1, lanes] * term


def mem_grad(g_mem, w_mem, raw, gain, conv, earlier):
    return pl.pallas_call(
        mem_grad_kernel,
        out_shape=(shape((1, D), F32), shape((RATE, D), F32)),
        grid=(1,),
        in_specs=[
            whole((KM, D)), whole((D, D)), whole((MROWS, D)), whole((1, D)), whole((RATE, D)), ANY,
        ],
        out_specs=[whole((1, D)), whole((RATE, D))],
        scratch_shapes=[pltpu.VMEM((D // DH, MEM, DH), F32)],
        compiler_params=params(LIMIT),
        name="mem_grad",
    )(g_mem, w_mem, raw, gain, conv, earlier)


def store_spans(grad, index, keep_ref, send_ref):
    span = DH // 4
    for x in range(2):
        for core, ref in enumerate((keep_ref, send_ref)):
            row = (2 * x + core) * span
            ref[(x,) + index] = grad[row : row + span, :].astype(BF)


def qkv_grad_kernel(gt_ref, xt_ref, gm_ref, xm_ref, *refs):
    for kind in range(3):
        grad = nn(gt_ref[:, kind * DH : (kind + 1) * DH].T, xt_ref[...])
        if kind > 0:
            grad = grad + nn(gm_ref[:, (kind - 1) * DH : kind * DH].T, xm_ref[...])
        store_spans(grad, (0, kind), *refs[-2:])


def qkv_grad(g_tok, x_tok, g_mem, x_mem, *earlier):
    out = shape((2, HEADS, 3, DH // 4, D), BF)
    block = pl.BlockSpec((2, 1, 3, DH // 4, D), lambda h: (0, h, 0, 0, 0))
    return pl.pallas_call(
        qkv_grad_kernel,
        out_shape=(out, out),
        grid=(HEADS,),
        in_specs=[
            pl.BlockSpec((SEQ_LEN, 3 * DH), lambda h: (0, h)),
            whole((SEQ_LEN, D)),
            pl.BlockSpec((KM, 2 * DH), lambda h: (0, h)),
            whole((KM, D)),
        ]
        + [ANY] * len(earlier),
        out_specs=[block, block],
        compiler_params=params(LIMIT),
        cost_estimate=cost(2 * HEADS * DH * D * (3 * SEQ_LEN + 2 * KM)),
        name="qkv_grad",
    )(g_tok, x_tok, g_mem, x_mem, *earlier)


def out_grad_kernel(own_ref, got_ref, g_ref, keep_ref, send_ref):
    for z, ref in enumerate((own_ref, got_ref)):
        store_spans(nn(ref[...].T, g_ref[...]), (z, 0), keep_ref, send_ref)


def out_grad(o, o_got, g_attn):
    out = shape((2, 2, HEADS, DH // 4, D), BF)
    block = pl.BlockSpec((2, 2, 1, DH // 4, D), lambda h: (0, 0, h, 0, 0))
    half = pl.BlockSpec((HALF, DH), lambda h: (0, h))
    return pl.pallas_call(
        out_grad_kernel,
        out_shape=(out, out),
        grid=(HEADS,),
        in_specs=[half, half, whole((HALF, D))],
        out_specs=[block, block],
        compiler_params=params(LIMIT),
        cost_estimate=cost(4 * HALF * HEADS * DH * D),
        name="out_grad",
    )(o, o_got, g_attn)


def pick(g, index, axis=0):
    return lax.dynamic_index_in_dim(g, index, axis, keepdims=False)


def after(value, *earlier):
    return pl.pallas_call(
        lambda *refs: None,
        out_shape=shape(value.shape, value.dtype),
        in_specs=[ANY] * (1 + len(earlier)),
        out_specs=ANY,
        input_output_aliases={0: 0},
        name="after",
    )(value, *earlier)


def doubled(g, axis, distance):
    return jnp.concatenate([g, swap(g, axis, distance)], axis=0)


def both(parts, axis, distance):
    return parts + [swap(p, axis, distance) for p in parts]


def doubled_cols(g, n_col, first=1):
    while first < n_col:
        g = doubled(g, "col", first)
        first *= 2
    return g


def halve_col(g, last=1):
    while g.shape[0] > 1:
        n = g.shape[0] // 2
        g = add_low(g[:n], swap(g[n:], "col", n * last))
    return g[0]


def halve_row(g):
    g = add_low(g[:2], swap(g[2:], "row", 2))
    return g[0].astype(F32) + swap(g[1], "row", 1).astype(F32)


def per_device(
    hidden, memory, compressed, seg_ids, positions, keep_mask, mem_seg, cotangent,
    w_qkv, w_out, w_up, w_down, norm_attn, norm_ffn, conv_w,
):
    n_col = lax.axis_size("col")
    heads_part = w_qkv.shape[2]
    part = max(heads_part // 2, 1)
    row, col = lax.axis_index("row"), lax.axis_index("col")
    z_high, z_low = row // 2, row % 2
    low_first = z_low == 0
    where = z_low.reshape(1).astype(jnp.int32)
    span = DH // 4

    def by_low(pair):
        return jnp.where(low_first, pair, jnp.flip(pair, axis=0))

    tokens = hidden.reshape(2, SEQ_LEN, QUARTER)
    tok_mine, tok_other = pick(tokens, z_high), pick(tokens, 1 - z_high)
    tok_far, tok_near = swap(tok_other, "row", 2), swap(tok_mine, "row", 1)
    tok_pieces = [tok_mine, tok_near, tok_far, swap(tok_far, "row", 1)]

    small = jnp.concatenate(
        [norm_attn, norm_ffn, conv_w.reshape(-1)]
        + [a.astype(F32) for a in (seg_ids, positions, keep_mask, mem_seg)]
    )
    small = after(small, tok_near)
    shared = jnp.stack([small] + [swap(small, "row", k) for k in (1, 2, 3)])
    gains = shared[:, : 5 * QUARTER].reshape(4, 5, QUARTER).transpose(1, 0, 2).reshape(5, D)
    gain1, gain2, conv = gains[0:1], gains[1:2], gains[2:5]
    spans = seg_ids.shape[0] // SEQ_LEN
    sequence = 2 * col + z_high
    ids = pick(shared, row ^ (sequence // spans))[5 * QUARTER :]
    ids = pick(ids.reshape(4, spans, SEQ_LEN), sequence % spans, 1)
    rolled = jnp.concatenate([ids[:3, HALF:], ids[:3, :HALF]], axis=1)
    seg, pos, keep = jnp.where(low_first, ids[:3], rolled)
    row_attr = jnp.stack([seg, pos])
    col_attr = jnp.stack([jnp.where(keep == 1, seg, -2.0), pos, ids[3]], axis=1)

    qkv = w_qkv.astype(BF).transpose(2, 1, 3, 0)
    outs = w_out.astype(BF)
    if heads_part % 2 == 0:
        qkv = by_low(qkv.reshape(2, part, 3, span, QUARTER))
        outs = by_low(outs.reshape(2, part, 1, span, QUARTER))
        near = jnp.concatenate([qkv[0], outs[0], outs[1]], axis=1)
        far = jnp.concatenate([qkv[1], outs[1], outs[0]], axis=1)
        heads = jnp.stack(
            [near, swap(far, "row", 1), swap(near, "row", 2), swap(far, "row", 3)]
        )
        heads = doubled_cols(heads[None], n_col)
    else:
        qkv = jnp.stack([qkv] + [swap(qkv, "row", k) for k in (1, 2, 3)])
        outs = jnp.stack([outs] + [swap(outs, "row", k) for k in (1, 2, 3)])
        qkv = doubled_cols(jnp.where(low_first, qkv, swap(qkv, "col", 1))[None], n_col, 2)
        outs = doubled_cols(outs[None], n_col, 2)
        outs = by_low(jnp.stack([outs, swap(outs, "col", 1)]))
        heads = jnp.concatenate([qkv, jnp.moveaxis(outs, 0, 3)], axis=3)
    heads = both(both([heads], "dp", 2), "dp", 1)
    w_tok, w_mem, w_back = join_weights([heads[0], heads[2], heads[1], heads[3]])

    own = after(jnp.stack([w_up.astype(BF), w_down.astype(BF).T]), tok_far, tok_near)
    w_far = swap(own, "row", 2)
    own = after(own, w_far, tok_pieces[3])
    w_near = swap(own, "row", 1)
    own = jnp.stack([own, w_near, w_far, swap(w_far, "row", 1)], axis=1)
    half_col = n_col // 2
    distance = 1
    while distance < half_col:
        own = jnp.concatenate([own, swap(own, "col", distance)], axis=3)
        distance *= 2
    own_y, own_x = swap(own, "col", half_col), swap(own, "dp", 2)
    far_up, far_down = swap(own_x[0], "col", half_col), swap(own_y[1], "dp", 2)

    memories = jnp.concatenate(
        [compressed.reshape(2, CMEM, QUARTER), memory.reshape(2, MEM, QUARTER)], axis=1
    )
    mem_other = after(pick(memories, 1 - z_high), w_far, tok_pieces[3])
    mem_far = swap(mem_other, "row", 2)
    mem_mine = after(pick(memories, z_high), mem_far, w_near)
    mem_near = swap(mem_mine, "row", 1)
    mem_pieces = [mem_mine, mem_near, mem_far, swap(mem_far, "row", 1)]

    x_tok, raw_tok = tok_norm(where, tok_pieces, gain1)
    tok_p = nt(x_tok, w_tok).astype(BF)
    x_mem, raw_mem = mem_norm(mem_pieces, gain1, conv)
    mem_p = nt(x_mem, w_mem).astype(BF)
    cots = after(cotangent.reshape(4, HALF, QUARTER), mem_p, tok_p)
    cot = jnp.concatenate(
        [pick(cots, row)] + [swap(pick(cots, row ^ k), "row", k) for k in (1, 2, 3)], axis=1
    )
    cot_got = swap(cot, "dp", 1)
    o, logs = attention_forward(tok_p, mem_p, row_attr, col_attr)
    o_got = swap(o[HALF:], "row", 1)
    rec_q, rec_m = reconstruction(tok_p, mem_p, cot)
    mid, x2 = residual_mid(raw_tok, o, o_got, w_back, gain2, rec_m)

    x2_got = swap(x2, "dp", 1)
    out_keep, out_send, gx_keep, gx_send, *grads = feed_forward(
        x2, x2_got, cot, cot_got, (own, own_y, own_x), far_up, far_down
    )
    gx_got = swap(gx_send, "dp", 1)
    g_mid, g_attn, go_keep, go_send, gain2_sum = mid_back(
        gx_keep, gx_got, mid, cot, gain2, w_back
    )
    go_got = swap(go_send, "row", 1)

    own, own_y, own_x, far_up, far_down = grads
    far_up, far_down = swap(far_up, "col", half_col), swap(far_down, "dp", 2)
    sum_x = own_x.at[0].set(add_low(own_x[0], far_up))
    sum_y = own_y.at[1].set(add_low(own_y[1], far_down))
    got_x, got_y = swap(sum_x, "dp", 2), swap(sum_y, "col", half_col)

    def to_owners(blocks):
        return [blocks[0]] + [swap(blocks[k], "row", k) for k in (1, 2, 3)]

    def in_order(blocks):
        blocks = [jnp.where(low_first, blocks[k], blocks[k ^ 1]) for k in range(4)]
        blocks = [jnp.where(z_high == 0, blocks[k], blocks[k ^ 2]) for k in range(4)]
        return jnp.concatenate(blocks, axis=0)

    out_got = swap(out_send, "dp", 1)
    out_low = (mid + (out_keep + out_got.astype(F32))).astype(BF)
    out_low = after(jnp.stack([out_low[:, block_of(k)] for k in range(4)]), go_got)
    outs = to_owners([out_low[k] for k in range(4)])
    g_out = out_grad(o, o_got, g_attn)

    g_tok, g_mem = attention_backward(
        tok_p, mem_p, go_keep, go_got, o, logs, rec_q, rec_m, row_attr, col_attr,
        sum_x, sum_y, out_low, g_out[0],
    )
    gx, gx_send, gain1_tok = tok_grad(g_tok, w_tok, raw_tok, *outs[1:])
    gx_got = swap(gx_send, "row", 1)

    total = (own.astype(F32) + got_x.astype(F32) + got_y.astype(F32)).astype(BF)
    distance = half_col
    while distance > 1:
        distance //= 2
        n = total.shape[3] // 2
        total = add_low(total[..., :n], swap(total[..., n:], "col", distance))
    odd = total[:, 1::2]
    g_qkv = qkv_grad(g_tok, x_tok, g_mem, x_mem, odd, gx_send)
    grad_qkv, grad_out = reduce_heads(g_qkv, g_out, n_col, heads_part, by_low, low_first)
    even = add_low(total[:, 0::2], swap(odd, "row", 1))
    grads = even[:, 0].astype(F32) + swap(even[:, 1], "row", 2).astype(F32)

    d_rows = input_grad(gx, gx_got, raw_tok, g_mid, gain1, even, g_qkv[0])
    d_input = in_order(to_owners([d_rows[k] for k in range(4)]))
    out = in_order(outs)
    gain1_mem, conv_sum = mem_grad(g_mem, w_mem, raw_mem, gain1, conv, g_qkv[0])
    total = jnp.concatenate([gain1_tok + gain1_mem, gain2_sum, conv_sum], axis=0)
    total = total.reshape(5, 4, QUARTER).transpose(1, 0, 2)
    for distance in (1, 2):
        total = total + swap(total, "dp", distance)
    distance = 1
    while distance < n_col:
        total = total + swap(total, "col", distance)
        distance *= 2
    total = total[:2] + swap(total[2:], "row", 2)
    total = total[0] + swap(total[1], "row", 1)
    return (
        out, d_input, grad_qkv, grad_out, grads[0], grads[1].T, total[0], total[1], total[2:]
    )


def reduce_heads(g_qkv, g_out, n_col, heads_part, by_low, low_first):
    span = DH // 4

    def over_dp(keep, send):
        g = add_low(keep, swap(send, "dp", 1))
        return add_low(g[0], swap(g[1], "dp", 2))

    def over_row(g):
        g = add_low(g[..., : D // 2], swap(g[..., D // 2 :], "row", 2))
        return g[..., :QUARTER], swap(g[..., QUARTER:], "row", 1)

    g_out = over_dp(*g_out)
    g_qkv = over_dp(*g_qkv)
    if heads_part % 2 == 0:
        part = heads_part // 2
        g_out = halve_col(jnp.swapaxes(g_out.reshape((2, n_col, part) + g_out.shape[2:]), 0, 1))
        g_qkv = halve_col(g_qkv.reshape((n_col, part) + g_qkv.shape[1:]))
        g_qkv = by_low(jnp.stack(over_row(g_qkv))).astype(F32)
        g_qkv = g_qkv.reshape(heads_part, 3, span, QUARTER)
        g_out, got = over_row(g_out)
        g_out = by_low(g_out.astype(F32) + jnp.flip(got, axis=0).astype(F32))
        g_out = g_out.reshape(heads_part, span, QUARTER)
    else:
        g_qkv = halve_col(g_qkv, 2)
        zeros = jnp.zeros_like(g_qkv)
        g_qkv = add_low(
            jnp.where(low_first, g_qkv, zeros), swap(jnp.where(low_first, zeros, g_qkv), "col", 1)
        )
        g_out = by_low(g_out)
        g_out = halve_col(add_low(g_out[0], swap(g_out[1], "col", 1)), 2)
        g_qkv = halve_row(jnp.moveaxis(g_qkv.reshape(3, span, 4, QUARTER), 2, 0))[None]
        g_out = halve_row(jnp.moveaxis(g_out.reshape(span, 4, QUARTER), 1, 0))[None]
    return g_qkv.transpose(3, 1, 0, 2), g_out


def solution(mesh):
    tokens, features = ("dp", "col"), "row"
    placed = (
        P(tokens, features),
        P(tokens, features),
        P(tokens, features),
        P(("dp", "row")),
        P(("dp", "row")),
        P(("dp", "row")),
        P(("dp", "row")),
        P(tokens, features),
        P("row", None, "col", "dp"),
        P("col", "dp", "row"),
        P("row", tokens),
        P(tokens, "row"),
        P("row"),
        P("row"),
        P(None, "row"),
    )
    return jax.shard_map(
        per_device,
        mesh=mesh,
        in_specs=placed,
        out_specs=(
            P(tokens, features),
            P(tokens, features),
            P("row", None, "col", "dp"),
            P("col", "dp", "row"),
            P("row", tokens),
            P(tokens, "row"),
            P("row"),
            P("row"),
            P(None, "row"),
        ),
        check_vma=False,
    )
```

time: 656 us -> 512 us (0.78)
  waiting for transfers between devices: 294 us -> 175 us
  Pallas kernels: 132 us -> 181 us
  local copies, waits for them, and re-layouts: 84.4 us -> 35.7 us
  between operations: 15.4 us -> 1.71 us
  matrix products: 21 us -> 10.6 us
    all_gather x3 -> x0, waiting for transfers between devices: 87.2 us -> none  [the longest x1 87.2 us: per_device(): ffn_all = lax.all_gather(ffn_part, everything, axis=0, tiled=False)]
    pallas_call x3 -> x13, Pallas kernels: 43.4 us -> 77.6 us  [the longest x1 43.3 us: feed_forward(): pl.pallas_call(ffn_kernel, out_shape=(shape((HALF, D), F32), shape((HALF,...]
    ppermute x35 -> x60, waiting for transfers between devices: 204 us -> 175 us  [swap(): return lax.ppermute(x, axis, [(i, i ^ distance) for i in range(n)])]
    ppermute x35 -> x60, starting transfers between devices: 44.2 us -> 66.3 us  [swap(): return lax.ppermute(x, axis, [(i, i ^ distance) for i in range(n)])]
    unnamed x152 -> x88, local copies, waits for them, and re-layouts: 36.9 us -> 16.3 us
    convert_element_type x14 -> x7, other arithmetic: 24.5 us -> 5.75 us  [add_low(): return (a.astype(F32) + b.astype(F32)).astype(BF)]
    all_to_all x4 -> x0, starting transfers between devices: 16.8 us -> none  [the longest x1 4.49 us: per_device(): lax.all_to_all(d_rows.reshape(4 * HALF, QUARTER), 'row', split_axis=0, co...]
    dot_general x5 -> x0, matrix products: 14.4 us -> none  [the longest x4 8.95 us: tn(): lax.dot_general(a, b, (((0,), (0,)), ((), ())), preferred_element_type=F32)]
  transfers between devices with their start and end apart: 42 -> 60, of which waited for: 19 -> 27; matrix products, arithmetic and copies ran while one was open for 17% -> 14% of each run, Pallas kernels for 14% -> 27%
where the time goes in v2:
time: 512 us; the launch traced here: 507 us
  Pallas kernels  181 us (35%)
  waiting for transfers between devices  175 us (34%)
  starting transfers between devices  66.3 us (13%)
  other arithmetic  37.9 us (7%)
  local copies, waits for them, and re-layouts  35.7 us (7%)
  matrix products  10.6 us (2%)
    ppermute x60, waiting for transfers between devices, swap(): return lax.ppermute(x, axis, [(i, i ^ distance) for i in range(n)])  175 us
    ppermute x60, starting transfers between devices, swap(): return lax.ppermute(x, axis, [(i, i ^ distance) for i in range(n)])  66.3 us
    pallas_call x1, Pallas kernels, feed_forward(): pl.pallas_call(ffn_kernel, out_shape=(shape((HALF, D), F32), shape((HALF,...  43.3 us
    pallas_call x1, Pallas kernels, attention_backward(): pl.pallas_call(backward_kernel, out_shape=(shape((SEQ_LEN, HEADS * 3 * DH...  36.8 us
    pallas_call x1, Pallas kernels, attention_forward(): pl.pallas_call(forward_kernel, out_shape=(shape((SEQ_LEN, HEADS * DH), BF...  25.3 us
    unnamed x88, local copies, waits for them, and re-layouts  16.3 us
    pallas_call x1, Pallas kernels, reconstruction(): pl.pallas_call(recon_kernel, out_shape=(shape((HEADS, DH, SEQ_LEN), F32),...  12 us
    pallas_call x1, Pallas kernels, qkv_grad(): pl.pallas_call(qkv_grad_kernel, out_shape=(out, out), grid=(HEADS,), in_s...  10.8 us
  transfers between devices with their start and end apart: 60, of which 27 were waited for; matrix products, arithmetic and copies ran while one was open for 14% of the time, Pallas kernels for 27%

profile of v2, /device:TPU:0, one launch (start us, length us, event | category | flops | bytes accessed | tf_op | source)
XLA Modules:
  0.0 507.5 jit_solution(1224007398964127758)
XLA Ops:
  9.0 10.5 %collective-permute-done.7 = bf16[2,5,32,256]{3,2,1,0:T(8,128)(2,1)S(1)} collective-permute-done((bf16[2,5,32,256]{3,2,1,0:T(8,128)(2,1)S(1)}, bf16[2,5,32,256]{3,2,1,0:T(8,128)(2,1)S(1)}, u32[]{:S(2)}, u32[]{:S(2)}) %collective-permute-start.7) | collective-permute-done | bytes 163872 | tf_op jit(solution)/shard_map/ppermute | solution.py:49
  22.6 4.8 collective-permute-start.1
  46.1 5.5 %collective-permute-done.refs_1_.p1.refs_2_ = bf16[1024,256]{1,0:T(8,128)(2,1)S(1)} collective-permute-done((bf16[1024,256]{1,0:T(8,128)(2,1)S(1)}, bf16[1024,256]{1,0:T(8,128)(2,1)S(1)}, u32[]{:S(2)}, u32[]{:S(2)}) %collective-permute-start) | collective-permute-done | bytes 524320 | tf_op jit(solution)/shard_map/ppermute | solution.py:49
  64.2 16.8 %collective-permute-done.2.p3.refs_2_ = bf16[1024,256]{1,0:T(8,128)(2,1)S(1)} collective-permute-done((bf16[1024,256]{1,0:T(8,128)(2,1)}, bf16[1024,256]{1,0:T(8,128)(2,1)S(1)}, u32[]{:S(2)}, u32[]{:S(2)}) %collective-permute-start.2) | collective-permute-done | bytes 524320 | tf_op jit(solution)/shard_map/ppermute | solution.py:49
  88.6 19.7 %collective-permute-done.15.refs_2_ = bf16[2,256,512]{2,1,0:T(8,128)(2,1)S(1)} collective-permute-done((bf16[2,256,512]{2,1,0:T(8,128)(2,1)}, bf16[2,256,512]{2,1,0:T(8,128)(2,1)S(1)}, u32[]{:S(2)}, u32[]{:S(2)}) %collective-permute-start.15) | collective-permute-done | bytes 524320 | tf_op jit(solution)/shard_map/ppermute | solution.py:49
  114.0 5.7 %tok_norm.1 = (bf16[1024,1024]{1,0:T(8,128)(2,1)}, bf16[1024,1024]{1,0:T(8,128)(2,1)}) custom-call(s32[1]{0:T(128)} %bitcast.where, bf16[1024,256]{1,0:T(8,128)(2,1)} %copy-done.14, bf16[1024,256]{1,0:T(8,128)(2,1)} %copy-done.8, bf16[1024,256]{1,0:T(8,128)(2,1)} %copy-done.15, bf16[1024,256]{1,0:T(8,128)(2,1)} %copy-done.9, f32[1,1024]{1,0:T(1,128)} %bitcast.220), custom_call_target="tpu_custom_call" | custom-call | tf_op jit(solution)/shard_map/tok_norm/pallas_call | solution.py:104
  123.8 7.5 %collective-permute-done.16.p1 = bf16[1024,256]{1,0:T(8,128)(2,1)S(1)} collective-permute-done((bf16[1024,256]{1,0:T(8,128)(2,1)}, bf16[1024,256]{1,0:T(8,128)(2,1)S(1)}, u32[]{:S(2)}, u32[]{:S(2)}) %collective-permute-start.16) | collective-permute-done | bytes 524320 | tf_op jit(solution)/shard_map/ppermute | solution.py:49
  132.8 7.8 %collective-permute-done.17.p3 = bf16[1024,256]{1,0:T(8,128)(2,1)} collective-permute-done((bf16[1024,256]{1,0:T(8,128)(2,1)}, bf16[1024,256]{1,0:T(8,128)(2,1)}, u32[]{:S(2)}, u32[]{:S(2)}) %collective-permute-start.17) | collective-permute-done | bytes 524320 | tf_op jit(solution)/shard_map/ppermute | solution.py:49
  140.6 5.2 %mem_norm.1 = (bf16[1152,1024]{1,0:T(8,128)(2,1)}, bf16[1024,1024]{1,0:T(8,128)(2,1)}) custom-call(bf16[1024,256]{1,0:T(8,128)(2,1)} %after.11.p0, bf16[1024,256]{1,0:T(8,128)(2,1)} %copy-done.25, bf16[1024,256]{1,0:T(8,128)(2,1)} %copy-done.17, bf16[1024,256]{1,0:T(8,128)(2,1)} %collective-permute-done.17.p3, f32[1,1024]{1,0:T(1,128)} %bitcast.221, ...), custom_call_target="tpu_custom_call" | custom-call | tf_op jit(solution)/shard_map/mem_norm/pallas_call | solution.py:140
  145.8 5.9 %join_weights.1 = (bf16[1536,1024]{1,0:T(8,128)(2,1)}, bf16[1024,1024]{1,0:T(8,128)(2,1)}, bf16[1024,1024]{1,0:T(8,128)(2,1)}) custom-call(bf16[2,4,2,5,32,256]{5,4,3,2,1,0:T(8,128)(2,1)} %copy-done.7, bf16[2,4,2,5,32,256]{5,4,3,2,1,0:T(8,128)(2,1)} %collective-permute-done.10.refs_1_, bf16[2,4,2,5,32,256]{5,4,3,2,1,0:T(8,128)(2,1)} %collective-permute-done.11.refs_2_, ...), custom_call_target="tpu_custom_call" | custom-call | tf_op jit(solution)/shard_map/join_weights/pallas_call | solution.py:175
  151.7 5.6 %convolution_convert_fusion.mem_ref.refs_1_ = bf16[1152,1024]{1,0:T(8,128)(2,1)} fusion(bf16[1152,1024]{1,0:T(8,128)(2,1)S(1)} %copy-done.38, bf16[1024,1024]{1,0:T(8,128)(2,1)} %get-tuple-element.75.w_ref), kind=kOutput, calls=%fused_computation.1 | convolution fusion | flops 2417098752 | bytes 6815744 | tf_op jit(solution)/shard_map/dot_general | solution.py:40
  157.3 4.9 convolution_convert_fusion.1.tok_ref.refs_2_
  168.0 25.3 %attention_forward.1 = (bf16[1024,512]{1,0:T(8,128)(2,1)}, f32[4,1,1024]{2,1,0:T(1,128)}) custom-call(bf16[1024,1536]{1,0:T(8,128)(2,1)} %convolution_convert_fusion.1.tok_ref.refs_2_, bf16[1152,1024]{1,0:T(8,128)(2,1)} %convolution_convert_fusion.mem_ref.refs_1_, f32[2,1024]{1,0:T(2,128)} %stack.113.row_ref, f32[1024,3]{1,0:T(8,128)} %copy.69.col_ref), custom_call_target="tpu_custom_call" | custom-call | flops 24999999488 | bytes 25000000 | tf_op jit(solution)/shard_map/attention_forward/pallas_call | solution.py:252
  201.6 12.0 %reconstruction.1 = (f32[4,128,1024]{2,1,0:T(8,128)}, f32[640,1024]{1,0:T(8,128)}) custom-call(bf16[1024,1536]{1,0:T(8,128)(2,1)} %convolution_convert_fusion.1.tok_ref.refs_2_, bf16[1152,1024]{1,0:T(8,128)(2,1)} %convolution_convert_fusion.mem_ref.refs_1_, bf16[512,1024]{1,0:T(8,128)(2,1)} %copy-done.12), custom_call_target="tpu_custom_call" | custom-call | flops 10000000000 | bytes 10000000 | tf_op jit(solution)/shard_map/reconstruction/pallas_call | solution.py:305
  213.6 4.9 residual_mid.1
  221.6 43.3 %feed_forward.1 = (f32[512,1024]{1,0:T(8,128)}, bf16[512,1024]{1,0:T(8,128)(2,1)}, f32[512,1024]{1,0:T(8,128)}, bf16[512,1024]{1,0:T(8,128)(2,1)}, bf16[2,4,256,...) custom-call(bf16[512,1024]{1,0:T(8,128)(2,1)} %get-tuple-element.80., ...), custom_call_target="tpu_custom_call" | custom-call | flops 25769803776 | bytes 25769804 | tf_op jit(solution)/shard_map/feed_forward/pallas_call | solution.py:535
  269.3 6.6 %mid_back.1 = (f32[512,1024]{1,0:T(8,128)}, bf16[512,1024]{1,0:T(8,128)(2,1)}, bf16[512,512]{1,0:T(8,128)(2,1)}, bf16[512,512]{1,0:T(8,128)(2,1)}, f32[1,1024]{1,0:T(1,128)}) custom-call(f32[512,1024]{1,0:T(8,128)} %get-tuple-element.83.gx_ref, bf16[512,1024]{1,0:T(8,128)(2,1)} %collective-permute-done.30.got_ref, f32[512,1024]{1,0:T(8,128)} %get-tuple-element.79.mid_ref, ...), custom_call_target="tpu_custom_call" | custom-call | flops 1073741824 | bytes 1073741 | tf_op jit(solution)/shard_map/mid_back/pallas_call | solution.py:577
  277.7 4.9 out_grad.1
  282.8 7.8 %collective-permute-done.36 = bf16[4,256,512]{2,1,0:T(8,128)(2,1)S(1)} collective-permute-done((bf16[4,256,512]{2,1,0:T(8,128)(2,1)}, bf16[4,256,512]{2,1,0:T(8,128)(2,1)S(1)}, u32[]{:S(2)}, u32[]{:S(2)}) %collective-permute-start.36) | collective-permute-done | bytes 1048608 | tf_op jit(solution)/shard_map/ppermute | solution.py:49
  309.6 36.8 %attention_backward.1 = (bf16[1024,1536]{1,0:T(8,128)(2,1)}, bf16[1152,1024]{1,0:T(8,128)(2,1)}) custom-call(bf16[1024,1536]{1,0:T(8,128)(2,1)} %convolution_convert_fusion.1.tok_ref.refs_2_, bf16[1152,1024]{1,0:T(8,128)(2,1)} %convolution_convert_fusion.mem_ref.refs_1_, bf16[512,512]{1,0:T(8,128)(2,1)} %get-tuple-element.86.own_ref, ...), custom_call_target="tpu_custom_call" | custom-call | flops 35000000512 | bytes 35000000 | tf_op jit(solution)/shard_map/attention_backward/pallas_call | solution.py:385
  346.5 7.7 %collective-permute-done.50 = bf16[2,4,32,1024]{3,2,1,0:T(8,128)(2,1)S(1)} collective-permute-done((bf16[2,4,32,1024]{3,2,1,0:T(8,128)(2,1)}, bf16[2,4,32,1024]{3,2,1,0:T(8,128)(2,1)S(1)}, u32[]{:S(2)}, u32[]{:S(2)}) %collective-permute-start.50) | collective-permute-done | bytes 524320 | tf_op jit(solution)/shard_map/ppermute | solution.py:49
  359.7 8.5 %collective-permute-done.33.refs_1_ = bf16[512,256]{1,0:T(8,128)(2,1)S(1)} collective-permute-done((bf16[512,256]{1,0:T(8,128)(2,1)S(1)}, bf16[512,256]{1,0:T(8,128)(2,1)S(1)}, u32[]{:S(2)}, u32[]{:S(2)}) %collective-permute-start.33) | collective-permute-done | bytes 262176 | tf_op jit(solution)/shard_map/ppermute | solution.py:49
  368.8 8.4 %tok_grad.1 = (f32[512,1024]{1,0:T(8,128)}, bf16[512,1024]{1,0:T(8,128)(2,1)}, f32[1,1024]{1,0:T(1,128)}) custom-call(bf16[1024,1536]{1,0:T(8,128)(2,1)} %get-tuple-element.95.g_ref.gt_ref, bf16[1536,1024]{1,0:T(8,128)(2,1)} %get-tuple-element.73.w_ref, bf16[1024,1024]{1,0:T(8,128)(2,1)} %get-tuple-element.71.raw_ref, ...), custom_call_target="tpu_custom_call" | custom-call | flops 3221225472 | bytes 3221225 | tf_op jit(solution)/shard_map/tok_grad/pallas_call | solution.py:614
  386.8 10.8 %qkv_grad.1 = (bf16[2,4,3,32,1024]{4,3,2,1,0:T(8,128)(2,1)}, bf16[2,4,3,32,1024]{4,3,2,1,0:T(8,128)(2,1)}) custom-call(bf16[1024,1536]{1,0:T(8,128)(2,1)} %get-tuple-element.95.g_ref.gt_ref, bf16[1024,1024]{1,0:T(8,128)(2,1)} %get-tuple-element.72.xt_ref, bf16[1152,1024]{1,0:T(8,128)(2,1)} %get-tuple-element.100.gm_ref.g_ref, ...), custom_call_target="tpu_custom_call" | custom-call | flops 5637144576 | bytes 5637144 | tf_op jit(solution)/shard_map/qkv_grad/pallas_call | solution.py:713
  397.6 6.8 %mem_grad.1 = (f32[1,1024]{1,0:T(1,128)}, f32[3,1024]{1,0:T(4,128)}) custom-call(bf16[1152,1024]{1,0:T(8,128)(2,1)} %get-tuple-element.100.gm_ref.g_ref, bf16[1024,1024]{1,0:T(8,128)(2,1)} %get-tuple-element.75.w_ref, bf16[1024,1024]{1,0:T(8,128)(2,1)} %get-tuple-element.105.raw_ref, f32[1,1024]{1,0:T(1,128)} %bitcast.222, f32[3,1024]{1,0:T(4,128)} %bitcast.216, ...), custom_call_target="tpu_custom_call" | custom-call | tf_op jit(solution)/shard_map/mem_grad/pallas_call | solution.py:680
  415.6 4.3 collective-permute-done.58
  426.8 16.2 %collective-permute-done.40 = bf16[2,2,256,512]{3,2,1,0:T(8,128)(2,1)S(1)} collective-permute-done((bf16[2,2,256,512]{3,2,1,0:T(8,128)(2,1)S(1)}, bf16[2,2,256,512]{3,2,1,0:T(8,128)(2,1)S(1)}, u32[]{:S(2)}, u32[]{:S(2)}) %collective-permute-start.40) | collective-permute-done | bytes 1048608 | tf_op jit(solution)/shard_map/ppermute | solution.py:49
  445.7 4.3 input_grad.1
  457.4 6.3 %collective-permute-done.41 = bf16[512,256]{1,0:T(8,128)(2,1)S(1)} collective-permute-done((bf16[512,256]{1,0:T(8,128)(2,1)S(1)}, bf16[512,256]{1,0:T(8,128)(2,1)S(1)}, u32[]{:S(2)}, u32[]{:S(2)}) %collective-permute-start.41) | collective-permute-done | bytes 262176 | tf_op jit(solution)/shard_map/ppermute | solution.py:49
  463.7 6.1 %collective-permute-done.43 = bf16[512,256]{1,0:T(8,128)(2,1)S(1)} collective-permute-done((bf16[512,256]{1,0:T(8,128)(2,1)S(1)}, bf16[512,256]{1,0:T(8,128)(2,1)S(1)}, u32[]{:S(2)}, u32[]{:S(2)}) %collective-permute-start.43) | collective-permute-done | bytes 262176 | tf_op jit(solution)/shard_map/ppermute | solution.py:49
  469.7 18.6 %collective-permute-done.42 = bf16[512,256]{1,0:T(8,128)(2,1)S(1)} collective-permute-done((bf16[512,256]{1,0:T(8,128)(2,1)S(1)}, bf16[512,256]{1,0:T(8,128)(2,1)S(1)}, u32[]{:S(2)}, u32[]{:S(2)}) %collective-permute-start.42) | collective-permute-done | bytes 262176 | tf_op jit(solution)/shard_map/ppermute | solution.py:49
  491.1 10.3 %collective-permute-done.47 = bf16[2,3,32,512]{3,2,1,0:T(8,128)(2,1)S(1)} collective-permute-done((bf16[2,3,32,512]{3,2,1,0:T(8,128)(2,1)S(1)}, bf16[2,3,32,512]{3,2,1,0:T(8,128)(2,1)S(1)}, u32[]{:S(2)}, u32[]{:S(2)}) %collective-permute-start.47) | collective-permute-done | bytes 196640 | tf_op jit(solution)/shard_map/ppermute | solution.py:49
  (295 shorter events, 156.1 us)
Async XLA Ops:
  22.6 35.8 %collective-permute-start.1 = (bf16[1024,256]{1,0:T(8,128)(2,1)}, bf16[1024,256]{1,0:T(8,128)(2,1)S(1)}, u32[]{:S(2)}, u32[]{:S(2)}) collective-permute-start(bf16[1024,256]{1,0:T(8,128)(2,1)} %get-tuple-element.171), channel_id=1, source_target_pairs={{0,4},{2,6},{4,0},{6,2},{1,5},{3,7},{5,1},{7,3},{8,12},{10,14},{12... | collective-permute-start | bytes 1572872 | tf_op jit(solution)/shard_map/ppermute | solution.py:49
  27.4 24.3 %collective-permute-start = (bf16[1024,256]{1,0:T(8,128)(2,1)S(1)}, bf16[1024,256]{1,0:T(8,128)(2,1)S(1)}, u32[]{:S(2)}, u32[]{:S(2)}) collective-permute-start(bf16[1024,256]{1,0:T(8,128)(2,1)S(1)} %get-tuple-element.172.p0), channel_id=1, source_target_pairs={{0,2},{2,0},{4,6},{6,4},{1,3},{3,1},{5,7},{7,5},{8,10},{10,8},{12,... | collective-permute-start | bytes 1572872 | tf_op jit(solution)/shard_map/ppermute | solution.py:49
  36.0 27.9 %collective-permute-start.11 = (bf16[2,4,2,5,32,256]{5,4,3,2,1,0:T(8,128)(2,1)S(1)}, bf16[2,4,2,5,32,256]{5,4,3,2,1,0:T(8,128)(2,1)}, u32[]{:S(2)}, u32[]{:S(2)}) collective-permute-start(bf16[2,4,2,5,32,256]{5,4,3,2,1,0:T(8,128)(2,1)S(1)} %pad_maximum_fusion.1.refs_0_), channel_id=1, source_target_pairs={{0,16},{8,24},{16,0},{24,8},{1,17},{9,25},{17,1},{25,9},{2,18},{10... | collective-permute-start | bytes 3932168 | tf_op jit(solution)/shard_map/ppermute | solution.py:49
  60.0 85.7 %collective-permute-start.10 = (bf16[2,4,2,5,32,256]{5,4,3,2,1,0:T(8,128)(2,1)S(1)}, bf16[2,4,2,5,32,256]{5,4,3,2,1,0:T(8,128)(2,1)}, u32[]{:S(2)}, u32[]{:S(2)}) collective-permute-start(bf16[2,4,2,5,32,256]{5,4,3,2,1,0:T(8,128)(2,1)S(1)} %pad_maximum_fusion.1.refs_0_), channel_id=1, source_target_pairs={{0,8},{8,0},{16,24},{24,16},{1,9},{9,1},{17,25},{25,17},{2,10},{10... | collective-permute-start | bytes 3932168 | tf_op jit(solution)/shard_map/ppermute | solution.py:49
  63.9 81.8 %collective-permute-start.12 = (bf16[2,4,2,5,32,256]{5,4,3,2,1,0:T(8,128)(2,1)}, bf16[2,4,2,5,32,256]{5,4,3,2,1,0:T(8,128)(2,1)}, u32[]{:S(2)}, u32[]{:S(2)}) collective-permute-start(bf16[2,4,2,5,32,256]{5,4,3,2,1,0:T(8,128)(2,1)} %collective-permute-done.11.refs_2_), channel_id=1, source_target_pairs={{0,8},{8,0},{16,24},{24,16},{1,9},{9,1},{17,25},{25,17},{2,10},{10... | collective-permute-start | bytes 3932168 | tf_op jit(solution)/shard_map/ppermute | solution.py:49
  82.6 25.7 %collective-permute-start.15 = (bf16[2,256,512]{2,1,0:T(8,128)(2,1)}, bf16[2,256,512]{2,1,0:T(8,128)(2,1)S(1)}, u32[]{:S(2)}, u32[]{:S(2)}) collective-permute-start(bf16[2,256,512]{2,1,0:T(8,128)(2,1)} %after.10), channel_id=1, source_target_pairs={{0,2},{2,0},{4,6},{6,4},{1,3},{3,1},{5,7},{7,5},{8,10},{10,8},{12,... | collective-permute-start | bytes 1572872 | tf_op jit(solution)/shard_map/ppermute | solution.py:49
  85.0 23.9 %collective-permute-start.14 = (bf16[1024,256]{1,0:T(8,128)(2,1)}, bf16[1024,256]{1,0:T(8,128)(2,1)S(1)}, u32[]{:S(2)}, u32[]{:S(2)}) collective-permute-start(bf16[1024,256]{1,0:T(8,128)(2,1)} %after.9), channel_id=1, source_target_pairs={{0,4},{2,6},{4,0},{6,2},{1,5},{3,7},{5,1},{7,3},{8,12},{10,14},{12... | collective-permute-start | bytes 1572872 | tf_op jit(solution)/shard_map/ppermute | solution.py:49
  86.6 33.4 %collective-permute-start.24 = (bf16[2,256,512]{2,1,0:T(8,128)(2,1)S(1)}, bf16[2,256,512]{2,1,0:T(8,128)(2,1)}, u32[]{:S(2)}, u32[]{:S(2)}) collective-permute-start(bf16[2,256,512]{2,1,0:T(8,128)(2,1)S(1)} %copy-done.11), channel_id=1, source_target_pairs={{0,2},{2,0},{4,6},{6,4},{1,3},{3,1},{5,7},{7,5},{8,10},{10,8},{12,... | collective-permute-start | bytes 1572872 | tf_op jit(solution)/shard_map/ppermute | solution.py:49
  112.2 28.4 %collective-permute-start.17 = (bf16[1024,256]{1,0:T(8,128)(2,1)}, bf16[1024,256]{1,0:T(8,128)(2,1)}, u32[]{:S(2)}, u32[]{:S(2)}) collective-permute-start(bf16[1024,256]{1,0:T(8,128)(2,1)} %copy-done.17), channel_id=1, source_target_pairs={{0,2},{2,0},{4,6},{6,4},{1,3},{3,1},{5,7},{7,5},{8,10},{10,8},{12,... | collective-permute-start | bytes 1572872 | tf_op jit(solution)/shard_map/ppermute | solution.py:49
  122.7 71.7 %collective-permute-start.26 = (bf16[2,4,256,512]{3,2,1,0:T(8,128)(2,1)}, bf16[2,4,256,512]{3,2,1,0:T(8,128)(2,1)}, u32[]{:S(2)}, u32[]{:S(2)}) collective-permute-start(bf16[2,4,256,512]{3,2,1,0:T(8,128)(2,1)} %pad_maximum_fusion.refs_4_), channel_id=1, source_target_pairs={{0,16},{8,24},{16,0},{24,8},{1,17},{9,25},{17,1},{25,9},{2,18},{10... | collective-permute-start | bytes 6291464 | tf_op jit(solution)/shard_map/ppermute | solution.py:49
  131.4 64.4 %collective-permute-start.25 = (bf16[2,4,256,512]{3,2,1,0:T(8,128)(2,1)}, bf16[2,4,256,512]{3,2,1,0:T(8,128)(2,1)}, u32[]{:S(2)}, u32[]{:S(2)}) collective-permute-start(bf16[2,4,256,512]{3,2,1,0:T(8,128)(2,1)} %pad_maximum_fusion.refs_4_), channel_id=1, source_target_pairs={{0,1},{1,0},{2,3},{3,2},{4,5},{5,4},{6,7},{7,6},{8,9},{9,8},{10,11... | collective-permute-start | bytes 6291464 | tf_op jit(solution)/shard_map/ppermute | solution.py:49
  163.5 35.1 %collective-permute-start.21 = (bf16[512,256]{1,0:T(8,128)(2,1)S(1)}, bf16[512,256]{1,0:T(8,128)(2,1)S(1)}, u32[]{:S(2)}, u32[]{:S(2)}) collective-permute-start(bf16[512,256]{1,0:T(8,128)(2,1)S(1)} %get-tuple-element.166), channel_id=1, source_target_pairs={{0,6},{2,4},{4,2},{6,0},{1,7},{3,5},{5,3},{7,1},{8,14},{10,12},{12... | collective-permute-start | bytes 786440 | tf_op jit(solution)/shard_map/ppermute | solution.py:49
  165.5 33.7 %collective-permute-start.20 = (bf16[512,256]{1,0:T(8,128)(2,1)S(1)}, bf16[512,256]{1,0:T(8,128)(2,1)}, u32[]{:S(2)}, u32[]{:S(2)}) collective-permute-start(bf16[512,256]{1,0:T(8,128)(2,1)S(1)} %get-tuple-element.167), channel_id=1, source_target_pairs={{0,4},{2,6},{4,0},{6,2},{1,5},{3,7},{5,1},{7,3},{8,12},{10,14},{12... | collective-permute-start | bytes 786440 | tf_op jit(solution)/shard_map/ppermute | solution.py:49
  165.9 33.3 %collective-permute-start.19 = (bf16[512,256]{1,0:T(8,128)(2,1)S(1)}, bf16[512,256]{1,0:T(8,128)(2,1)}, u32[]{:S(2)}, u32[]{:S(2)}) collective-permute-start(bf16[512,256]{1,0:T(8,128)(2,1)S(1)} %get-tuple-element.168), channel_id=1, source_target_pairs={{0,2},{2,0},{4,6},{6,4},{1,3},{3,1},{5,7},{7,5},{8,10},{10,8},{12,... | collective-permute-start | bytes 786440 | tf_op jit(solution)/shard_map/ppermute | solution.py:49
  195.8 23.0 %collective-permute-start.27 = (bf16[4,256,512]{2,1,0:T(8,128)(2,1)S(1)}, bf16[4,256,512]{2,1,0:T(8,128)(2,1)}, u32[]{:S(2)}, u32[]{:S(2)}) collective-permute-start(bf16[4,256,512]{2,1,0:T(8,128)(2,1)S(1)} %slice_bitcast_fusion.1), channel_id=1, source_target_pairs={{0,1},{1,0},{2,3},{3,2},{4,5},{5,4},{6,7},{7,6},{8,9},{9,8},{10,11... | collective-permute-start | bytes 3145736 | tf_op jit(solution)/shard_map/ppermute | solution.py:49
  198.7 22.9 %collective-permute-start.28 = (bf16[4,256,512]{2,1,0:T(8,128)(2,1)S(1)}, bf16[4,256,512]{2,1,0:T(8,128)(2,1)}, u32[]{:S(2)}, u32[]{:S(2)}) collective-permute-start(bf16[4,256,512]{2,1,0:T(8,128)(2,1)S(1)} %slice_bitcast_fusion), channel_id=1, source_target_pairs={{0,16},{8,24},{16,0},{24,8},{1,17},{9,25},{17,1},{25,9},{2,18},{10... | collective-permute-start | bytes 3145736 | tf_op jit(solution)/shard_map/ppermute | solution.py:49
  264.9 25.7 %collective-permute-start.36 = (bf16[4,256,512]{2,1,0:T(8,128)(2,1)}, bf16[4,256,512]{2,1,0:T(8,128)(2,1)S(1)}, u32[]{:S(2)}, u32[]{:S(2)}) collective-permute-start(bf16[4,256,512]{2,1,0:T(8,128)(2,1)} %get-tuple-element.92), channel_id=1, source_target_pairs={{0,16},{8,24},{16,0},{24,8},{1,17},{9,25},{17,1},{25,9},{2,18},{10... | collective-permute-start | bytes 3145736 | tf_op jit(solution)/shard_map/ppermute | solution.py:49
  266.3 26.9 %collective-permute-start.35 = (bf16[4,256,512]{2,1,0:T(8,128)(2,1)}, bf16[4,256,512]{2,1,0:T(8,128)(2,1)}, u32[]{:S(2)}, u32[]{:S(2)}) collective-permute-start(bf16[4,256,512]{2,1,0:T(8,128)(2,1)} %get-tuple-element.90), channel_id=1, source_target_pairs={{0,1},{1,0},{2,3},{3,2},{4,5},{5,4},{6,7},{7,6},{8,9},{9,8},{10,11... | collective-permute-start | bytes 3145736 | tf_op jit(solution)/shard_map/ppermute | solution.py:49
  267.3 29.5 %collective-permute-start.29 = (bf16[512,1024]{1,0:T(8,128)(2,1)}, bf16[512,1024]{1,0:T(8,128)(2,1)}, u32[]{:S(2)}, u32[]{:S(2)}) collective-permute-start(bf16[512,1024]{1,0:T(8,128)(2,1)} %get-tuple-element.82), channel_id=1, source_target_pairs={{0,8},{8,0},{16,24},{24,16},{1,9},{9,1},{17,25},{25,17},{2,10},{10... | collective-permute-start | bytes 3145736 | tf_op jit(solution)/shard_map/ppermute | solution.py:49
  275.9 24.0 %collective-permute-start.31 = (bf16[512,512]{1,0:T(8,128)(2,1)}, bf16[512,512]{1,0:T(8,128)(2,1)}, u32[]{:S(2)}, u32[]{:S(2)}) collective-permute-start(bf16[512,512]{1,0:T(8,128)(2,1)} %get-tuple-element.85), channel_id=1, source_target_pairs={{0,2},{2,0},{4,6},{6,4},{1,3},{3,1},{5,7},{7,5},{8,10},{10,8},{12,... | collective-permute-start | bytes 1572872 | tf_op jit(solution)/shard_map/ppermute | solution.py:49
  282.6 22.9 %collective-permute-start.49 = (bf16[2,2,4,32,1024]{4,3,2,1,0:T(8,128)(2,1)}, bf16[2,2,4,32,1024]{4,3,2,1,0:T(8,128)(2,1)}, u32[]{:S(2)}, u32[]{:S(2)}) collective-permute-start(bf16[2,2,4,32,1024]{4,3,2,1,0:T(8,128)(2,1)} %get-tuple-element.103), channel_id=1, source_target_pairs={{0,8},{8,0},{16,24},{24,16},{1,9},{9,1},{17,25},{25,17},{2,10},{10... | collective-permute-start | bytes 3145736 | tf_op jit(solution)/shard_map/ppermute | solution.py:49
  292.0 88.7 %collective-permute-start.39 = (bf16[2,4,256,512]{3,2,1,0:T(8,128)(2,1)}, bf16[2,4,256,512]{3,2,1,0:T(8,128)(2,1)S(1)}, u32[]{:S(2)}, u32[]{:S(2)}) collective-permute-start(bf16[2,4,256,512]{3,2,1,0:T(8,128)(2,1)} %fusion.6.refs_1_), channel_id=1, source_target_pairs={{0,1},{1,0},{2,3},{3,2},{4,5},{5,4},{6,7},{7,6},{8,9},{9,8},{10,11... | collective-permute-start | bytes 6291464 | tf_op jit(solution)/shard_map/ppermute | solution.py:49
  295.8 84.8 %collective-permute-start.38 = (bf16[2,4,256,512]{3,2,1,0:T(8,128)(2,1)}, bf16[2,4,256,512]{3,2,1,0:T(8,128)(2,1)}, u32[]{:S(2)}, u32[]{:S(2)}) collective-permute-start(bf16[2,4,256,512]{3,2,1,0:T(8,128)(2,1)} %fusion.4.refs_0_), channel_id=1, source_target_pairs={{0,16},{8,24},{16,0},{24,8},{1,17},{9,25},{17,1},{25,9},{2,18},{10... | collective-permute-start | bytes 6291464 | tf_op jit(solution)/shard_map/ppermute | solution.py:49
  301.9 56.8 %collective-permute-start.32 = (bf16[512,256]{1,0:T(8,128)(2,1)}, bf16[512,256]{1,0:T(8,128)(2,1)}, u32[]{:S(2)}, u32[]{:S(2)}) collective-permute-start(bf16[512,256]{1,0:T(8,128)(2,1)} %get-tuple-element.158), channel_id=1, source_target_pairs={{0,2},{2,0},{4,6},{6,4},{1,3},{3,1},{5,7},{7,5},{8,10},{10,8},{12,... | collective-permute-start | bytes 786440 | tf_op jit(solution)/shard_map/ppermute | solution.py:49
  303.6 56.1 %collective-permute-start.34 = (bf16[512,256]{1,0:T(8,128)(2,1)}, bf16[512,256]{1,0:T(8,128)(2,1)}, u32[]{:S(2)}, u32[]{:S(2)}) collective-permute-start(bf16[512,256]{1,0:T(8,128)(2,1)} %get-tuple-element.159), channel_id=1, source_target_pairs={{0,6},{2,4},{4,2},{6,0},{1,7},{3,5},{5,3},{7,1},{8,14},{10,12},{12... | collective-permute-start | bytes 786440 | tf_op jit(solution)/shard_map/ppermute | solution.py:49
  308.3 45.8 %collective-permute-start.50 = (bf16[2,4,32,1024]{3,2,1,0:T(8,128)(2,1)}, bf16[2,4,32,1024]{3,2,1,0:T(8,128)(2,1)S(1)}, u32[]{:S(2)}, u32[]{:S(2)}) collective-permute-start(bf16[2,4,32,1024]{3,2,1,0:T(8,128)(2,1)} %slice_bitcast_fusion.8), channel_id=1, source_target_pairs={{0,16},{8,24},{16,0},{24,8},{1,17},{9,25},{17,1},{25,9},{2,18},{10... | collective-permute-start | bytes 1572872 | tf_op jit(solution)/shard_map/ppermute | solution.py:49
  377.2 68.5 %collective-permute-start.37 = (bf16[512,1024]{1,0:T(8,128)(2,1)}, bf16[512,1024]{1,0:T(8,128)(2,1)}, u32[]{:S(2)}, u32[]{:S(2)}) collective-permute-start(bf16[512,1024]{1,0:T(8,128)(2,1)} %get-tuple-element.97.refs_1_), channel_id=1, source_target_pairs={{0,2},{2,0},{4,6},{6,4},{1,3},{3,1},{5,7},{7,5},{8,10},{10,8},{12,... | collective-permute-start | bytes 3145736 | tf_op jit(solution)/shard_map/ppermute | solution.py:49
  378.0 30.3 %collective-permute-start.52 = (bf16[2,2,32,512]{3,2,1,0:T(8,128)(2,1)}, bf16[2,2,32,512]{3,2,1,0:T(8,128)(2,1)S(1)}, u32[]{:S(2)}, u32[]{:S(2)}) collective-permute-start(bf16[2,2,32,512]{3,2,1,0:T(8,128)(2,1)} %slice.351), channel_id=1, source_target_pairs={{0,4},{2,6},{4,0},{6,2},{1,5},{3,7},{5,1},{7,3},{8,12},{10,14},{12... | collective-permute-start | bytes 393224 | tf_op jit(solution)/shard_map/ppermute | solution.py:49
  425.7 29.3 %collective-permute-start.45 = (bf16[4,3,32,1024]{3,2,1,0:T(8,128)(2,1)S(1)}, bf16[4,3,32,1024]{3,2,1,0:T(8,128)(2,1)}, u32[]{:S(2)}, u32[]{:S(2)}) collective-permute-start(bf16[4,3,32,1024]{3,2,1,0:T(8,128)(2,1)S(1)} %slice_bitcast_fusion.2), channel_id=1, source_target_pairs={{0,16},{8,24},{16,0},{24,8},{1,17},{9,25},{17,1},{25,9},{2,18},{10... | collective-permute-start | bytes 2359304 | tf_op jit(solution)/shard_map/ppermute | solution.py:49
  443.3 47.4 %collective-permute-start.54 = (bf16[2,256,512]{2,1,0:T(8,128)(2,1)S(1)}, bf16[2,256,512]{2,1,0:T(8,128)(2,1)S(1)}, u32[]{:S(2)}, u32[]{:S(2)}) collective-permute-start(bf16[2,256,512]{2,1,0:T(8,128)(2,1)S(1)} %slice_bitcast_fusion.6), channel_id=1, source_target_pairs={{0,4},{2,6},{4,0},{6,2},{1,5},{3,7},{5,1},{7,3},{8,12},{10,14},{12... | collective-permute-start | bytes 1572872 | tf_op jit(solution)/shard_map/ppermute | solution.py:49
  453.8 34.6 %collective-permute-start.42 = (bf16[512,256]{1,0:T(8,128)(2,1)S(1)}, bf16[512,256]{1,0:T(8,128)(2,1)S(1)}, u32[]{:S(2)}, u32[]{:S(2)}) collective-permute-start(bf16[512,256]{1,0:T(8,128)(2,1)S(1)} %get-tuple-element.157), channel_id=1, source_target_pairs={{0,4},{2,6},{4,0},{6,2},{1,5},{3,7},{5,1},{7,3},{8,12},{10,14},{12... | collective-permute-start | bytes 786440 | tf_op jit(solution)/shard_map/ppermute | solution.py:49
  456.4 34.0 %collective-permute-start.46 = (bf16[1,2,3,32,1024]{4,3,2,1,0:T(8,128)(2,1)S(1)}, bf16[1,2,3,32,1024]{4,3,2,1,0:T(8,128)(2,1)S(1)}, u32[]{:S(2)}, u32[]{:S(2)}) collective-permute-start(bf16[1,2,3,32,1024]{4,3,2,1,0:T(8,128)(2,1)S(1)} %slice_bitcast_fusion.10), channel_id=1, source_target_pairs={{0,1},{1,0},{2,3},{3,2},{4,5},{5,4},{6,7},{7,6},{8,9},{9,8},{10,11... | collective-permute-start | bytes 1179656 | tf_op jit(solution)/shard_map/ppermute | solution.py:49
  (69 other events, 635.1 us)

commit v3 on v2

--- a/solution.py
+++ b/solution.py
@@ -115,7 +115,7 @@
     )(where, *pieces, gain)
 
 
-def mem_norm_kernel(p0, p1, p2, p3, gain_ref, conv_ref, low_ref, raw_ref, keep_ref):
+def mem_norm_kernel(p0, p1, p2, p3, gain_ref, conv_ref, _, low_ref, raw_ref, keep_ref):
     for block in range(MROWS // 256):
         rows = slice(block * 256, block * 256 + 256)
         pieces = [p[rows, :] for p in (p0, p1, p2, p3)]
@@ -136,17 +136,17 @@
         low_ref[MROWS:, lanes] = packed.astype(BF)
 
 
-def mem_norm(pieces, gain, conv):
+def mem_norm(pieces, gain, conv, earlier):
     return pl.pallas_call(
         mem_norm_kernel,
         out_shape=(shape((KM, D), BF), shape((MROWS, D), BF)),
         grid=(1,),
-        in_specs=[whole((MROWS, QUARTER))] * 4 + [whole((1, D)), whole((RATE, D))],
+        in_specs=[whole((MROWS, QUARTER))] * 4 + [whole((1, D)), whole((RATE, D)), ANY],
         out_specs=[whole((KM, D)), whole((MROWS, D))],
         scratch_shapes=[pltpu.VMEM((D // DH, MEM, DH), F32)],
         compiler_params=params(LIMIT),
         name="mem_norm",
-    )(*pieces, gain, conv)
+    )(*pieces, gain, conv, earlier)
 
 
 def join_kernel(*refs):
@@ -274,7 +274,8 @@
     )(tok_p, mem_p, row_attr, col_attr)
 
 
-def recon_kernel(tok_ref, mem_ref, _, gq_ref, gm_ref):
+def recon_kernel(tok_ref, mem_ref, *refs):
+    gq_ref, gm_ref = refs[-2:]
     q = tok_ref[:, :DH]
     old, new = slice(CMEM, CMEM + OLD), slice(MROWS, KM)
     keys, values = slice(0, DH), slice(DH, 2 * DH)
@@ -301,7 +302,7 @@
     gm_ref[MEM:, values] = -nn(pn_low, gap_t)
 
 
-def reconstruction(tok_p, mem_p, earlier):
+def reconstruction(tok_p, mem_p, *earlier):
     return pl.pallas_call(
         recon_kernel,
         out_shape=(
@@ -312,8 +313,8 @@
         in_specs=[
             pl.BlockSpec((SEQ_LEN, 3 * DH), lambda h: (0, h)),
             pl.BlockSpec((KM, 2 * DH), lambda h: (0, h)),
-            ANY,
-        ],
+        ]
+        + [ANY] * len(earlier),
         out_specs=[
             pl.BlockSpec((1, DH, SEQ_LEN), lambda h: (h, 0, 0)),
             pl.BlockSpec((MEM + NEWC, 2 * DH), lambda h: (0, h)),
@@ -321,7 +322,7 @@
         compiler_params=params(LIMIT),
         cost_estimate=cost(10_000_000_000),
         name="reconstruction",
-    )(tok_p, mem_p, earlier)
+    )(tok_p, mem_p, *earlier)
 
 
 def backward_kernel(
@@ -495,19 +496,21 @@
     g_pre = (g_act * slope).astype(BF)
     out_ref[...] += nt(act, w_down)
     gx_ref[...] += nt(g_pre, w_up)
-    grad_up = nn(xt_ref[...], g_pre).astype(BF).reshape(4, QUARTER, TILE)
-    grad_down = nn(ct_ref[...], act).astype(BF).reshape(4, QUARTER, TILE)
+    grad_up = nn(xt_ref[...], g_pre).astype(BF)
+    grad_down = nn(ct_ref[...], act).astype(BF)
 
     for k in range(3):
         @pl.when(block == k)
         def _():
-            grads[k][0] = grad_up
-            grads[k][1] = grad_down
+            for j, row in enumerate((0, 2, 1, 3)):
+                grads[k][0, j] = grad_up[block_of(row), :]
+                grads[k][1, j] = grad_down[block_of(row), :]
 
     @pl.when(block == 3)
     def _():
-        grads[3][...] = grad_up
-        grads[4][...] = grad_down
+        for j, row in enumerate((0, 2, 1, 3)):
+            grads[3][j] = grad_up[block_of(row), :]
+            grads[4][j] = grad_down[block_of(row), :]
 
     @pl.when(step == last)
     def _():
@@ -550,6 +553,26 @@
     )(x2, x2_got, cot, cot_got, *plain, far_up, far_down)
 
 
+def out_sum_kernel(mid_ref, keep_ref, got_ref, *refs):
+    total = mid_ref[...] + (keep_ref[...] + got_ref[...].astype(F32))
+    for k, ref in enumerate(refs[-4:]):
+        ref[...] = total[:, block_of(k)].astype(BF)
+
+
+def out_sum(mid, keep, got, *earlier):
+    block = 256
+    rows = lambda width: pl.BlockSpec((block, width), lambda i: (i, 0))
+    return pl.pallas_call(
+        out_sum_kernel,
+        out_shape=(shape((HALF, QUARTER), BF),) * 4,
+        grid=(HALF // block,),
+        in_specs=[rows(D)] * 3 + [ANY] * len(earlier),
+        out_specs=[rows(QUARTER)] * 4,
+        compiler_params=params(LIMIT),
+        name="out_sum",
+    )(mid, keep, got, *earlier)
+
+
 def mid_back_kernel(gx_ref, got_ref, mid_ref, cot_ref, gain_ref, w_ref, gm_ref, ga_ref, keep_ref, send_ref, gn_ref):
     @pl.when(pl.program_id(0) == 0)
     def _():
@@ -623,21 +646,19 @@
             whole((1, D)),
         ],
         compiler_params=params(LIMIT),
-        cost_estimate=cost(2 * SEQ_LEN * HEADS * 3 * DH * D),
         name="tok_grad",
     )(g_tok, w_tok, raw, *earlier)
 
 
 def input_grad_kernel(keep_ref, got_ref, raw_ref, gm_ref, gain_ref, *refs):
-    out_ref = refs[-1]
     unit, factor = center_rows(raw_ref[...].astype(F32))
     got = [got_ref[:, block_of(k ^ 1)].astype(F32) for k in range(4)]
     s = (keep_ref[...] + jnp.concatenate(got, axis=1)) * gain_ref[...]
     g = gm_ref[...] + factor * (
         s - jnp.mean(s, axis=1, keepdims=True) - unit * jnp.mean(s * unit, axis=1, keepdims=True)
     )
-    for k in range(4):
-        out_ref[k] = g[:, k * QUARTER : (k + 1) * QUARTER].astype(BF)
+    for k, ref in enumerate(refs[-4:]):
+        ref[...] = g[:, block_of(k)].astype(BF)
 
 
 def input_grad(keep, got, raw, g_mid, gain, *earlier):
@@ -645,17 +666,17 @@
     rows = pl.BlockSpec((block, D), lambda i: (i, 0))
     return pl.pallas_call(
         input_grad_kernel,
-        out_shape=shape((4, HALF, QUARTER), BF),
+        out_shape=(shape((HALF, QUARTER), BF),) * 4,
         grid=(HALF // block,),
         in_specs=[rows, rows, rows, rows, whole((1, D))] + [ANY] * len(earlier),
-        out_specs=pl.BlockSpec((4, block, QUARTER), lambda i: (0, i, 0)),
-        compiler_params=params(LIMIT),
-        cost_estimate=cost(2 * HALF * D * D),
+        out_specs=[pl.BlockSpec((block, QUARTER), lambda i: (i, 0))] * 4,
+        compiler_params=params(LIMIT),
         name="input_grad",
     )(keep, got, raw, g_mid, gain, *earlier)
 
 
-def mem_grad_kernel(g_ref, w_ref, raw_ref, gain_ref, conv_ref, _, gn_ref, gc_ref, unit_ref):
+def mem_grad_kernel(g_ref, w_ref, raw_ref, gain_ref, conv_ref, *refs):
+    gn_ref, gc_ref, unit_ref = refs[-3:]
     total = jnp.zeros((1, D), F32)
     for block in range(MROWS // 256):
         rows = slice(block * 256, block * 256 + 256)
@@ -676,19 +697,20 @@
             gn_ref[:, lanes] += conv_ref[t : t + 1, lanes] * term
 
 
-def mem_grad(g_mem, w_mem, raw, gain, conv, earlier):
+def mem_grad(g_mem, w_mem, raw, gain, conv, *earlier):
     return pl.pallas_call(
         mem_grad_kernel,
         out_shape=(shape((1, D), F32), shape((RATE, D), F32)),
         grid=(1,),
         in_specs=[
-            whole((KM, D)), whole((D, D)), whole((MROWS, D)), whole((1, D)), whole((RATE, D)), ANY,
-        ],
+            whole((KM, D)), whole((D, D)), whole((MROWS, D)), whole((1, D)), whole((RATE, D)),
+        ]
+        + [ANY] * len(earlier),
         out_specs=[whole((1, D)), whole((RATE, D))],
         scratch_shapes=[pltpu.VMEM((D // DH, MEM, DH), F32)],
         compiler_params=params(LIMIT),
         name="mem_grad",
-    )(g_mem, w_mem, raw, gain, conv, earlier)
+    )(g_mem, w_mem, raw, gain, conv, *earlier)
 
 
 def store_spans(grad, index, keep_ref, send_ref):
@@ -723,19 +745,18 @@
         + [ANY] * len(earlier),
         out_specs=[block, block],
         compiler_params=params(LIMIT),
-        cost_estimate=cost(2 * HEADS * DH * D * (3 * SEQ_LEN + 2 * KM)),
         name="qkv_grad",
     )(g_tok, x_tok, g_mem, x_mem, *earlier)
 
 
 def out_grad_kernel(own_ref, got_ref, g_ref, keep_ref, send_ref):
     for z, ref in enumerate((own_ref, got_ref)):
-        store_spans(nn(ref[...].T, g_ref[...]), (z, 0), keep_ref, send_ref)
+        store_spans(nn(ref[...].T, g_ref[...]), (0, z), keep_ref, send_ref)
 
 
 def out_grad(o, o_got, g_attn):
-    out = shape((2, 2, HEADS, DH // 4, D), BF)
-    block = pl.BlockSpec((2, 2, 1, DH // 4, D), lambda h: (0, 0, h, 0, 0))
+    out = shape((2, HEADS, 2, DH // 4, D), BF)
+    block = pl.BlockSpec((2, 1, 2, DH // 4, D), lambda h: (0, h, 0, 0, 0))
     half = pl.BlockSpec((HALF, DH), lambda h: (0, h))
     return pl.pallas_call(
         out_grad_kernel,
@@ -744,9 +765,51 @@
         in_specs=[half, half, whole((HALF, D))],
         out_specs=[block, block],
         compiler_params=params(LIMIT),
-        cost_estimate=cost(4 * HALF * HEADS * DH * D),
         name="out_grad",
     )(o, o_got, g_attn)
+
+
+def merge_kernel(count, lanes, *refs):
+    outs = refs[-2:]
+    for j, out in enumerate(outs):
+        if lanes:
+            half = slice(j * out.shape[-1], (j + 1) * out.shape[-1])
+            parts = [ref[:, half] for ref in refs[:count]]
+        else:
+            parts = [ref[...] for ref in refs[j * count : (j + 1) * count]]
+        out[...] = sum(part.astype(F32) for part in parts).astype(BF)
+
+
+def merge(arrays, *earlier, lanes=False, axis=0, work=0):
+    dims = arrays[0].shape
+    count = len(arrays)
+    if lanes:
+        out = dims[:-1] + (dims[-1] // 2,)
+        flat = [a.reshape(-1, dims[-1]) for a in arrays]
+        rows = flat[0].shape[0]
+        grid, out_dims = (1,), (rows, out[-1])
+        ins, blocks = [whole(flat[0].shape)] * count, [whole(out_dims)] * 2
+    else:
+        out = dims[:axis] + (dims[axis] // 2,) + dims[axis + 1 :]
+        outer = dims[0] if axis else 1
+        flat = [a.reshape(2 * outer, -1, dims[-1]) for a in arrays]
+        block = (1,) + flat[0].shape[1:]
+        grid, out_dims = (outer,), (outer,) + block[1:]
+        low = pl.BlockSpec(block, lambda i: (2 * i, 0, 0))
+        high = pl.BlockSpec(block, lambda i: (2 * i + 1, 0, 0))
+        same = pl.BlockSpec(block, lambda i: (i, 0, 0))
+        ins, blocks, flat = [low] * count + [high] * count, [same] * 2, flat * 2
+    pair = pl.pallas_call(
+        functools.partial(merge_kernel, count, lanes),
+        out_shape=(shape(out_dims, BF),) * 2,
+        grid=grid,
+        in_specs=ins + [ANY] * len(earlier),
+        out_specs=blocks,
+        compiler_params=params(LIMIT),
+        cost_estimate=cost(work) if work else None,
+        name="merge",
+    )(*flat, *earlier)
+    return [g.reshape(out) for g in pair]
 
 
 def pick(g, index, axis=0):
@@ -812,12 +875,37 @@
     tok_far, tok_near = swap(tok_other, "row", 2), swap(tok_mine, "row", 1)
     tok_pieces = [tok_mine, tok_near, tok_far, swap(tok_far, "row", 1)]
 
+    qkv = w_qkv.astype(BF).transpose(2, 1, 3, 0)
+    outs = w_out.astype(BF)
+    if heads_part % 2 == 0:
+        qkv = by_low(qkv.reshape(2, part, 3, span, QUARTER))
+        outs = by_low(outs.reshape(2, part, 1, span, QUARTER))
+        near = jnp.concatenate([qkv[0], outs[0], outs[1]], axis=1)
+        far = jnp.concatenate([qkv[1], outs[1], outs[0]], axis=1)
+        heads = jnp.stack(
+            [near, swap(far, "row", 1), swap(near, "row", 2), swap(far, "row", 3)]
+        )
+        heads = doubled_cols(after(heads[None], tok_near), n_col)
+    else:
+        qkv = jnp.stack([qkv] + [swap(qkv, "row", k) for k in (1, 2, 3)])
+        outs = jnp.stack([outs] + [swap(outs, "row", k) for k in (1, 2, 3)])
+        qkv = doubled_cols(jnp.where(low_first, qkv, swap(qkv, "col", 1))[None], n_col, 2)
+        outs = doubled_cols(outs[None], n_col, 2)
+        outs = by_low(jnp.stack([outs, swap(outs, "col", 1)]))
+        heads = jnp.concatenate([qkv, jnp.moveaxis(outs, 0, 3)], axis=3)
+    own = after(jnp.stack([w_up.astype(BF), w_down.astype(BF).T]), tok_far, tok_near)
+    w_far = swap(own, "row", 2)
+    heads = both([after(heads, w_far, tok_pieces[3])], "dp", 2)
+    own = after(own, w_far, tok_pieces[3])
+    w_near = swap(own, "row", 1)
+    w_both = swap(w_far, "row", 1)
     small = jnp.concatenate(
         [norm_attn, norm_ffn, conv_w.reshape(-1)]
         + [a.astype(F32) for a in (seg_ids, positions, keep_mask, mem_seg)]
     )
     small = after(small, tok_near)
-    shared = jnp.stack([small] + [swap(small, "row", k) for k in (1, 2, 3)])
+    shared = jnp.stack([small, swap(small, "row", 2)])
+    shared = jnp.stack([shared, swap(shared, "row", 1)], axis=1).reshape(4, -1)
     gains = shared[:, : 5 * QUARTER].reshape(4, 5, QUARTER).transpose(1, 0, 2).reshape(5, D)
     gain1, gain2, conv = gains[0:1], gains[1:2], gains[2:5]
     spans = seg_ids.shape[0] // SEQ_LEN
@@ -829,32 +917,14 @@
     row_attr = jnp.stack([seg, pos])
     col_attr = jnp.stack([jnp.where(keep == 1, seg, -2.0), pos, ids[3]], axis=1)
 
-    qkv = w_qkv.astype(BF).transpose(2, 1, 3, 0)
-    outs = w_out.astype(BF)
-    if heads_part % 2 == 0:
-        qkv = by_low(qkv.reshape(2, part, 3, span, QUARTER))
-        outs = by_low(outs.reshape(2, part, 1, span, QUARTER))
-        near = jnp.concatenate([qkv[0], outs[0], outs[1]], axis=1)
-        far = jnp.concatenate([qkv[1], outs[1], outs[0]], axis=1)
-        heads = jnp.stack(
-            [near, swap(far, "row", 1), swap(near, "row", 2), swap(far, "row", 3)]
-        )
-        heads = doubled_cols(heads[None], n_col)
-    else:
-        qkv = jnp.stack([qkv] + [swap(qkv, "row", k) for k in (1, 2, 3)])
-        outs = jnp.stack([outs] + [swap(outs, "row", k) for k in (1, 2, 3)])
-        qkv = doubled_cols(jnp.where(low_first, qkv, swap(qkv, "col", 1))[None], n_col, 2)
-        outs = doubled_cols(outs[None], n_col, 2)
-        outs = by_low(jnp.stack([outs, swap(outs, "col", 1)]))
-        heads = jnp.concatenate([qkv, jnp.moveaxis(outs, 0, 3)], axis=3)
-    heads = both(both([heads], "dp", 2), "dp", 1)
+    memories = jnp.concatenate(
+        [compressed.reshape(2, CMEM, QUARTER), memory.reshape(2, MEM, QUARTER)], axis=1
+    )
+    mem_other = after(pick(memories, 1 - z_high), w_far, tok_pieces[3])
+    mem_far = swap(mem_other, "row", 2)
+    heads = both([after(h, mem_far, w_near, w_both) for h in heads], "dp", 1)
     w_tok, w_mem, w_back = join_weights([heads[0], heads[2], heads[1], heads[3]])
-
-    own = after(jnp.stack([w_up.astype(BF), w_down.astype(BF).T]), tok_far, tok_near)
-    w_far = swap(own, "row", 2)
-    own = after(own, w_far, tok_pieces[3])
-    w_near = swap(own, "row", 1)
-    own = jnp.stack([own, w_near, w_far, swap(w_far, "row", 1)], axis=1)
+    own = jnp.stack([own, after(w_near, mem_far, heads[2], heads[3]), w_far, w_both], axis=1)
     half_col = n_col // 2
     distance = 1
     while distance < half_col:
@@ -863,27 +933,21 @@
     own_y, own_x = swap(own, "col", half_col), swap(own, "dp", 2)
     far_up, far_down = swap(own_x[0], "col", half_col), swap(own_y[1], "dp", 2)
 
-    memories = jnp.concatenate(
-        [compressed.reshape(2, CMEM, QUARTER), memory.reshape(2, MEM, QUARTER)], axis=1
-    )
-    mem_other = after(pick(memories, 1 - z_high), w_far, tok_pieces[3])
-    mem_far = swap(mem_other, "row", 2)
     mem_mine = after(pick(memories, z_high), mem_far, w_near)
     mem_near = swap(mem_mine, "row", 1)
     mem_pieces = [mem_mine, mem_near, mem_far, swap(mem_far, "row", 1)]
 
-    x_tok, raw_tok = tok_norm(where, tok_pieces, gain1)
+    x_tok, raw_tok = tok_norm(where, tok_pieces, after(gain1, heads[2]))
     tok_p = nt(x_tok, w_tok).astype(BF)
-    x_mem, raw_mem = mem_norm(mem_pieces, gain1, conv)
+    x_mem, raw_mem = mem_norm(mem_pieces, gain1, conv, tok_p)
     mem_p = nt(x_mem, w_mem).astype(BF)
-    cots = after(cotangent.reshape(4, HALF, QUARTER), mem_p, tok_p)
-    cot = jnp.concatenate(
-        [pick(cots, row)] + [swap(pick(cots, row ^ k), "row", k) for k in (1, 2, 3)], axis=1
-    )
+    cots = cotangent.reshape(4, HALF, QUARTER)
+    cots = [after(pick(cots, row ^ k), mem_p, tok_p) for k in range(4)]
+    cot = jnp.concatenate([cots[0]] + [swap(cots[k], "row", k) for k in (1, 2, 3)], axis=1)
     cot_got = swap(cot, "dp", 1)
     o, logs = attention_forward(tok_p, mem_p, row_attr, col_attr)
     o_got = swap(o[HALF:], "row", 1)
-    rec_q, rec_m = reconstruction(tok_p, mem_p, cot)
+    rec_q, rec_m = reconstruction(tok_p, mem_p, cot, own_x, own_y)
     mid, x2 = residual_mid(raw_tok, o, o_got, w_back, gain2, rec_m)
 
     x2_got = swap(x2, "dp", 1)
@@ -897,7 +961,8 @@
     go_got = swap(go_send, "row", 1)
 
     own, own_y, own_x, far_up, far_down = grads
-    far_up, far_down = swap(far_up, "col", half_col), swap(far_down, "dp", 2)
+    far_up = after(swap(far_up, "col", half_col), go_got)
+    far_down = after(swap(far_down, "dp", 2), go_got)
     sum_x = own_x.at[0].set(add_low(own_x[0], far_up))
     sum_y = own_y.at[1].set(add_low(own_y[1], far_down))
     got_x, got_y = swap(sum_x, "dp", 2), swap(sum_y, "col", half_col)
@@ -911,82 +976,98 @@
         return jnp.concatenate(blocks, axis=0)
 
     out_got = swap(out_send, "dp", 1)
-    out_low = (mid + (out_keep + out_got.astype(F32))).astype(BF)
-    out_low = after(jnp.stack([out_low[:, block_of(k)] for k in range(4)]), go_got)
-    outs = to_owners([out_low[k] for k in range(4)])
     g_out = out_grad(o, o_got, g_attn)
+    outs = out_sum(mid, out_keep, out_got, g_out[1])
+    outs = to_owners([outs[0]] + [after(piece, go_got) for piece in outs[1:]])
 
     g_tok, g_mem = attention_backward(
         tok_p, mem_p, go_keep, go_got, o, logs, rec_q, rec_m, row_attr, col_attr,
-        sum_x, sum_y, out_low, g_out[0],
+        sum_x, sum_y, outs[0],
     )
     gx, gx_send, gain1_tok = tok_grad(g_tok, w_tok, raw_tok, *outs[1:])
     gx_got = swap(gx_send, "row", 1)
-
-    total = (own.astype(F32) + got_x.astype(F32) + got_y.astype(F32)).astype(BF)
     distance = half_col
-    while distance > 1:
-        distance //= 2
-        n = total.shape[3] // 2
-        total = add_low(total[..., :n], swap(total[..., n:], "col", distance))
-    odd = total[:, 1::2]
-    g_qkv = qkv_grad(g_tok, x_tok, g_mem, x_mem, odd, gx_send)
-    grad_qkv, grad_out = reduce_heads(g_qkv, g_out, n_col, heads_part, by_low, low_first)
-    even = add_low(total[:, 0::2], swap(odd, "row", 1))
-    grads = even[:, 0].astype(F32) + swap(even[:, 1], "row", 2).astype(F32)
-
-    d_rows = input_grad(gx, gx_got, raw_tok, g_mid, gain1, even, g_qkv[0])
-    d_input = in_order(to_owners([d_rows[k] for k in range(4)]))
-    out = in_order(outs)
-    gain1_mem, conv_sum = mem_grad(g_mem, w_mem, raw_mem, gain1, conv, g_qkv[0])
-    total = jnp.concatenate([gain1_tok + gain1_mem, gain2_sum, conv_sum], axis=0)
-    total = total.reshape(5, 4, QUARTER).transpose(1, 0, 2)
+    if distance > 1:
+        total = (own.astype(F32) + got_x.astype(F32) + got_y.astype(F32)).astype(BF)
+        while distance > 1:
+            distance //= 2
+            n = total.shape[3] // 2
+            total = add_low(total[..., :n], swap(total[..., n:], "col", distance))
+        even, odd = total[:, :2], total[:, 2:]
+    else:
+        even, odd = merge([own, got_x, got_y], gx_send, axis=1)
+
+    def halves(g):
+        return g.reshape((n_col, part) + g.shape[1:])
+
+    g_qkv = qkv_grad(g_tok, x_tok, g_mem, x_mem, odd)
+    g_out, out_send = merge([g_out[0], swap(g_out[1], "dp", 1)], g_qkv[1])
+    out_got = swap(out_send, "dp", 2)
+    gain1_mem, conv_sum = mem_grad(g_mem, w_mem, raw_mem, gain1, conv, out_send)
+    d_rows = input_grad(gx, gx_got, raw_tok, g_mid, gain1, gain1_mem)
+    d_input = to_owners(d_rows)
+    if heads_part % 2 == 0:
+        g_out, out_send = merge([halves(g_out[0]), halves(out_got[0])], d_rows[0])
+    even, even_send = merge([even, swap(odd, "row", 1)], out_send, axis=1, work=20_000_000_000)
+    even_got = swap(even_send[:, 0], "row", 2)
+    g_qkv, qkv_send = merge([g_qkv[0], swap(g_qkv[1], "dp", 1)], even_send)
+    qkv_got = swap(qkv_send, "dp", 2)
+    if heads_part % 2 == 0:
+        def over_row(g, got, first, second):
+            g, send = merge([g, got], first, lanes=True)
+            g, last = merge([g, swap(send, "row", 2)], second, lanes=True)
+            return g, swap(last, "row", 1), send
+
+        out_pair = over_row(g_out[0], swap(out_send[0], "col", 1), qkv_send, *d_input[3:])
+        g_qkv, qkv_send = merge(
+            [halves(g_qkv[0]), halves(qkv_got[0])], out_pair[2], *d_input[1:]
+        )
+        g_qkv, got, last = over_row(
+            g_qkv[0], swap(qkv_send[0], "col", 1), out_pair[0], out_pair[0]
+        )
+        grad_qkv = by_low(jnp.stack([g_qkv, got])).astype(F32)
+        grad_qkv = grad_qkv.reshape(heads_part, 3, span, QUARTER)
+        g_out, got, _ = out_pair
+        g_out, got = jnp.swapaxes(g_out, 0, 1), jnp.swapaxes(got, 0, 1)
+        grad_out = by_low(g_out.astype(F32) + jnp.flip(got, axis=0).astype(F32))
+        grad_out = grad_out.reshape(heads_part, span, QUARTER)
+    else:
+        g_out, g_qkv = add_low(g_out[0], out_got[0]), add_low(g_qkv[0], qkv_got[0])
+        g_qkv = halve_col(g_qkv, 2)
+        qkv_send = g_qkv
+        grad_qkv, grad_out = reduce_heads(g_qkv, g_out, by_low, low_first)
+        last = d_rows[0]
+    vectors = jnp.concatenate([gain1_tok + gain1_mem, gain2_sum, conv_sum], axis=0)
+    vectors = after(vectors, qkv_send)
+    vectors = vectors.reshape(5, 4, QUARTER).transpose(1, 0, 2)
     for distance in (1, 2):
-        total = total + swap(total, "dp", distance)
+        vectors = vectors + swap(vectors, "dp", distance)
     distance = 1
     while distance < n_col:
-        total = total + swap(total, "col", distance)
+        vectors = vectors + swap(vectors, "col", distance)
         distance *= 2
-    total = total[:2] + swap(total[2:], "row", 2)
-    total = total[0] + swap(total[1], "row", 1)
+    vectors = after(vectors, last, even_got)
+    vectors = vectors[:2] + swap(vectors[2:], "row", 2)
+    vectors = vectors[0] + swap(vectors[1], "row", 1)
+    grad_qkv = grad_qkv.transpose(3, 1, 0, 2)
+    grads = even[:, 0].astype(F32) + even_got.astype(F32)
+    d_input, out = in_order(d_input), in_order(outs)
     return (
-        out, d_input, grad_qkv, grad_out, grads[0], grads[1].T, total[0], total[1], total[2:]
-    )
-
-
-def reduce_heads(g_qkv, g_out, n_col, heads_part, by_low, low_first):
+        out, d_input, grad_qkv, grad_out, grads[0], grads[1].T, vectors[0], vectors[1], vectors[2:]
+    )
+
+
+def reduce_heads(g_qkv, g_out, by_low, low_first):
     span = DH // 4
-
-    def over_dp(keep, send):
-        g = add_low(keep, swap(send, "dp", 1))
-        return add_low(g[0], swap(g[1], "dp", 2))
-
-    def over_row(g):
-        g = add_low(g[..., : D // 2], swap(g[..., D // 2 :], "row", 2))
-        return g[..., :QUARTER], swap(g[..., QUARTER:], "row", 1)
-
-    g_out = over_dp(*g_out)
-    g_qkv = over_dp(*g_qkv)
-    if heads_part % 2 == 0:
-        part = heads_part // 2
-        g_out = halve_col(jnp.swapaxes(g_out.reshape((2, n_col, part) + g_out.shape[2:]), 0, 1))
-        g_qkv = halve_col(g_qkv.reshape((n_col, part) + g_qkv.shape[1:]))
-        g_qkv = by_low(jnp.stack(over_row(g_qkv))).astype(F32)
-        g_qkv = g_qkv.reshape(heads_part, 3, span, QUARTER)
-        g_out, got = over_row(g_out)
-        g_out = by_low(g_out.astype(F32) + jnp.flip(got, axis=0).astype(F32))
-        g_out = g_out.reshape(heads_part, span, QUARTER)
-    else:
-        g_qkv = halve_col(g_qkv, 2)
-        zeros = jnp.zeros_like(g_qkv)
-        g_qkv = add_low(
-            jnp.where(low_first, g_qkv, zeros), swap(jnp.where(low_first, zeros, g_qkv), "col", 1)
-        )
-        g_out = by_low(g_out)
-        g_out = halve_col(add_low(g_out[0], swap(g_out[1], "col", 1)), 2)
-        g_qkv = halve_row(jnp.moveaxis(g_qkv.reshape(3, span, 4, QUARTER), 2, 0))[None]
-        g_out = halve_row(jnp.moveaxis(g_out.reshape(span, 4, QUARTER), 1, 0))[None]
-    return g_qkv.transpose(3, 1, 0, 2), g_out
+    zeros = jnp.zeros_like(g_qkv)
+    g_qkv = add_low(
+        jnp.where(low_first, g_qkv, zeros), swap(jnp.where(low_first, zeros, g_qkv), "col", 1)
+    )
+    g_out = by_low(jnp.swapaxes(g_out, 0, 1))
+    g_out = halve_col(add_low(g_out[0], swap(g_out[1], "col", 1)), 2)
+    g_qkv = halve_row(jnp.moveaxis(g_qkv.reshape(3, span, 4, QUARTER), 2, 0))[None]
+    g_out = halve_row(jnp.moveaxis(g_out.reshape(span, 4, QUARTER), 1, 0))[None]
+    return g_qkv, g_out
 
 
 def solution(mesh):

time: 512 us -> 485 us (0.947)
  waiting for transfers between devices: 175 us -> 132 us
  Pallas kernels: 181 us -> 208 us
  other arithmetic: 37.9 us -> 25 us
    ppermute x60 -> x59, waiting for transfers between devices: 175 us -> 132 us  [swap(): return lax.ppermute(x, axis, [(i, i ^ distance) for i in range(n)])]
    pallas_call x1 -> x12, Pallas kernels: 4.34 us -> 31.8 us  [the longest x10 24 us: merge(): pl.pallas_call(functools.partial(merge_kernel, count, lanes), out_shape=(...]
    convert_element_type x9 -> x0, other arithmetic: 11.4 us -> none  [the longest x7 5.75 us: add_low(): return (a.astype(F32) + b.astype(F32)).astype(BF)]
    ppermute x60 -> x59, starting transfers between devices: 66.3 us -> 63.5 us  [swap(): return lax.ppermute(x, axis, [(i, i ^ distance) for i in range(n)])]
    unnamed x88 -> x132, local copies, waits for them, and re-layouts: 16.3 us -> 18.1 us
  transfers between devices with their start and end apart: 60 -> 59, of which waited for: 27 -> 25; matrix products, arithmetic and copies ran while one was open for 14% -> 11% of each run, Pallas kernels for 27% -> 34%
where the time goes in v3:
time: 485 us; the launch traced here: 480 us
  Pallas kernels  208 us (43%)
  waiting for transfers between devices  132 us (27%)
  starting transfers between devices  63.5 us (13%)
  local copies, waits for them, and re-layouts  35.9 us (7%)
  other arithmetic  25 us (5%)
  matrix products  13.4 us (3%)
    ppermute x59, waiting for transfers between devices, swap(): return lax.ppermute(x, axis, [(i, i ^ distance) for i in range(n)])  132 us
    ppermute x59, starting transfers between devices, swap(): return lax.ppermute(x, axis, [(i, i ^ distance) for i in range(n)])  63.5 us
    pallas_call x1, Pallas kernels, feed_forward(): pl.pallas_call(ffn_kernel, out_shape=(shape((HALF, D), F32), shape((HALF,...  43.1 us
    pallas_call x1, Pallas kernels, attention_backward(): pl.pallas_call(backward_kernel, out_shape=(shape((SEQ_LEN, HEADS * 3 * DH...  37 us
    pallas_call x1, Pallas kernels, attention_forward(): pl.pallas_call(forward_kernel, out_shape=(shape((SEQ_LEN, HEADS * DH), BF...  25.3 us
    pallas_call x10, Pallas kernels, merge(): pl.pallas_call(functools.partial(merge_kernel, count, lanes), out_shape=(...  24 us
    unnamed x132, local copies, waits for them, and re-layouts  18.1 us
    dot_general x2, matrix products, nt(): lax.dot_general(a, b, (((1,), (1,)), ((), ())), preferred_element_type=F32)  13.4 us
  transfers between devices with their start and end apart: 59, of which 25 were waited for; matrix products, arithmetic and copies ran while one was open for 11% of the time, Pallas kernels for 34%

profile of v3, /device:TPU:0, one launch (start us, length us, event | category | flops | bytes accessed | tf_op | source)
XLA Modules:
  0.0 479.6 jit_solution(2575586315285138481)
XLA Ops:
  3.6 5.1 %collective-permute-start.7 = (bf16[2,5,32,256]{3,2,1,0:T(8,128)(2,1)}, bf16[2,5,32,256]{3,2,1,0:T(8,128)(2,1)}, u32[]{:S(2)}, u32[]{:S(2)}) collective-permute-start(bf16[2,5,32,256]{3,2,1,0:T(8,128)(2,1)} %get-tuple-element.223), channel_id=1, source_target_pairs={{0,6},{2,4},{4,2},{6,0},{1,7},{3,5},{5,3},{7,1},{8,14},{10,12},{12... | collective-permute-start | bytes 491528 | tf_op jit(solution)/shard_map/ppermute | solution.py:49
  14.8 20.3 %collective-permute-done.6 = bf16[2,5,32,256]{3,2,1,0:T(8,128)(2,1)} collective-permute-done((bf16[2,5,32,256]{3,2,1,0:T(8,128)(2,1)}, bf16[2,5,32,256]{3,2,1,0:T(8,128)(2,1)}, u32[]{:S(2)}, u32[]{:S(2)}) %collective-permute-start.6) | collective-permute-done | bytes 163872 | tf_op jit(solution)/shard_map/ppermute | solution.py:49
  37.1 4.9 %collective-permute-done.refs_1_.refs_2_.p1 = bf16[1024,256]{1,0:T(8,128)(2,1)S(1)} collective-permute-done((bf16[1024,256]{1,0:T(8,128)(2,1)S(1)}, bf16[1024,256]{1,0:T(8,128)(2,1)S(1)}, u32[]{:S(2)}, u32[]{:S(2)}) %collective-permute-start) | collective-permute-done | bytes 524320 | tf_op jit(solution)/shard_map/ppermute | solution.py:49
  49.2 9.5 %collective-permute-done.8 = bf16[1,4,2,5,32,256]{5,4,3,2,1,0:T(8,128)(2,1)S(1)} collective-permute-done((bf16[1,4,2,5,32,256]{5,4,3,2,1,0:T(8,128)(2,1)}, bf16[1,4,2,5,32,256]{5,4,3,2,1,0:T(8,128)(2,1)S(1)}, u32[]{:S(2)}, u32[]{:S(2)}) %collective-permute-start.8) | collective-permute-done | bytes 655392 | tf_op jit(solution)/shard_map/ppermute | solution.py:49
  59.9 9.1 %collective-permute-done.2.refs_2_.p3 = bf16[1024,256]{1,0:T(8,128)(2,1)S(1)} collective-permute-done((bf16[1024,256]{1,0:T(8,128)(2,1)}, bf16[1024,256]{1,0:T(8,128)(2,1)S(1)}, u32[]{:S(2)}, u32[]{:S(2)}) %collective-permute-start.2) | collective-permute-done | bytes 524320 | tf_op jit(solution)/shard_map/ppermute | solution.py:49
  80.9 3.1 collective-permute-start.10
  88.4 25.9 %collective-permute-done.4 = f32[2,5376]{1,0:T(2,128)} collective-permute-done((f32[2,5376]{1,0:T(2,128)S(1)}, f32[2,5376]{1,0:T(2,128)}, u32[]{:S(2)}, u32[]{:S(2)}) %collective-permute-start.4) | collective-permute-done | bytes 43040 | tf_op jit(solution)/shard_map/ppermute | solution.py:49
  130.6 5.8 %join_weights.1 = (bf16[1536,1024]{1,0:T(8,128)(2,1)}, bf16[1024,1024]{1,0:T(8,128)(2,1)}, bf16[1024,1024]{1,0:T(8,128)(2,1)}) custom-call(bf16[2,4,2,5,32,256]{5,4,3,2,1,0:T(8,128)(2,1)} %after.28.refs_0_, bf16[2,4,2,5,32,256]{5,4,3,2,1,0:T(8,128)(2,1)} %copy-done.4, bf16[2,4,2,5,32,256]{5,4,3,2,1,0:T(8,128)(2,1)} %after.30.refs_2_, ...), custom_call_target="tpu_custom_call" | custom-call | tf_op jit(solution)/shard_map/join_weights/pallas_call | solution.py:175
  136.4 5.3 %tok_norm.1 = (bf16[1024,1024]{1,0:T(8,128)(2,1)}, bf16[1024,1024]{1,0:T(8,128)(2,1)}) custom-call(s32[1]{0:T(128)} %bitcast.where, bf16[1024,256]{1,0:T(8,128)(2,1)} %copy-done.23, bf16[1024,256]{1,0:T(8,128)(2,1)} %copy-done.5, bf16[1024,256]{1,0:T(8,128)(2,1)} %copy-done.24, bf16[1024,256]{1,0:T(8,128)(2,1)} %copy-done.6, f32[1,1024]{1,0:T(1,128)} %after.29.gain_ref), custom_call_target="tpu_custom_call" | custom-call | tf_op jit(solution)/shard_map/tok_norm/pallas_call | solution.py:104
  141.8 7.7 %convolution_convert_fusion.1._.tok_ref.refs_2_ = bf16[1024,1536]{1,0:T(8,128)(2,1)} fusion(bf16[1024,1024]{1,0:T(8,128)(2,1)} %get-tuple-element.100.xt_ref, bf16[1536,1024]{1,0:T(8,128)(2,1)} %get-tuple-element.101.w_ref), kind=kOutput, calls=%fused_computation.1 | convolution fusion | flops 3222798336 | bytes 8388608 | tf_op jit(solution)/shard_map/dot_general | solution.py:40
  149.5 5.3 %mem_norm.1 = (bf16[1152,1024]{1,0:T(8,128)(2,1)}, bf16[1024,1024]{1,0:T(8,128)(2,1)}) custom-call(bf16[1024,256]{1,0:T(8,128)(2,1)} %after.31.p0, bf16[1024,256]{1,0:T(8,128)(2,1)} %collective-permute-done.16.p1, bf16[1024,256]{1,0:T(8,128)(2,1)} %copy-done.1, bf16[1024,256]{1,0:T(8,128)(2,1)} %collective-permute-done.17.p3, f32[1,1024]{1,0:T(1,128)} %bitcast.205, ...), custom_call_target="tpu_custom_call" | custom-call | tf_op jit(solution)/shard_map/mem_norm/pallas_call | solution.py:140
  154.8 5.7 %convolution_convert_fusion.mem_ref.refs_1_ = bf16[1152,1024]{1,0:T(8,128)(2,1)} fusion(bf16[1152,1024]{1,0:T(8,128)(2,1)} %get-tuple-element.102.xm_ref, bf16[1024,1024]{1,0:T(8,128)(2,1)S(1)} %copy-done.22), kind=kOutput, calls=%fused_computation | convolution fusion | flops 2417098752 | bytes 6815744 | tf_op jit(solution)/shard_map/dot_general | solution.py:40
  164.9 25.3 %attention_forward.1 = (bf16[1024,512]{1,0:T(8,128)(2,1)}, f32[4,1,1024]{2,1,0:T(1,128)}) custom-call(bf16[1024,1536]{1,0:T(8,128)(2,1)} %convolution_convert_fusion.1._.tok_ref.refs_2_, bf16[1152,1024]{1,0:T(8,128)(2,1)} %convolution_convert_fusion.mem_ref.refs_1_, f32[2,1024]{1,0:T(2,128)} %stack.93.row_ref, f32[1024,3]{1,0:T(8,128)} %copy.84.col_ref), custom_call_target="tpu_custom_call" | custom-call | flops 24999999488 | bytes 25000000 | tf_op jit(solution)/shard_map/attention_forward/pallas_call | solution.py:252
  198.0 12.0 %reconstruction.1 = (f32[4,128,1024]{2,1,0:T(8,128)}, f32[640,1024]{1,0:T(8,128)}) custom-call(bf16[1024,1536]{1,0:T(8,128)(2,1)} %convolution_convert_fusion.1._.tok_ref.refs_2_, bf16[1152,1024]{1,0:T(8,128)(2,1)} %convolution_convert_fusion.mem_ref.refs_1_, bf16[512,1024]{1,0:T(8,128)(2,1)} %copy-done.19, ...), custom_call_target="tpu_custom_call" | custom-call | flops 10000000000 | bytes 10000000 | tf_op jit(solution)/shard_map/reconstruction/pallas_call | solution.py:306
  210.8 5.1 %residual_mid.1 = (f32[512,1024]{1,0:T(8,128)}, bf16[512,1024]{1,0:T(8,128)(2,1)}) custom-call(bf16[1024,1024]{1,0:T(8,128)(2,1)} %get-tuple-element.99.raw_ref, bf16[1024,512]{1,0:T(8,128)(2,1)} %get-tuple-element.104.own_ref.o_ref, bf16[512,512]{1,0:T(8,128)(2,1)} %copy-done.27, bf16[1024,1024]{1,0:T(8,128)(2,1)} %get-tuple-element.105.w_ref, ...), custom_call_target="tpu_custom_call" | custom-call | flops 2147483648 | bytes 2147483 | tf_op jit(solution)/shard_map/residual_mid/pallas_call | solution.py:439
  216.0 4.5 collective-permute-done.27.refs_8_
  223.1 43.1 %feed_forward.1 = (f32[512,1024]{1,0:T(8,128)}, bf16[512,1024]{1,0:T(8,128)(2,1)}, f32[512,1024]{1,0:T(8,128)}, bf16[512,1024]{1,0:T(8,128)(2,1)}, bf16[2,4,256,...) custom-call(bf16[512,1024]{1,0:T(8,128)(2,1)} %get-tuple-element.108, ...), custom_call_target="tpu_custom_call" | custom-call | flops 25769803776 | bytes 25769804 | tf_op jit(solution)/shard_map/feed_forward/pallas_call | solution.py:538
  270.2 6.5 %mid_back.1 = (f32[512,1024]{1,0:T(8,128)}, bf16[512,1024]{1,0:T(8,128)(2,1)}, bf16[512,512]{1,0:T(8,128)(2,1)}, bf16[512,512]{1,0:T(8,128)(2,1)}, f32[1,1024]{1,0:T(1,128)}) custom-call(f32[512,1024]{1,0:T(8,128)} %get-tuple-element.111.gx_ref, bf16[512,1024]{1,0:T(8,128)(2,1)} %copy-done.35, f32[512,1024]{1,0:T(8,128)} %get-tuple-element.107.mid_ref, ...), custom_call_target="tpu_custom_call" | custom-call | flops 1073741824 | bytes 1073741 | tf_op jit(solution)/shard_map/mid_back/pallas_call | solution.py:600
  282.2 5.0 %out_grad.1 = (bf16[2,4,2,32,1024]{4,3,2,1,0:T(8,128)(2,1)}, bf16[2,4,2,32,1024]{4,3,2,1,0:T(8,128)(2,1)}) custom-call(bf16[1024,512]{1,0:T(8,128)(2,1)} %get-tuple-element.104.own_ref.o_ref, bf16[512,512]{1,0:T(8,128)(2,1)} %copy-done.27, bf16[512,1024]{1,0:T(8,128)(2,1)} %get-tuple-element.113.g_ref), custom_call_target="tpu_custom_call" | custom-call | tf_op jit(solution)/shard_map/out_grad/pallas_call | solution.py:761
  287.2 3.4 out_sum.1
  304.9 37.0 %attention_backward.1 = (bf16[1024,1536]{1,0:T(8,128)(2,1)}, bf16[1152,1024]{1,0:T(8,128)(2,1)}) custom-call(bf16[1024,1536]{1,0:T(8,128)(2,1)} %convolution_convert_fusion.1._.tok_ref.refs_2_, bf16[1152,1024]{1,0:T(8,128)(2,1)} %convolution_convert_fusion.mem_ref.refs_1_, bf16[512,512]{1,0:T(8,128)(2,1)} %get-tuple-element.120.own_ref, ...), custom_call_target="tpu_custom_call" | custom-call | flops 35000000512 | bytes 35000000 | tf_op jit(solution)/shard_map/attention_backward/pallas_call | solution.py:386
  341.9 8.4 %tok_grad.1 = (f32[512,1024]{1,0:T(8,128)}, bf16[512,1024]{1,0:T(8,128)(2,1)}, f32[1,1024]{1,0:T(1,128)}) custom-call(bf16[1024,1536]{1,0:T(8,128)(2,1)} %get-tuple-element.127.g_ref.gt_ref, bf16[1536,1024]{1,0:T(8,128)(2,1)} %get-tuple-element.101.w_ref, bf16[1024,1024]{1,0:T(8,128)(2,1)} %get-tuple-element.99.raw_ref, bf16[512,256]{1,0:T(8,128)(2,1)} %copy-done.29, ...), custom_call_target="tpu_custom_call" | custom-call | tf_op jit(solution)/shard_map/tok_grad/pallas_call | solution.py:637
  351.7 4.1 merge.10
  357.8 10.6 %qkv_grad.1 = (bf16[2,4,3,32,1024]{4,3,2,1,0:T(8,128)(2,1)}, bf16[2,4,3,32,1024]{4,3,2,1,0:T(8,128)(2,1)}) custom-call(bf16[1024,1536]{1,0:T(8,128)(2,1)} %get-tuple-element.127.g_ref.gt_ref, bf16[1024,1024]{1,0:T(8,128)(2,1)} %get-tuple-element.100.xt_ref, bf16[1152,1024]{1,0:T(8,128)(2,1)} %get-tuple-element.131.gm_ref.g_ref, ...), custom_call_target="tpu_custom_call" | custom-call | tf_op jit(solution)/shard_map/qkv_grad/pallas_call | solution.py:735
  372.8 6.8 %mem_grad.1 = (f32[1,1024]{1,0:T(1,128)}, f32[3,1024]{1,0:T(4,128)}) custom-call(bf16[1152,1024]{1,0:T(8,128)(2,1)} %get-tuple-element.131.gm_ref.g_ref, bf16[1024,1024]{1,0:T(8,128)(2,1)} %get-tuple-element.103.w_ref, bf16[1024,1024]{1,0:T(8,128)(2,1)} %get-tuple-element.132.raw_ref, f32[1,1024]{1,0:T(1,128)} %bitcast.206, f32[3,1024]{1,0:T(4,128)} %bitcast.199, ...), custom_call_target="tpu_custom_call" | custom-call | tf_op jit(solution)/shard_map/mem_grad/pallas_call | solution.py:701
  379.6 4.3 input_grad.1
  390.4 14.4 %collective-permute-done.44 = bf16[2,2,256,512]{3,2,1,0:T(8,128)(2,1)} collective-permute-done((bf16[2,2,256,512]{3,2,1,0:T(8,128)(2,1)}, bf16[2,2,256,512]{3,2,1,0:T(8,128)(2,1)}, u32[]{:S(2)}, u32[]{:S(2)}) %collective-permute-start.44) | collective-permute-done | bytes 1048608 | tf_op jit(solution)/shard_map/ppermute | solution.py:49
  408.5 3.2 merge.14
  423.1 4.2 collective-permute-done.46
  434.9 5.4 %collective-permute-done.53.refs_2_ = bf16[2,256,512]{2,1,0:T(8,128)(2,1)S(1)} collective-permute-done((bf16[2,256,512]{2,1,0:T(8,128)(2,1)}, bf16[2,256,512]{2,1,0:T(8,128)(2,1)S(1)}, u32[]{:S(2)}, u32[]{:S(2)}) %collective-permute-start.53) | collective-permute-done | bytes 524320 | tf_op jit(solution)/shard_map/ppermute | solution.py:49
  462.4 8.1 %collective-permute-done.50 = bf16[2,3,32,512]{3,2,1,0:T(8,128)(2,1)S(1)} collective-permute-done((bf16[2,3,32,512]{3,2,1,0:T(8,128)(2,1)}, bf16[2,3,32,512]{3,2,1,0:T(8,128)(2,1)S(1)}, u32[]{:S(2)}, u32[]{:S(2)}) %collective-permute-start.50) | collective-permute-done | bytes 196640 | tf_op jit(solution)/shard_map/ppermute | solution.py:49
  474.0 3.7 collective-permute-done.51
  (341 shorter events, 155.2 us)
Async XLA Ops:
  3.6 31.5 %collective-permute-start.7 = (bf16[2,5,32,256]{3,2,1,0:T(8,128)(2,1)}, bf16[2,5,32,256]{3,2,1,0:T(8,128)(2,1)}, u32[]{:S(2)}, u32[]{:S(2)}) collective-permute-start(bf16[2,5,32,256]{3,2,1,0:T(8,128)(2,1)} %get-tuple-element.223), channel_id=1, source_target_pairs={{0,6},{2,4},{4,2},{6,0},{1,7},{3,5},{5,3},{7,1},{8,14},{10,12},{12... | collective-permute-start | bytes 491528 | tf_op jit(solution)/shard_map/ppermute | solution.py:49
  8.7 26.4 %collective-permute-start.5 = (bf16[2,5,32,256]{3,2,1,0:T(8,128)(2,1)}, bf16[2,5,32,256]{3,2,1,0:T(8,128)(2,1)}, u32[]{:S(2)}, u32[]{:S(2)}) collective-permute-start(bf16[2,5,32,256]{3,2,1,0:T(8,128)(2,1)} %get-tuple-element.223), channel_id=1, source_target_pairs={{0,2},{2,0},{4,6},{6,4},{1,3},{3,1},{5,7},{7,5},{8,10},{10,8},{12,... | collective-permute-start | bytes 491528 | tf_op jit(solution)/shard_map/ppermute | solution.py:49
  8.7 26.4 %collective-permute-start.6 = (bf16[2,5,32,256]{3,2,1,0:T(8,128)(2,1)}, bf16[2,5,32,256]{3,2,1,0:T(8,128)(2,1)}, u32[]{:S(2)}, u32[]{:S(2)}) collective-permute-start(bf16[2,5,32,256]{3,2,1,0:T(8,128)(2,1)} %get-tuple-element.222), channel_id=1, source_target_pairs={{0,4},{2,6},{4,0},{6,2},{1,5},{3,7},{5,1},{7,3},{8,12},{10,14},{12... | collective-permute-start | bytes 491528 | tf_op jit(solution)/shard_map/ppermute | solution.py:49
  10.2 35.1 %collective-permute-start.1 = (bf16[1024,256]{1,0:T(8,128)(2,1)}, bf16[1024,256]{1,0:T(8,128)(2,1)S(1)}, u32[]{:S(2)}, u32[]{:S(2)}) collective-permute-start(bf16[1024,256]{1,0:T(8,128)(2,1)} %get-tuple-element.217), channel_id=1, source_target_pairs={{0,4},{2,6},{4,0},{6,2},{1,5},{3,7},{5,1},{7,3},{8,12},{10,14},{12... | collective-permute-start | bytes 1572872 | tf_op jit(solution)/shard_map/ppermute | solution.py:49
  12.5 29.5 %collective-permute-start = (bf16[1024,256]{1,0:T(8,128)(2,1)S(1)}, bf16[1024,256]{1,0:T(8,128)(2,1)S(1)}, u32[]{:S(2)}, u32[]{:S(2)}) collective-permute-start(bf16[1024,256]{1,0:T(8,128)(2,1)S(1)} %get-tuple-element.218.p0), channel_id=1, source_target_pairs={{0,2},{2,0},{4,6},{6,4},{1,3},{3,1},{5,7},{7,5},{8,10},{10,8},{12,... | collective-permute-start | bytes 1572872 | tf_op jit(solution)/shard_map/ppermute | solution.py:49
  72.3 42.9 %collective-permute-start.14 = (bf16[2,4,2,5,32,256]{5,4,3,2,1,0:T(8,128)(2,1)}, bf16[2,4,2,5,32,256]{5,4,3,2,1,0:T(8,128)(2,1)S(1)}, u32[]{:S(2)}, u32[]{:S(2)}) collective-permute-start(bf16[2,4,2,5,32,256]{5,4,3,2,1,0:T(8,128)(2,1)} %after.25.refs_0_), channel_id=1, source_target_pairs={{0,16},{8,24},{16,0},{24,8},{1,17},{9,25},{17,1},{25,9},{2,18},{10... | collective-permute-start | bytes 3932168 | tf_op jit(solution)/shard_map/ppermute | solution.py:49
  79.4 35.7 %collective-permute-start.11 = (bf16[2,256,512]{2,1,0:T(8,128)(2,1)}, bf16[2,256,512]{2,1,0:T(8,128)(2,1)S(1)}, u32[]{:S(2)}, u32[]{:S(2)}) collective-permute-start(bf16[2,256,512]{2,1,0:T(8,128)(2,1)} %after.27), channel_id=1, source_target_pairs={{0,2},{2,0},{4,6},{6,4},{1,3},{3,1},{5,7},{7,5},{8,10},{10,8},{12,... | collective-permute-start | bytes 1572872 | tf_op jit(solution)/shard_map/ppermute | solution.py:49
  80.9 34.2 %collective-permute-start.10 = (bf16[1024,256]{1,0:T(8,128)(2,1)}, bf16[1024,256]{1,0:T(8,128)(2,1)S(1)}, u32[]{:S(2)}, u32[]{:S(2)}) collective-permute-start(bf16[1024,256]{1,0:T(8,128)(2,1)} %after.26), channel_id=1, source_target_pairs={{0,4},{2,6},{4,0},{6,2},{1,5},{3,7},{5,1},{7,3},{8,12},{10,14},{12... | collective-permute-start | bytes 1572872 | tf_op jit(solution)/shard_map/ppermute | solution.py:49
  84.1 31.1 %collective-permute-start.12 = (bf16[2,256,512]{2,1,0:T(8,128)(2,1)S(1)}, bf16[2,256,512]{2,1,0:T(8,128)(2,1)S(1)}, u32[]{:S(2)}, u32[]{:S(2)}) collective-permute-start(bf16[2,256,512]{2,1,0:T(8,128)(2,1)S(1)} %copy-done.9), channel_id=1, source_target_pairs={{0,2},{2,0},{4,6},{6,4},{1,3},{3,1},{5,7},{7,5},{8,10},{10,8},{12,... | collective-permute-start | bytes 1572872 | tf_op jit(solution)/shard_map/ppermute | solution.py:49
  84.5 29.8 %collective-permute-start.4 = (f32[2,5376]{1,0:T(2,128)S(1)}, f32[2,5376]{1,0:T(2,128)}, u32[]{:S(2)}, u32[]{:S(2)}) collective-permute-start(f32[2,5376]{1,0:T(2,128)S(1)} %get-tuple-element.227), channel_id=1, source_target_pairs={{0,2},{2,0},{4,6},{6,4},{1,3},{3,1},{5,7},{7,5},{8,10},{10,8},{12,... | collective-permute-start | bytes 129032 | tf_op jit(solution)/shard_map/ppermute | solution.py:49
  121.9 27.6 %collective-permute-start.16 = (bf16[1024,256]{1,0:T(8,128)(2,1)}, bf16[1024,256]{1,0:T(8,128)(2,1)}, u32[]{:S(2)}, u32[]{:S(2)}) collective-permute-start(bf16[1024,256]{1,0:T(8,128)(2,1)} %after.31.p0), channel_id=1, source_target_pairs={{0,2},{2,0},{4,6},{6,4},{1,3},{3,1},{5,7},{7,5},{8,10},{10,8},{12,... | collective-permute-start | bytes 1572872 | tf_op jit(solution)/shard_map/ppermute | solution.py:49
  123.2 26.3 %collective-permute-start.17 = (bf16[1024,256]{1,0:T(8,128)(2,1)S(1)}, bf16[1024,256]{1,0:T(8,128)(2,1)}, u32[]{:S(2)}, u32[]{:S(2)}) collective-permute-start(bf16[1024,256]{1,0:T(8,128)(2,1)S(1)} %copy-done.2), channel_id=1, source_target_pairs={{0,2},{2,0},{4,6},{6,4},{1,3},{3,1},{5,7},{7,5},{8,10},{10,8},{12,... | collective-permute-start | bytes 1572872 | tf_op jit(solution)/shard_map/ppermute | solution.py:49
  127.6 65.8 %collective-permute-start.23 = (bf16[2,4,256,512]{3,2,1,0:T(8,128)(2,1)}, bf16[2,4,256,512]{3,2,1,0:T(8,128)(2,1)}, u32[]{:S(2)}, u32[]{:S(2)}) collective-permute-start(bf16[2,4,256,512]{3,2,1,0:T(8,128)(2,1)} %pad_maximum_fusion.refs_4_), channel_id=1, source_target_pairs={{0,1},{1,0},{2,3},{3,2},{4,5},{5,4},{6,7},{7,6},{8,9},{9,8},{10,11... | collective-permute-start | bytes 6291464 | tf_op jit(solution)/shard_map/ppermute | solution.py:49
  130.1 66.6 %collective-permute-start.22 = (bf16[2,4,256,512]{3,2,1,0:T(8,128)(2,1)}, bf16[2,4,256,512]{3,2,1,0:T(8,128)(2,1)}, u32[]{:S(2)}, u32[]{:S(2)}) collective-permute-start(bf16[2,4,256,512]{3,2,1,0:T(8,128)(2,1)} %pad_maximum_fusion.refs_4_), channel_id=1, source_target_pairs={{0,16},{8,24},{16,0},{24,8},{1,17},{9,25},{17,1},{25,9},{2,18},{10... | collective-permute-start | bytes 6291464 | tf_op jit(solution)/shard_map/ppermute | solution.py:49
  160.4 31.8 %collective-permute-start.19 = (bf16[512,256]{1,0:T(8,128)(2,1)}, bf16[512,256]{1,0:T(8,128)(2,1)S(1)}, u32[]{:S(2)}, u32[]{:S(2)}) collective-permute-start(bf16[512,256]{1,0:T(8,128)(2,1)} %after.33), channel_id=1, source_target_pairs={{0,2},{2,0},{4,6},{6,4},{1,3},{3,1},{5,7},{7,5},{8,10},{10,8},{12,... | collective-permute-start | bytes 786440 | tf_op jit(solution)/shard_map/ppermute | solution.py:49
  161.4 30.9 %collective-permute-start.20 = (bf16[512,256]{1,0:T(8,128)(2,1)S(1)}, bf16[512,256]{1,0:T(8,128)(2,1)S(1)}, u32[]{:S(2)}, u32[]{:S(2)}) collective-permute-start(bf16[512,256]{1,0:T(8,128)(2,1)S(1)} %copy-done.31), channel_id=1, source_target_pairs={{0,4},{2,6},{4,0},{6,2},{1,5},{3,7},{5,1},{7,3},{8,12},{10,14},{12... | collective-permute-start | bytes 786440 | tf_op jit(solution)/shard_map/ppermute | solution.py:49
  162.8 29.5 %collective-permute-start.21 = (bf16[512,256]{1,0:T(8,128)(2,1)S(1)}, bf16[512,256]{1,0:T(8,128)(2,1)S(1)}, u32[]{:S(2)}, u32[]{:S(2)}) collective-permute-start(bf16[512,256]{1,0:T(8,128)(2,1)S(1)} %copy-done.32), channel_id=1, source_target_pairs={{0,6},{2,4},{4,2},{6,0},{1,7},{3,5},{5,3},{7,1},{8,14},{10,12},{12... | collective-permute-start | bytes 786440 | tf_op jit(solution)/shard_map/ppermute | solution.py:49
  195.1 25.4 %collective-permute-start.27 = (bf16[4,256,512]{2,1,0:T(8,128)(2,1)S(1)}, bf16[4,256,512]{2,1,0:T(8,128)(2,1)}, u32[]{:S(2)}, u32[]{:S(2)}) collective-permute-start(bf16[4,256,512]{2,1,0:T(8,128)(2,1)S(1)} %slice_bitcast_fusion), channel_id=1, source_target_pairs={{0,16},{8,24},{16,0},{24,8},{1,17},{9,25},{17,1},{25,9},{2,18},{10... | collective-permute-start | bytes 3145736 | tf_op jit(solution)/shard_map/ppermute | solution.py:49
  266.8 27.4 %collective-permute-start.35 = (bf16[4,256,512]{2,1,0:T(8,128)(2,1)}, bf16[4,256,512]{2,1,0:T(8,128)(2,1)S(1)}, u32[]{:S(2)}, u32[]{:S(2)}) collective-permute-start(bf16[4,256,512]{2,1,0:T(8,128)(2,1)} %get-tuple-element.126), channel_id=1, source_target_pairs={{0,16},{8,24},{16,0},{24,8},{1,17},{9,25},{17,1},{25,9},{2,18},{10... | collective-permute-start | bytes 3145736 | tf_op jit(solution)/shard_map/ppermute | solution.py:49
  267.4 31.9 %collective-permute-start.34 = (bf16[4,256,512]{2,1,0:T(8,128)(2,1)}, bf16[4,256,512]{2,1,0:T(8,128)(2,1)S(1)}, u32[]{:S(2)}, u32[]{:S(2)}) collective-permute-start(bf16[4,256,512]{2,1,0:T(8,128)(2,1)} %get-tuple-element.124), channel_id=1, source_target_pairs={{0,1},{1,0},{2,3},{3,2},{4,5},{5,4},{6,7},{7,6},{8,9},{9,8},{10,11... | collective-permute-start | bytes 3145736 | tf_op jit(solution)/shard_map/ppermute | solution.py:49
  287.2 81.2 %collective-permute-start.37 = (bf16[2,4,2,32,1024]{4,3,2,1,0:T(8,128)(2,1)}, bf16[2,4,2,32,1024]{4,3,2,1,0:T(8,128)(2,1)}, u32[]{:S(2)}, u32[]{:S(2)}) collective-permute-start(bf16[2,4,2,32,1024]{4,3,2,1,0:T(8,128)(2,1)} %get-tuple-element.114.refs_0_), channel_id=1, source_target_pairs={{0,8},{8,0},{16,24},{24,16},{1,9},{9,1},{17,25},{25,17},{2,10},{10... | collective-permute-start | bytes 3145736 | tf_op jit(solution)/shard_map/ppermute | solution.py:49
  293.7 48.1 %collective-permute-start.32 = (bf16[512,256]{1,0:T(8,128)(2,1)}, bf16[512,256]{1,0:T(8,128)(2,1)}, u32[]{:S(2)}, u32[]{:S(2)}) collective-permute-start(bf16[512,256]{1,0:T(8,128)(2,1)} %after.38), channel_id=1, source_target_pairs={{0,4},{2,6},{4,0},{6,2},{1,5},{3,7},{5,1},{7,3},{8,12},{10,14},{12... | collective-permute-start | bytes 786440 | tf_op jit(solution)/shard_map/ppermute | solution.py:49
  294.3 47.6 %collective-permute-start.33 = (bf16[512,256]{1,0:T(8,128)(2,1)}, bf16[512,256]{1,0:T(8,128)(2,1)}, u32[]{:S(2)}, u32[]{:S(2)}) collective-permute-start(bf16[512,256]{1,0:T(8,128)(2,1)} %after.39), channel_id=1, source_target_pairs={{0,6},{2,4},{4,2},{6,0},{1,7},{3,5},{5,3},{7,1},{8,14},{10,12},{12... | collective-permute-start | bytes 786440 | tf_op jit(solution)/shard_map/ppermute | solution.py:49
  299.3 51.1 %collective-permute-start.39 = (bf16[2,4,256,512]{3,2,1,0:T(8,128)(2,1)}, bf16[2,4,256,512]{3,2,1,0:T(8,128)(2,1)S(1)}, u32[]{:S(2)}, u32[]{:S(2)}) collective-permute-start(bf16[2,4,256,512]{3,2,1,0:T(8,128)(2,1)} %fusion.5.refs_1_), channel_id=1, source_target_pairs={{0,1},{1,0},{2,3},{3,2},{4,5},{5,4},{6,7},{7,6},{8,9},{9,8},{10,11... | collective-permute-start | bytes 6291464 | tf_op jit(solution)/shard_map/ppermute | solution.py:49
  304.5 47.0 %collective-permute-start.38 = (bf16[2,4,256,512]{3,2,1,0:T(8,128)(2,1)}, bf16[2,4,256,512]{3,2,1,0:T(8,128)(2,1)}, u32[]{:S(2)}, u32[]{:S(2)}) collective-permute-start(bf16[2,4,256,512]{3,2,1,0:T(8,128)(2,1)} %fusion.3.refs_0_), channel_id=1, source_target_pairs={{0,16},{8,24},{16,0},{24,8},{1,17},{9,25},{17,1},{25,9},{2,18},{10... | collective-permute-start | bytes 6291464 | tf_op jit(solution)/shard_map/ppermute | solution.py:49
  350.3 29.3 %collective-permute-start.36 = (bf16[512,1024]{1,0:T(8,128)(2,1)}, bf16[512,1024]{1,0:T(8,128)(2,1)}, u32[]{:S(2)}, u32[]{:S(2)}) collective-permute-start(bf16[512,1024]{1,0:T(8,128)(2,1)} %get-tuple-element.129.refs_6_), channel_id=1, source_target_pairs={{0,2},{2,0},{4,6},{6,4},{1,3},{3,1},{5,7},{7,5},{8,10},{10,8},{12,... | collective-permute-start | bytes 3145736 | tf_op jit(solution)/shard_map/ppermute | solution.py:49
  355.8 49.0 %collective-permute-start.44 = (bf16[2,2,256,512]{3,2,1,0:T(8,128)(2,1)}, bf16[2,2,256,512]{3,2,1,0:T(8,128)(2,1)}, u32[]{:S(2)}, u32[]{:S(2)}) collective-permute-start(bf16[2,2,256,512]{3,2,1,0:T(8,128)(2,1)} %bitcast.176), channel_id=1, source_target_pairs={{0,2},{2,0},{4,6},{6,4},{1,3},{3,1},{5,7},{7,5},{8,10},{10,8},{12,... | collective-permute-start | bytes 3145736 | tf_op jit(solution)/shard_map/ppermute | solution.py:49
  372.8 34.5 %collective-permute-start.43 = (bf16[2,4,3,32,1024]{4,3,2,1,0:T(8,128)(2,1)S(1)}, bf16[2,4,3,32,1024]{4,3,2,1,0:T(8,128)(2,1)S(1)}, u32[]{:S(2)}, u32[]{:S(2)}) collective-permute-start(bf16[2,4,3,32,1024]{4,3,2,1,0:T(8,128)(2,1)S(1)} %copy-done.28), channel_id=1, source_target_pairs={{0,8},{8,0},{16,24},{24,16},{1,9},{9,1},{17,25},{25,17},{2,10},{10... | collective-permute-start | bytes 4718600 | tf_op jit(solution)/shard_map/ppermute | solution.py:49
  383.9 30.9 %collective-permute-start.40 = (bf16[512,256]{1,0:T(8,128)(2,1)}, bf16[512,256]{1,0:T(8,128)(2,1)}, u32[]{:S(2)}, u32[]{:S(2)}) collective-permute-start(bf16[512,256]{1,0:T(8,128)(2,1)} %get-tuple-element.140), channel_id=1, source_target_pairs={{0,2},{2,0},{4,6},{6,4},{1,3},{3,1},{5,7},{7,5},{8,10},{10,8},{12,... | collective-permute-start | bytes 786440 | tf_op jit(solution)/shard_map/ppermute | solution.py:49
  383.9 31.0 %collective-permute-start.41 = (bf16[512,256]{1,0:T(8,128)(2,1)}, bf16[512,256]{1,0:T(8,128)(2,1)}, u32[]{:S(2)}, u32[]{:S(2)}) collective-permute-start(bf16[512,256]{1,0:T(8,128)(2,1)} %get-tuple-element.141), channel_id=1, source_target_pairs={{0,4},{2,6},{4,0},{6,2},{1,5},{3,7},{5,1},{7,3},{8,12},{10,14},{12... | collective-permute-start | bytes 786440 | tf_op jit(solution)/shard_map/ppermute | solution.py:49
  386.4 29.9 %collective-permute-start.42 = (bf16[512,256]{1,0:T(8,128)(2,1)}, bf16[512,256]{1,0:T(8,128)(2,1)S(1)}, u32[]{:S(2)}, u32[]{:S(2)}) collective-permute-start(bf16[512,256]{1,0:T(8,128)(2,1)} %get-tuple-element.142), channel_id=1, source_target_pairs={{0,6},{2,4},{4,2},{6,0},{1,7},{3,5},{5,3},{7,1},{8,14},{10,12},{12... | collective-permute-start | bytes 786440 | tf_op jit(solution)/shard_map/ppermute | solution.py:49
  414.8 25.5 %collective-permute-start.53 = (bf16[2,256,512]{2,1,0:T(8,128)(2,1)}, bf16[2,256,512]{2,1,0:T(8,128)(2,1)S(1)}, u32[]{:S(2)}, u32[]{:S(2)}) collective-permute-start(bf16[2,256,512]{2,1,0:T(8,128)(2,1)} %get-tuple-element.147), channel_id=1, source_target_pairs={{0,4},{2,6},{4,0},{6,2},{1,5},{3,7},{5,1},{7,3},{8,12},{10,14},{12... | collective-permute-start | bytes 1572872 | tf_op jit(solution)/shard_map/ppermute | solution.py:49
  (90 other events, 701.3 us)

commit v4 on v3

--- a/solution.py
+++ b/solution.py
@@ -671,6 +671,7 @@
         in_specs=[rows, rows, rows, rows, whole((1, D))] + [ANY] * len(earlier),
         out_specs=[pl.BlockSpec((block, QUARTER), lambda i: (i, 0))] * 4,
         compiler_params=params(LIMIT),
+        cost_estimate=cost(20_000_000_000),
         name="input_grad",
     )(keep, got, raw, g_mid, gain, *earlier)
 
@@ -1008,22 +1009,22 @@
     d_input = to_owners(d_rows)
     if heads_part % 2 == 0:
         g_out, out_send = merge([halves(g_out[0]), halves(out_got[0])], d_rows[0])
-    even, even_send = merge([even, swap(odd, "row", 1)], out_send, axis=1, work=20_000_000_000)
+    g_qkv, qkv_send = merge([g_qkv[0], swap(g_qkv[1], "dp", 1)], out_send)
+    qkv_got = swap(qkv_send, "dp", 2)
+    even, even_send = merge([even, swap(odd, "row", 1)], qkv_send, axis=1)
     even_got = swap(even_send[:, 0], "row", 2)
-    g_qkv, qkv_send = merge([g_qkv[0], swap(g_qkv[1], "dp", 1)], even_send)
-    qkv_got = swap(qkv_send, "dp", 2)
     if heads_part % 2 == 0:
         def over_row(g, got, first, second):
             g, send = merge([g, got], first, lanes=True)
             g, last = merge([g, swap(send, "row", 2)], second, lanes=True)
             return g, swap(last, "row", 1), send
 
-        out_pair = over_row(g_out[0], swap(out_send[0], "col", 1), qkv_send, *d_input[3:])
         g_qkv, qkv_send = merge(
-            [halves(g_qkv[0]), halves(qkv_got[0])], out_pair[2], *d_input[1:]
+            [halves(g_qkv[0]), halves(qkv_got[0])], even_send, *d_input[1:]
         )
+        out_pair = over_row(g_out[0], swap(out_send[0], "col", 1), qkv_send, qkv_send)
         g_qkv, got, last = over_row(
-            g_qkv[0], swap(qkv_send[0], "col", 1), out_pair[0], out_pair[0]
+            g_qkv[0], swap(qkv_send[0], "col", 1), out_pair[2], out_pair[2]
         )
         grad_qkv = by_low(jnp.stack([g_qkv, got])).astype(F32)
         grad_qkv = grad_qkv.reshape(heads_part, 3, span, QUARTER)
@@ -1046,7 +1047,7 @@
     while distance < n_col:
         vectors = vectors + swap(vectors, "col", distance)
         distance *= 2
-    vectors = after(vectors, last, even_got)
+    vectors = after(vectors, g_qkv, even_got)
     vectors = vectors[:2] + swap(vectors[2:], "row", 2)
     vectors = vectors[0] + swap(vectors[1], "row", 1)
     grad_qkv = grad_qkv.transpose(3, 1, 0, 2)

time: 485 us -> 481 us (level)
    unnamed x132 -> x134, local copies, waits for them, and re-layouts: 18.1 us -> 19.1 us
  transfers between devices with their start and end apart: 59 -> 59, of which waited for: 25 -> 22; matrix products, arithmetic and copies ran while one was open for 11% -> 11% of each run, Pallas kernels for 34% -> 35%
where the time goes in v4:
time: 481 us; the launch traced here: 476 us
  Pallas kernels  208 us (43%)
  waiting for transfers between devices  129 us (27%)
  starting transfers between devices  62.3 us (13%)
  local copies, waits for them, and re-layouts  36.9 us (8%)
  other arithmetic  24.9 us (5%)
  matrix products  13.3 us (3%)
    ppermute x59, waiting for transfers between devices, swap(): return lax.ppermute(x, axis, [(i, i ^ distance) for i in range(n)])  129 us
    ppermute x59, starting transfers between devices, swap(): return lax.ppermute(x, axis, [(i, i ^ distance) for i in range(n)])  62.3 us
    pallas_call x1, Pallas kernels, feed_forward(): pl.pallas_call(ffn_kernel, out_shape=(shape((HALF, D), F32), shape((HALF,...  43.1 us
    pallas_call x1, Pallas kernels, attention_backward(): pl.pallas_call(backward_kernel, out_shape=(shape((SEQ_LEN, HEADS * 3 * DH...  37 us
    pallas_call x1, Pallas kernels, attention_forward(): pl.pallas_call(forward_kernel, out_shape=(shape((SEQ_LEN, HEADS * DH), BF...  25.3 us
    pallas_call x10, Pallas kernels, merge(): pl.pallas_call(functools.partial(merge_kernel, count, lanes), out_shape=(...  23.9 us
    unnamed x134, local copies, waits for them, and re-layouts  19.1 us
    dot_general x2, matrix products, nt(): lax.dot_general(a, b, (((1,), (1,)), ((), ())), preferred_element_type=F32)  13.3 us
  transfers between devices with their start and end apart: 59, of which 22 were waited for; matrix products, arithmetic and copies ran while one was open for 11% of the time, Pallas kernels for 35%

profile of v4, /device:TPU:0, one launch (start us, length us, event | category | flops | bytes accessed | tf_op | source)
XLA Modules:
  0.0 475.9 jit_solution(4593577109636981059)
XLA Ops:
  3.6 5.1 %collective-permute-start.7 = (bf16[2,5,32,256]{3,2,1,0:T(8,128)(2,1)}, bf16[2,5,32,256]{3,2,1,0:T(8,128)(2,1)}, u32[]{:S(2)}, u32[]{:S(2)}) collective-permute-start(bf16[2,5,32,256]{3,2,1,0:T(8,128)(2,1)} %get-tuple-element.223), channel_id=1, source_target_pairs={{0,6},{2,4},{4,2},{6,0},{1,7},{3,5},{5,3},{7,1},{8,14},{10,12},{12... | collective-permute-start | bytes 491528 | tf_op jit(solution)/shard_map/ppermute | solution.py:49
  14.8 20.3 %collective-permute-done.6 = bf16[2,5,32,256]{3,2,1,0:T(8,128)(2,1)} collective-permute-done((bf16[2,5,32,256]{3,2,1,0:T(8,128)(2,1)}, bf16[2,5,32,256]{3,2,1,0:T(8,128)(2,1)}, u32[]{:S(2)}, u32[]{:S(2)}) %collective-permute-start.6) | collective-permute-done | bytes 163872 | tf_op jit(solution)/shard_map/ppermute | solution.py:49
  37.1 4.9 %collective-permute-done.refs_1_.refs_2_.p1 = bf16[1024,256]{1,0:T(8,128)(2,1)S(1)} collective-permute-done((bf16[1024,256]{1,0:T(8,128)(2,1)S(1)}, bf16[1024,256]{1,0:T(8,128)(2,1)S(1)}, u32[]{:S(2)}, u32[]{:S(2)}) %collective-permute-start) | collective-permute-done | bytes 524320 | tf_op jit(solution)/shard_map/ppermute | solution.py:49
  49.2 9.5 %collective-permute-done.8 = bf16[1,4,2,5,32,256]{5,4,3,2,1,0:T(8,128)(2,1)S(1)} collective-permute-done((bf16[1,4,2,5,32,256]{5,4,3,2,1,0:T(8,128)(2,1)}, bf16[1,4,2,5,32,256]{5,4,3,2,1,0:T(8,128)(2,1)S(1)}, u32[]{:S(2)}, u32[]{:S(2)}) %collective-permute-start.8) | collective-permute-done | bytes 655392 | tf_op jit(solution)/shard_map/ppermute | solution.py:49
  59.8 9.2 %collective-permute-done.2.refs_2_.p3 = bf16[1024,256]{1,0:T(8,128)(2,1)S(1)} collective-permute-done((bf16[1024,256]{1,0:T(8,128)(2,1)}, bf16[1024,256]{1,0:T(8,128)(2,1)S(1)}, u32[]{:S(2)}, u32[]{:S(2)}) %collective-permute-start.2) | collective-permute-done | bytes 524320 | tf_op jit(solution)/shard_map/ppermute | solution.py:49
  81.0 3.1 collective-permute-start.10
  88.5 25.8 %collective-permute-done.4 = f32[2,5376]{1,0:T(2,128)} collective-permute-done((f32[2,5376]{1,0:T(2,128)S(1)}, f32[2,5376]{1,0:T(2,128)}, u32[]{:S(2)}, u32[]{:S(2)}) %collective-permute-start.4) | collective-permute-done | bytes 43040 | tf_op jit(solution)/shard_map/ppermute | solution.py:49
  130.6 5.8 %join_weights.1 = (bf16[1536,1024]{1,0:T(8,128)(2,1)}, bf16[1024,1024]{1,0:T(8,128)(2,1)}, bf16[1024,1024]{1,0:T(8,128)(2,1)}) custom-call(bf16[2,4,2,5,32,256]{5,4,3,2,1,0:T(8,128)(2,1)} %after.28.refs_0_, bf16[2,4,2,5,32,256]{5,4,3,2,1,0:T(8,128)(2,1)} %copy-done.4, bf16[2,4,2,5,32,256]{5,4,3,2,1,0:T(8,128)(2,1)} %after.30.refs_2_, ...), custom_call_target="tpu_custom_call" | custom-call | tf_op jit(solution)/shard_map/join_weights/pallas_call | solution.py:175
  136.4 5.3 %tok_norm.1 = (bf16[1024,1024]{1,0:T(8,128)(2,1)}, bf16[1024,1024]{1,0:T(8,128)(2,1)}) custom-call(s32[1]{0:T(128)} %bitcast.where, bf16[1024,256]{1,0:T(8,128)(2,1)} %copy-done.23, bf16[1024,256]{1,0:T(8,128)(2,1)} %copy-done.5, bf16[1024,256]{1,0:T(8,128)(2,1)} %copy-done.24, bf16[1024,256]{1,0:T(8,128)(2,1)} %copy-done.6, f32[1,1024]{1,0:T(1,128)} %after.29.gain_ref), custom_call_target="tpu_custom_call" | custom-call | tf_op jit(solution)/shard_map/tok_norm/pallas_call | solution.py:104
  141.8 7.7 %convolution_convert_fusion.1._.tok_ref.refs_2_ = bf16[1024,1536]{1,0:T(8,128)(2,1)} fusion(bf16[1024,1024]{1,0:T(8,128)(2,1)} %get-tuple-element.100.xt_ref, bf16[1536,1024]{1,0:T(8,128)(2,1)} %get-tuple-element.101.w_ref), kind=kOutput, calls=%fused_computation.1 | convolution fusion | flops 3222798336 | bytes 8388608 | tf_op jit(solution)/shard_map/dot_general | solution.py:40
  149.5 5.3 %mem_norm.1 = (bf16[1152,1024]{1,0:T(8,128)(2,1)}, bf16[1024,1024]{1,0:T(8,128)(2,1)}) custom-call(bf16[1024,256]{1,0:T(8,128)(2,1)} %after.31.p0, bf16[1024,256]{1,0:T(8,128)(2,1)} %collective-permute-done.16.p1, bf16[1024,256]{1,0:T(8,128)(2,1)} %copy-done.1, bf16[1024,256]{1,0:T(8,128)(2,1)} %collective-permute-done.17.p3, f32[1,1024]{1,0:T(1,128)} %bitcast.221, ...), custom_call_target="tpu_custom_call" | custom-call | tf_op jit(solution)/shard_map/mem_norm/pallas_call | solution.py:140
  154.7 5.7 %convolution_convert_fusion.mem_ref.refs_1_ = bf16[1152,1024]{1,0:T(8,128)(2,1)} fusion(bf16[1152,1024]{1,0:T(8,128)(2,1)} %get-tuple-element.102.xm_ref, bf16[1024,1024]{1,0:T(8,128)(2,1)S(1)} %copy-done.22), kind=kOutput, calls=%fused_computation | convolution fusion | flops 2417098752 | bytes 6815744 | tf_op jit(solution)/shard_map/dot_general | solution.py:40
  164.9 25.3 %attention_forward.1 = (bf16[1024,512]{1,0:T(8,128)(2,1)}, f32[4,1,1024]{2,1,0:T(1,128)}) custom-call(bf16[1024,1536]{1,0:T(8,128)(2,1)} %convolution_convert_fusion.1._.tok_ref.refs_2_, bf16[1152,1024]{1,0:T(8,128)(2,1)} %convolution_convert_fusion.mem_ref.refs_1_, f32[2,1024]{1,0:T(2,128)} %stack.93.row_ref, f32[1024,3]{1,0:T(8,128)} %copy.85.col_ref), custom_call_target="tpu_custom_call" | custom-call | flops 24999999488 | bytes 25000000 | tf_op jit(solution)/shard_map/attention_forward/pallas_call | solution.py:252
  198.0 11.9 %reconstruction.1 = (f32[4,128,1024]{2,1,0:T(8,128)}, f32[640,1024]{1,0:T(8,128)}) custom-call(bf16[1024,1536]{1,0:T(8,128)(2,1)} %convolution_convert_fusion.1._.tok_ref.refs_2_, bf16[1152,1024]{1,0:T(8,128)(2,1)} %convolution_convert_fusion.mem_ref.refs_1_, bf16[512,1024]{1,0:T(8,128)(2,1)} %copy-done.20, ...), custom_call_target="tpu_custom_call" | custom-call | flops 10000000000 | bytes 10000000 | tf_op jit(solution)/shard_map/reconstruction/pallas_call | solution.py:306
  210.8 5.1 %residual_mid.1 = (f32[512,1024]{1,0:T(8,128)}, bf16[512,1024]{1,0:T(8,128)(2,1)}) custom-call(bf16[1024,1024]{1,0:T(8,128)(2,1)} %get-tuple-element.99.raw_ref, bf16[1024,512]{1,0:T(8,128)(2,1)} %get-tuple-element.104.own_ref.o_ref, bf16[512,512]{1,0:T(8,128)(2,1)} %copy-done.27, bf16[1024,1024]{1,0:T(8,128)(2,1)} %get-tuple-element.105.w_ref, ...), custom_call_target="tpu_custom_call" | custom-call | flops 2147483648 | bytes 2147483 | tf_op jit(solution)/shard_map/residual_mid/pallas_call | solution.py:439
  215.9 4.5 collective-permute-done.27.refs_8_
  223.1 43.1 %feed_forward.1 = (f32[512,1024]{1,0:T(8,128)}, bf16[512,1024]{1,0:T(8,128)(2,1)}, f32[512,1024]{1,0:T(8,128)}, bf16[512,1024]{1,0:T(8,128)(2,1)}, bf16[2,4,256,...) custom-call(bf16[512,1024]{1,0:T(8,128)(2,1)} %get-tuple-element.108, ...), custom_call_target="tpu_custom_call" | custom-call | flops 25769803776 | bytes 25769804 | tf_op jit(solution)/shard_map/feed_forward/pallas_call | solution.py:538
  270.1 6.5 %mid_back.1 = (f32[512,1024]{1,0:T(8,128)}, bf16[512,1024]{1,0:T(8,128)(2,1)}, bf16[512,512]{1,0:T(8,128)(2,1)}, bf16[512,512]{1,0:T(8,128)(2,1)}, f32[1,1024]{1,0:T(1,128)}) custom-call(f32[512,1024]{1,0:T(8,128)} %get-tuple-element.111.gx_ref, bf16[512,1024]{1,0:T(8,128)(2,1)} %copy-done.37, f32[512,1024]{1,0:T(8,128)} %get-tuple-element.107.mid_ref, ...), custom_call_target="tpu_custom_call" | custom-call | flops 1073741824 | bytes 1073741 | tf_op jit(solution)/shard_map/mid_back/pallas_call | solution.py:600
  282.2 4.9 %out_grad.1 = (bf16[2,4,2,32,1024]{4,3,2,1,0:T(8,128)(2,1)}, bf16[2,4,2,32,1024]{4,3,2,1,0:T(8,128)(2,1)}) custom-call(bf16[1024,512]{1,0:T(8,128)(2,1)} %get-tuple-element.104.own_ref.o_ref, bf16[512,512]{1,0:T(8,128)(2,1)} %copy-done.27, bf16[512,1024]{1,0:T(8,128)(2,1)} %get-tuple-element.113.g_ref), custom_call_target="tpu_custom_call" | custom-call | tf_op jit(solution)/shard_map/out_grad/pallas_call | solution.py:762
  287.1 3.4 out_sum.1
  304.9 37.0 %attention_backward.1 = (bf16[1024,1536]{1,0:T(8,128)(2,1)}, bf16[1152,1024]{1,0:T(8,128)(2,1)}) custom-call(bf16[1024,1536]{1,0:T(8,128)(2,1)} %convolution_convert_fusion.1._.tok_ref.refs_2_, bf16[1152,1024]{1,0:T(8,128)(2,1)} %convolution_convert_fusion.mem_ref.refs_1_, bf16[512,512]{1,0:T(8,128)(2,1)} %get-tuple-element.120.own_ref, ...), custom_call_target="tpu_custom_call" | custom-call | flops 35000000512 | bytes 35000000 | tf_op jit(solution)/shard_map/attention_backward/pallas_call | solution.py:386
  342.0 8.4 %tok_grad.1 = (f32[512,1024]{1,0:T(8,128)}, bf16[512,1024]{1,0:T(8,128)(2,1)}, f32[1,1024]{1,0:T(1,128)}) custom-call(bf16[1024,1536]{1,0:T(8,128)(2,1)} %get-tuple-element.127.g_ref.gt_ref, bf16[1536,1024]{1,0:T(8,128)(2,1)} %get-tuple-element.101.w_ref, bf16[1024,1024]{1,0:T(8,128)(2,1)} %get-tuple-element.99.raw_ref, bf16[512,256]{1,0:T(8,128)(2,1)} %copy-done.28, ...), custom_call_target="tpu_custom_call" | custom-call | tf_op jit(solution)/shard_map/tok_grad/pallas_call | solution.py:637
  351.8 4.1 merge.10
  357.8 10.6 %qkv_grad.1 = (bf16[2,4,3,32,1024]{4,3,2,1,0:T(8,128)(2,1)}, bf16[2,4,3,32,1024]{4,3,2,1,0:T(8,128)(2,1)}) custom-call(bf16[1024,1536]{1,0:T(8,128)(2,1)} %get-tuple-element.127.g_ref.gt_ref, bf16[1024,1024]{1,0:T(8,128)(2,1)} %get-tuple-element.100.xt_ref, bf16[1152,1024]{1,0:T(8,128)(2,1)} %get-tuple-element.131.gm_ref.g_ref, ...), custom_call_target="tpu_custom_call" | custom-call | tf_op jit(solution)/shard_map/qkv_grad/pallas_call | solution.py:736
  372.7 6.8 %mem_grad.1 = (f32[1,1024]{1,0:T(1,128)}, f32[3,1024]{1,0:T(4,128)}) custom-call(bf16[1152,1024]{1,0:T(8,128)(2,1)} %get-tuple-element.131.gm_ref.g_ref, bf16[1024,1024]{1,0:T(8,128)(2,1)} %get-tuple-element.103.w_ref, bf16[1024,1024]{1,0:T(8,128)(2,1)} %get-tuple-element.132.raw_ref, f32[1,1024]{1,0:T(1,128)} %bitcast.222, f32[3,1024]{1,0:T(4,128)} %bitcast.212, ...), custom_call_target="tpu_custom_call" | custom-call | tf_op jit(solution)/shard_map/mem_grad/pallas_call | solution.py:702
  379.4 4.3 input_grad.1
  391.4 3.2 merge.13
  396.2 8.5 %collective-permute-done.46 = bf16[2,2,256,512]{3,2,1,0:T(8,128)(2,1)S(1)} collective-permute-done((bf16[2,2,256,512]{3,2,1,0:T(8,128)(2,1)}, bf16[2,2,256,512]{3,2,1,0:T(8,128)(2,1)S(1)}, u32[]{:S(2)}, u32[]{:S(2)}) %collective-permute-start.46) | collective-permute-done | bytes 1048608 | tf_op jit(solution)/shard_map/ppermute | solution.py:49
  409.0 7.5 %collective-permute-done.42.refs_7_ = bf16[512,256]{1,0:T(8,128)(2,1)S(1)} collective-permute-done((bf16[512,256]{1,0:T(8,128)(2,1)}, bf16[512,256]{1,0:T(8,128)(2,1)S(1)}, u32[]{:S(2)}, u32[]{:S(2)}) %collective-permute-start.42) | collective-permute-done | bytes 262176 | tf_op jit(solution)/shard_map/ppermute | solution.py:49
  429.0 11.1 %collective-permute-done.53.refs_2_ = bf16[2,256,512]{2,1,0:T(8,128)(2,1)S(1)} collective-permute-done((bf16[2,256,512]{2,1,0:T(8,128)(2,1)}, bf16[2,256,512]{2,1,0:T(8,128)(2,1)S(1)}, u32[]{:S(2)}, u32[]{:S(2)}) %collective-permute-start.53) | collective-permute-done | bytes 524320 | tf_op jit(solution)/shard_map/ppermute | solution.py:49
  452.0 8.0 %collective-permute-done.49 = bf16[2,3,32,512]{3,2,1,0:T(8,128)(2,1)S(1)} collective-permute-done((bf16[2,3,32,512]{3,2,1,0:T(8,128)(2,1)}, bf16[2,3,32,512]{3,2,1,0:T(8,128)(2,1)S(1)}, u32[]{:S(2)}, u32[]{:S(2)}) %collective-permute-start.49) | collective-permute-done | bytes 196640 | tf_op jit(solution)/shard_map/ppermute | solution.py:49
  463.1 4.6 collective-permute-done.57
  (343 shorter events, 147.6 us)
Async XLA Ops:
  3.6 31.5 %collective-permute-start.7 = (bf16[2,5,32,256]{3,2,1,0:T(8,128)(2,1)}, bf16[2,5,32,256]{3,2,1,0:T(8,128)(2,1)}, u32[]{:S(2)}, u32[]{:S(2)}) collective-permute-start(bf16[2,5,32,256]{3,2,1,0:T(8,128)(2,1)} %get-tuple-element.223), channel_id=1, source_target_pairs={{0,6},{2,4},{4,2},{6,0},{1,7},{3,5},{5,3},{7,1},{8,14},{10,12},{12... | collective-permute-start | bytes 491528 | tf_op jit(solution)/shard_map/ppermute | solution.py:49
  8.7 26.4 %collective-permute-start.5 = (bf16[2,5,32,256]{3,2,1,0:T(8,128)(2,1)}, bf16[2,5,32,256]{3,2,1,0:T(8,128)(2,1)}, u32[]{:S(2)}, u32[]{:S(2)}) collective-permute-start(bf16[2,5,32,256]{3,2,1,0:T(8,128)(2,1)} %get-tuple-element.223), channel_id=1, source_target_pairs={{0,2},{2,0},{4,6},{6,4},{1,3},{3,1},{5,7},{7,5},{8,10},{10,8},{12,... | collective-permute-start | bytes 491528 | tf_op jit(solution)/shard_map/ppermute | solution.py:49
  8.7 26.4 %collective-permute-start.6 = (bf16[2,5,32,256]{3,2,1,0:T(8,128)(2,1)}, bf16[2,5,32,256]{3,2,1,0:T(8,128)(2,1)}, u32[]{:S(2)}, u32[]{:S(2)}) collective-permute-start(bf16[2,5,32,256]{3,2,1,0:T(8,128)(2,1)} %get-tuple-element.222), channel_id=1, source_target_pairs={{0,4},{2,6},{4,0},{6,2},{1,5},{3,7},{5,1},{7,3},{8,12},{10,14},{12... | collective-permute-start | bytes 491528 | tf_op jit(solution)/shard_map/ppermute | solution.py:49
  10.2 35.1 %collective-permute-start.1 = (bf16[1024,256]{1,0:T(8,128)(2,1)}, bf16[1024,256]{1,0:T(8,128)(2,1)S(1)}, u32[]{:S(2)}, u32[]{:S(2)}) collective-permute-start(bf16[1024,256]{1,0:T(8,128)(2,1)} %get-tuple-element.217), channel_id=1, source_target_pairs={{0,4},{2,6},{4,0},{6,2},{1,5},{3,7},{5,1},{7,3},{8,12},{10,14},{12... | collective-permute-start | bytes 1572872 | tf_op jit(solution)/shard_map/ppermute | solution.py:49
  12.5 29.5 %collective-permute-start = (bf16[1024,256]{1,0:T(8,128)(2,1)S(1)}, bf16[1024,256]{1,0:T(8,128)(2,1)S(1)}, u32[]{:S(2)}, u32[]{:S(2)}) collective-permute-start(bf16[1024,256]{1,0:T(8,128)(2,1)S(1)} %get-tuple-element.218.p0), channel_id=1, source_target_pairs={{0,2},{2,0},{4,6},{6,4},{1,3},{3,1},{5,7},{7,5},{8,10},{10,8},{12,... | collective-permute-start | bytes 1572872 | tf_op jit(solution)/shard_map/ppermute | solution.py:49
  46.1 25.4 %collective-permute-start.9 = (bf16[2,256,512]{2,1,0:T(8,128)(2,1)}, bf16[2,256,512]{2,1,0:T(8,128)(2,1)S(1)}, u32[]{:S(2)}, u32[]{:S(2)}) collective-permute-start(bf16[2,256,512]{2,1,0:T(8,128)(2,1)} %after.24.refs_0_), channel_id=1, source_target_pairs={{0,4},{2,6},{4,0},{6,2},{1,5},{3,7},{5,1},{7,3},{8,12},{10,14},{12... | collective-permute-start | bytes 1572872 | tf_op jit(solution)/shard_map/ppermute | solution.py:49
  72.3 42.8 %collective-permute-start.14 = (bf16[2,4,2,5,32,256]{5,4,3,2,1,0:T(8,128)(2,1)}, bf16[2,4,2,5,32,256]{5,4,3,2,1,0:T(8,128)(2,1)S(1)}, u32[]{:S(2)}, u32[]{:S(2)}) collective-permute-start(bf16[2,4,2,5,32,256]{5,4,3,2,1,0:T(8,128)(2,1)} %after.25.refs_0_), channel_id=1, source_target_pairs={{0,16},{8,24},{16,0},{24,8},{1,17},{9,25},{17,1},{25,9},{2,18},{10... | collective-permute-start | bytes 3932168 | tf_op jit(solution)/shard_map/ppermute | solution.py:49
  79.4 35.7 %collective-permute-start.11 = (bf16[2,256,512]{2,1,0:T(8,128)(2,1)}, bf16[2,256,512]{2,1,0:T(8,128)(2,1)S(1)}, u32[]{:S(2)}, u32[]{:S(2)}) collective-permute-start(bf16[2,256,512]{2,1,0:T(8,128)(2,1)} %after.27), channel_id=1, source_target_pairs={{0,2},{2,0},{4,6},{6,4},{1,3},{3,1},{5,7},{7,5},{8,10},{10,8},{12,... | collective-permute-start | bytes 1572872 | tf_op jit(solution)/shard_map/ppermute | solution.py:49
  81.0 34.1 %collective-permute-start.10 = (bf16[1024,256]{1,0:T(8,128)(2,1)}, bf16[1024,256]{1,0:T(8,128)(2,1)S(1)}, u32[]{:S(2)}, u32[]{:S(2)}) collective-permute-start(bf16[1024,256]{1,0:T(8,128)(2,1)} %after.26), channel_id=1, source_target_pairs={{0,4},{2,6},{4,0},{6,2},{1,5},{3,7},{5,1},{7,3},{8,12},{10,14},{12... | collective-permute-start | bytes 1572872 | tf_op jit(solution)/shard_map/ppermute | solution.py:49
  84.1 31.0 %collective-permute-start.12 = (bf16[2,256,512]{2,1,0:T(8,128)(2,1)S(1)}, bf16[2,256,512]{2,1,0:T(8,128)(2,1)S(1)}, u32[]{:S(2)}, u32[]{:S(2)}) collective-permute-start(bf16[2,256,512]{2,1,0:T(8,128)(2,1)S(1)} %copy-done.9), channel_id=1, source_target_pairs={{0,2},{2,0},{4,6},{6,4},{1,3},{3,1},{5,7},{7,5},{8,10},{10,8},{12,... | collective-permute-start | bytes 1572872 | tf_op jit(solution)/shard_map/ppermute | solution.py:49
  84.5 29.7 %collective-permute-start.4 = (f32[2,5376]{1,0:T(2,128)S(1)}, f32[2,5376]{1,0:T(2,128)}, u32[]{:S(2)}, u32[]{:S(2)}) collective-permute-start(f32[2,5376]{1,0:T(2,128)S(1)} %get-tuple-element.227), channel_id=1, source_target_pairs={{0,2},{2,0},{4,6},{6,4},{1,3},{3,1},{5,7},{7,5},{8,10},{10,8},{12,... | collective-permute-start | bytes 129032 | tf_op jit(solution)/shard_map/ppermute | solution.py:49
  121.9 27.6 %collective-permute-start.16 = (bf16[1024,256]{1,0:T(8,128)(2,1)}, bf16[1024,256]{1,0:T(8,128)(2,1)}, u32[]{:S(2)}, u32[]{:S(2)}) collective-permute-start(bf16[1024,256]{1,0:T(8,128)(2,1)} %after.31.p0), channel_id=1, source_target_pairs={{0,2},{2,0},{4,6},{6,4},{1,3},{3,1},{5,7},{7,5},{8,10},{10,8},{12,... | collective-permute-start | bytes 1572872 | tf_op jit(solution)/shard_map/ppermute | solution.py:49
  123.2 26.2 %collective-permute-start.17 = (bf16[1024,256]{1,0:T(8,128)(2,1)S(1)}, bf16[1024,256]{1,0:T(8,128)(2,1)}, u32[]{:S(2)}, u32[]{:S(2)}) collective-permute-start(bf16[1024,256]{1,0:T(8,128)(2,1)S(1)} %copy-done.2), channel_id=1, source_target_pairs={{0,2},{2,0},{4,6},{6,4},{1,3},{3,1},{5,7},{7,5},{8,10},{10,8},{12,... | collective-permute-start | bytes 1572872 | tf_op jit(solution)/shard_map/ppermute | solution.py:49
  127.6 65.9 %collective-permute-start.23 = (bf16[2,4,256,512]{3,2,1,0:T(8,128)(2,1)}, bf16[2,4,256,512]{3,2,1,0:T(8,128)(2,1)}, u32[]{:S(2)}, u32[]{:S(2)}) collective-permute-start(bf16[2,4,256,512]{3,2,1,0:T(8,128)(2,1)} %pad_maximum_fusion.refs_4_), channel_id=1, source_target_pairs={{0,1},{1,0},{2,3},{3,2},{4,5},{5,4},{6,7},{7,6},{8,9},{9,8},{10,11... | collective-permute-start | bytes 6291464 | tf_op jit(solution)/shard_map/ppermute | solution.py:49
  130.0 66.6 %collective-permute-start.22 = (bf16[2,4,256,512]{3,2,1,0:T(8,128)(2,1)}, bf16[2,4,256,512]{3,2,1,0:T(8,128)(2,1)}, u32[]{:S(2)}, u32[]{:S(2)}) collective-permute-start(bf16[2,4,256,512]{3,2,1,0:T(8,128)(2,1)} %pad_maximum_fusion.refs_4_), channel_id=1, source_target_pairs={{0,16},{8,24},{16,0},{24,8},{1,17},{9,25},{17,1},{25,9},{2,18},{10... | collective-permute-start | bytes 6291464 | tf_op jit(solution)/shard_map/ppermute | solution.py:49
  160.4 31.8 %collective-permute-start.19 = (bf16[512,256]{1,0:T(8,128)(2,1)}, bf16[512,256]{1,0:T(8,128)(2,1)S(1)}, u32[]{:S(2)}, u32[]{:S(2)}) collective-permute-start(bf16[512,256]{1,0:T(8,128)(2,1)} %after.33), channel_id=1, source_target_pairs={{0,2},{2,0},{4,6},{6,4},{1,3},{3,1},{5,7},{7,5},{8,10},{10,8},{12,... | collective-permute-start | bytes 786440 | tf_op jit(solution)/shard_map/ppermute | solution.py:49
  161.3 30.9 %collective-permute-start.20 = (bf16[512,256]{1,0:T(8,128)(2,1)S(1)}, bf16[512,256]{1,0:T(8,128)(2,1)S(1)}, u32[]{:S(2)}, u32[]{:S(2)}) collective-permute-start(bf16[512,256]{1,0:T(8,128)(2,1)S(1)} %copy-done.30), channel_id=1, source_target_pairs={{0,4},{2,6},{4,0},{6,2},{1,5},{3,7},{5,1},{7,3},{8,12},{10,14},{12... | collective-permute-start | bytes 786440 | tf_op jit(solution)/shard_map/ppermute | solution.py:49
  162.8 29.4 %collective-permute-start.21 = (bf16[512,256]{1,0:T(8,128)(2,1)S(1)}, bf16[512,256]{1,0:T(8,128)(2,1)S(1)}, u32[]{:S(2)}, u32[]{:S(2)}) collective-permute-start(bf16[512,256]{1,0:T(8,128)(2,1)S(1)} %copy-done.31), channel_id=1, source_target_pairs={{0,6},{2,4},{4,2},{6,0},{1,7},{3,5},{5,3},{7,1},{8,14},{10,12},{12... | collective-permute-start | bytes 786440 | tf_op jit(solution)/shard_map/ppermute | solution.py:49
  195.0 25.4 %collective-permute-start.27 = (bf16[4,256,512]{2,1,0:T(8,128)(2,1)S(1)}, bf16[4,256,512]{2,1,0:T(8,128)(2,1)}, u32[]{:S(2)}, u32[]{:S(2)}) collective-permute-start(bf16[4,256,512]{2,1,0:T(8,128)(2,1)S(1)} %slice_bitcast_fusion), channel_id=1, source_target_pairs={{0,16},{8,24},{16,0},{24,8},{1,17},{9,25},{17,1},{25,9},{2,18},{10... | collective-permute-start | bytes 3145736 | tf_op jit(solution)/shard_map/ppermute | solution.py:49
  197.9 25.1 %collective-permute-start.26 = (bf16[4,256,512]{2,1,0:T(8,128)(2,1)S(1)}, bf16[4,256,512]{2,1,0:T(8,128)(2,1)}, u32[]{:S(2)}, u32[]{:S(2)}) collective-permute-start(bf16[4,256,512]{2,1,0:T(8,128)(2,1)S(1)} %slice_bitcast_fusion.1), channel_id=1, source_target_pairs={{0,1},{1,0},{2,3},{3,2},{4,5},{5,4},{6,7},{7,6},{8,9},{9,8},{10,11... | collective-permute-start | bytes 3145736 | tf_op jit(solution)/shard_map/ppermute | solution.py:49
  266.8 27.6 %collective-permute-start.35 = (bf16[4,256,512]{2,1,0:T(8,128)(2,1)}, bf16[4,256,512]{2,1,0:T(8,128)(2,1)S(1)}, u32[]{:S(2)}, u32[]{:S(2)}) collective-permute-start(bf16[4,256,512]{2,1,0:T(8,128)(2,1)} %get-tuple-element.126), channel_id=1, source_target_pairs={{0,16},{8,24},{16,0},{24,8},{1,17},{9,25},{17,1},{25,9},{2,18},{10... | collective-permute-start | bytes 3145736 | tf_op jit(solution)/shard_map/ppermute | solution.py:49
  267.4 31.9 %collective-permute-start.34 = (bf16[4,256,512]{2,1,0:T(8,128)(2,1)}, bf16[4,256,512]{2,1,0:T(8,128)(2,1)S(1)}, u32[]{:S(2)}, u32[]{:S(2)}) collective-permute-start(bf16[4,256,512]{2,1,0:T(8,128)(2,1)} %get-tuple-element.124), channel_id=1, source_target_pairs={{0,1},{1,0},{2,3},{3,2},{4,5},{5,4},{6,7},{7,6},{8,9},{9,8},{10,11... | collective-permute-start | bytes 3145736 | tf_op jit(solution)/shard_map/ppermute | solution.py:49
  287.1 81.3 %collective-permute-start.37 = (bf16[2,4,2,32,1024]{4,3,2,1,0:T(8,128)(2,1)}, bf16[2,4,2,32,1024]{4,3,2,1,0:T(8,128)(2,1)}, u32[]{:S(2)}, u32[]{:S(2)}) collective-permute-start(bf16[2,4,2,32,1024]{4,3,2,1,0:T(8,128)(2,1)} %get-tuple-element.114.refs_0_), channel_id=1, source_target_pairs={{0,8},{8,0},{16,24},{24,16},{1,9},{9,1},{17,25},{25,17},{2,10},{10... | collective-permute-start | bytes 3145736 | tf_op jit(solution)/shard_map/ppermute | solution.py:49
  293.7 48.2 %collective-permute-start.32 = (bf16[512,256]{1,0:T(8,128)(2,1)}, bf16[512,256]{1,0:T(8,128)(2,1)}, u32[]{:S(2)}, u32[]{:S(2)}) collective-permute-start(bf16[512,256]{1,0:T(8,128)(2,1)} %after.38), channel_id=1, source_target_pairs={{0,4},{2,6},{4,0},{6,2},{1,5},{3,7},{5,1},{7,3},{8,12},{10,14},{12... | collective-permute-start | bytes 786440 | tf_op jit(solution)/shard_map/ppermute | solution.py:49
  294.3 47.6 %collective-permute-start.33 = (bf16[512,256]{1,0:T(8,128)(2,1)}, bf16[512,256]{1,0:T(8,128)(2,1)}, u32[]{:S(2)}, u32[]{:S(2)}) collective-permute-start(bf16[512,256]{1,0:T(8,128)(2,1)} %after.39), channel_id=1, source_target_pairs={{0,6},{2,4},{4,2},{6,0},{1,7},{3,5},{5,3},{7,1},{8,14},{10,12},{12... | collective-permute-start | bytes 786440 | tf_op jit(solution)/shard_map/ppermute | solution.py:49
  299.2 51.2 %collective-permute-start.39 = (bf16[2,4,256,512]{3,2,1,0:T(8,128)(2,1)}, bf16[2,4,256,512]{3,2,1,0:T(8,128)(2,1)S(1)}, u32[]{:S(2)}, u32[]{:S(2)}) collective-permute-start(bf16[2,4,256,512]{3,2,1,0:T(8,128)(2,1)} %fusion.5.refs_1_), channel_id=1, source_target_pairs={{0,1},{1,0},{2,3},{3,2},{4,5},{5,4},{6,7},{7,6},{8,9},{9,8},{10,11... | collective-permute-start | bytes 6291464 | tf_op jit(solution)/shard_map/ppermute | solution.py:49
  304.5 46.9 %collective-permute-start.38 = (bf16[2,4,256,512]{3,2,1,0:T(8,128)(2,1)}, bf16[2,4,256,512]{3,2,1,0:T(8,128)(2,1)}, u32[]{:S(2)}, u32[]{:S(2)}) collective-permute-start(bf16[2,4,256,512]{3,2,1,0:T(8,128)(2,1)} %fusion.3.refs_0_), channel_id=1, source_target_pairs={{0,16},{8,24},{16,0},{24,8},{1,17},{9,25},{17,1},{25,9},{2,18},{10... | collective-permute-start | bytes 6291464 | tf_op jit(solution)/shard_map/ppermute | solution.py:49
  350.4 29.1 %collective-permute-start.36 = (bf16[512,1024]{1,0:T(8,128)(2,1)}, bf16[512,1024]{1,0:T(8,128)(2,1)}, u32[]{:S(2)}, u32[]{:S(2)}) collective-permute-start(bf16[512,1024]{1,0:T(8,128)(2,1)} %get-tuple-element.129.refs_6_), channel_id=1, source_target_pairs={{0,2},{2,0},{4,6},{6,4},{1,3},{3,1},{5,7},{7,5},{8,10},{10,8},{12,... | collective-permute-start | bytes 3145736 | tf_op jit(solution)/shard_map/ppermute | solution.py:49
  355.8 48.9 %collective-permute-start.46 = (bf16[2,2,256,512]{3,2,1,0:T(8,128)(2,1)}, bf16[2,2,256,512]{3,2,1,0:T(8,128)(2,1)S(1)}, u32[]{:S(2)}, u32[]{:S(2)}) collective-permute-start(bf16[2,2,256,512]{3,2,1,0:T(8,128)(2,1)} %bitcast.188), channel_id=1, source_target_pairs={{0,2},{2,0},{4,6},{6,4},{1,3},{3,1},{5,7},{7,5},{8,10},{10,8},{12,... | collective-permute-start | bytes 3145736 | tf_op jit(solution)/shard_map/ppermute | solution.py:49
  383.8 25.2 %collective-permute-start.40 = (bf16[512,256]{1,0:T(8,128)(2,1)}, bf16[512,256]{1,0:T(8,128)(2,1)S(1)}, u32[]{:S(2)}, u32[]{:S(2)}) collective-permute-start(bf16[512,256]{1,0:T(8,128)(2,1)} %get-tuple-element.140), channel_id=1, source_target_pairs={{0,2},{2,0},{4,6},{6,4},{1,3},{3,1},{5,7},{7,5},{8,10},{10,8},{12,... | collective-permute-start | bytes 786440 | tf_op jit(solution)/shard_map/ppermute | solution.py:49
  386.3 30.1 %collective-permute-start.42 = (bf16[512,256]{1,0:T(8,128)(2,1)}, bf16[512,256]{1,0:T(8,128)(2,1)S(1)}, u32[]{:S(2)}, u32[]{:S(2)}) collective-permute-start(bf16[512,256]{1,0:T(8,128)(2,1)} %get-tuple-element.142), channel_id=1, source_target_pairs={{0,6},{2,4},{4,2},{6,0},{1,7},{3,5},{5,3},{7,1},{8,14},{10,12},{12... | collective-permute-start | bytes 786440 | tf_op jit(solution)/shard_map/ppermute | solution.py:49
  408.3 31.9 %collective-permute-start.53 = (bf16[2,256,512]{2,1,0:T(8,128)(2,1)}, bf16[2,256,512]{2,1,0:T(8,128)(2,1)S(1)}, u32[]{:S(2)}, u32[]{:S(2)}) collective-permute-start(bf16[2,256,512]{2,1,0:T(8,128)(2,1)} %get-tuple-element.149), channel_id=1, source_target_pairs={{0,4},{2,6},{4,0},{6,2},{1,5},{3,7},{5,1},{7,3},{8,12},{10,14},{12... | collective-permute-start | bytes 1572872 | tf_op jit(solution)/shard_map/ppermute | solution.py:49
  (91 other events, 772.8 us)

commit v5 on v4

--- a/solution.py
+++ b/solution.py
@@ -97,7 +97,7 @@
 
 
 def tok_norm(where, pieces, gain):
-    block = 256
+    block = 128
     count = SEQ_LEN // block
     piece = pl.BlockSpec((block, QUARTER), lambda i, w: ((i + w[0] * (count // 2)) % count, 0))
     out = pl.BlockSpec((block, D), lambda i, w: (i, 0))
@@ -116,22 +116,23 @@
 
 
 def mem_norm_kernel(p0, p1, p2, p3, gain_ref, conv_ref, _, low_ref, raw_ref, keep_ref):
-    for block in range(MROWS // 256):
-        rows = slice(block * 256, block * 256 + 256)
+    def norm_rows(block, carry):
+        rows = pl.ds(pl.multiple_of(block * 256, 256), 256)
         pieces = [p[rows, :] for p in (p0, p1, p2, p3)]
         normed = norm_block(pieces, gain_ref)
         for k in range(4):
             low_ref[rows, block_of(k)] = normed[k].astype(BF)
             raw_ref[rows, block_of(k)] = pieces[k]
-            if block * 256 >= CMEM:
-                start = block * 256 - CMEM
-                for j in range(2):
-                    keep_ref[k * 2 + j, start : start + 256, :] = normed[k][:, j * DH : j * DH + DH]
+            for j in range(2):
+                keep_ref[k * 2 + j, rows, :] = normed[k][:, j * DH : j * DH + DH]
+        return carry
+
+    lax.fori_loop(0, MROWS // 256, norm_rows, 0)
     for j in range(D // DH):
         lanes = slice(j * DH, j * DH + DH)
         packed = 0.0
         for t in range(RATE):
-            picked = keep_ref[j, pl.ds(t, NEWC, stride=RATE), :]
+            picked = keep_ref[j, pl.ds(CMEM + t, NEWC, stride=RATE), :]
             packed = packed + conv_ref[t : t + 1, lanes] * picked
         low_ref[MROWS:, lanes] = packed.astype(BF)
 
@@ -143,7 +144,7 @@
         grid=(1,),
         in_specs=[whole((MROWS, QUARTER))] * 4 + [whole((1, D)), whole((RATE, D)), ANY],
         out_specs=[whole((KM, D)), whole((MROWS, D))],
-        scratch_shapes=[pltpu.VMEM((D // DH, MEM, DH), F32)],
+        scratch_shapes=[pltpu.VMEM((D // DH, MROWS, DH), F32)],
         compiler_params=params(LIMIT),
         name="mem_norm",
     )(*pieces, gain, conv, earlier)
@@ -434,7 +435,7 @@
 
 
 def residual_mid(raw, o, o_got, w_out, gain, earlier):
-    block = 256
+    block = 128
     rows = lambda width: pl.BlockSpec((block, width), lambda i: (i, 0))
     return pl.pallas_call(
         mid_kernel,
@@ -464,14 +465,20 @@
     def _():
         out_ref[...] = jnp.zeros_like(out_ref)
         gx_ref[...] = jnp.zeros_like(gx_ref)
-        for (own, got), full, turned in (
-            ((x_own, x_got), x_ref, xt_ref),
-            ((c_own, c_got), c_ref, ct_ref),
-        ):
-            for j, half in enumerate((own, got)):
-                full[j * HALF : (j + 1) * HALF, :] = half[...]
-                for i in range(0, HALF, 256):
-                    turned[:, j * HALF + i : j * HALF + i + 256] = half[i : i + 256, :].T
+
+        def turn(i, carry):
+            rows = pl.ds(pl.multiple_of(i * 256, 256), 256)
+            for halves, full, turned in (
+                ((x_own, x_got), x_ref, xt_ref),
+                ((c_own, c_got), c_ref, ct_ref),
+            ):
+                for j, half in enumerate(halves):
+                    target = pl.ds(pl.multiple_of(j * HALF + i * 256, 256), 256)
+                    full[target, :] = half[rows, :]
+                    turned[:, target] = half[rows, :].T
+            return carry
+
+        lax.fori_loop(0, HALF // 256, turn, 0)
 
     for k, ref in enumerate(plain):
         @pl.when(block == k)
@@ -560,7 +567,7 @@
 
 
 def out_sum(mid, keep, got, *earlier):
-    block = 256
+    block = 128
     rows = lambda width: pl.BlockSpec((block, width), lambda i: (i, 0))
     return pl.pallas_call(
         out_sum_kernel,
@@ -594,7 +601,7 @@
 
 
 def mid_back(gx, gx_got, mid, cot, gain, w_out):
-    block = 256
+    block = 128
     rows = lambda width: pl.BlockSpec((block, width), lambda i: (i, 0))
     half = shape((HALF, HEADS * DH), BF)
     return pl.pallas_call(
@@ -631,7 +638,7 @@
 
 
 def tok_grad(g_tok, w_tok, raw, *earlier):
-    block = 256
+    block = 128
     steps, half = SEQ_LEN // block, HALF // block
     rows = lambda width: pl.BlockSpec((block, width), lambda i: ((i + half) % steps, 0))
     return pl.pallas_call(
@@ -662,7 +669,7 @@
 
 
 def input_grad(keep, got, raw, g_mid, gain, *earlier):
-    block = 256
+    block = 128
     rows = pl.BlockSpec((block, D), lambda i: (i, 0))
     return pl.pallas_call(
         input_grad_kernel,
@@ -678,21 +685,19 @@
 
 def mem_grad_kernel(g_ref, w_ref, raw_ref, gain_ref, conv_ref, *refs):
     gn_ref, gc_ref, unit_ref = refs[-3:]
-    total = jnp.zeros((1, D), F32)
-    for block in range(MROWS // 256):
-        rows = slice(block * 256, block * 256 + 256)
+    def rows_sum(block, total):
+        rows = pl.ds(pl.multiple_of(block * 256, 256), 256)
         unit, _ = center_rows(raw_ref[rows, :].astype(F32))
-        total = total + jnp.sum(nn(g_ref[rows, :], w_ref[...]) * unit, axis=0, keepdims=True)
-        if block * 256 >= CMEM:
-            start = block * 256 - CMEM
-            for j in range(D // DH):
-                unit_ref[j, start : start + 256, :] = unit[:, j * DH : j * DH + DH]
-    gn_ref[...] = total
+        for j in range(D // DH):
+            unit_ref[j, rows, :] = unit[:, j * DH : j * DH + DH]
+        return total + jnp.sum(nn(g_ref[rows, :], w_ref[...]) * unit, axis=0, keepdims=True)
+
+    gn_ref[...] = lax.fori_loop(0, MROWS // 256, rows_sum, jnp.zeros((1, D), F32))
     packed = nn(g_ref[MROWS:, :], w_ref[...])
     for j in range(D // DH):
         lanes = slice(j * DH, j * DH + DH)
         for t in range(RATE):
-            picked = unit_ref[j, pl.ds(t, NEWC, stride=RATE), :]
+            picked = unit_ref[j, pl.ds(CMEM + t, NEWC, stride=RATE), :]
             term = jnp.sum(packed[:, lanes] * picked, axis=0, keepdims=True)
             gc_ref[t : t + 1, lanes] = term * gain_ref[:, lanes]
             gn_ref[:, lanes] += conv_ref[t : t + 1, lanes] * term
@@ -708,7 +713,7 @@
         ]
         + [ANY] * len(earlier),
         out_specs=[whole((1, D)), whole((RATE, D))],
-        scratch_shapes=[pltpu.VMEM((D // DH, MEM, DH), F32)],
+        scratch_shapes=[pltpu.VMEM((D // DH, MROWS, DH), F32)],
         compiler_params=params(LIMIT),
         name="mem_grad",
     )(g_mem, w_mem, raw, gain, conv, *earlier)

time: 481 us -> 484 us (level)
  Pallas kernels: 208 us -> 216 us
  transfers between devices with their start and end apart: 59 -> 59, of which waited for: 22 -> 21; matrix products, arithmetic and copies ran while one was open for 11% -> 11% of each run, Pallas kernels for 35% -> 36%
where the time goes in v5:
time: 484 us; the launch traced here: 482 us
  Pallas kernels  216 us (45%)
  waiting for transfers between devices  126 us (26%)
  starting transfers between devices  63 us (13%)
  local copies, waits for them, and re-layouts  37.8 us (8%)
  other arithmetic  24.9 us (5%)
  matrix products  13.3 us (3%)
    ppermute x59, waiting for transfers between devices, swap(): return lax.ppermute(x, axis, [(i, i ^ distance) for i in range(n)])  126 us
    ppermute x59, starting transfers between devices, swap(): return lax.ppermute(x, axis, [(i, i ^ distance) for i in range(n)])  63 us
    pallas_call x1, Pallas kernels, feed_forward(): pl.pallas_call(ffn_kernel, out_shape=(shape((HALF, D), F32), shape((HALF,...  43.5 us
    pallas_call x1, Pallas kernels, attention_backward(): pl.pallas_call(backward_kernel, out_shape=(shape((SEQ_LEN, HEADS * 3 * DH...  36.9 us
    pallas_call x1, Pallas kernels, attention_forward(): pl.pallas_call(forward_kernel, out_shape=(shape((SEQ_LEN, HEADS * DH), BF...  25.3 us
    pallas_call x10, Pallas kernels, merge(): pl.pallas_call(functools.partial(merge_kernel, count, lanes), out_shape=(...  23.7 us
    unnamed x134, local copies, waits for them, and re-layouts  20.1 us
    dot_general x2, matrix products, nt(): lax.dot_general(a, b, (((1,), (1,)), ((), ())), preferred_element_type=F32)  13.3 us
  transfers between devices with their start and end apart: 59, of which 21 were waited for; matrix products, arithmetic and copies ran while one was open for 11% of the time, Pallas kernels for 36%

profile of v5, /device:TPU:0, one launch (start us, length us, event | category | flops | bytes accessed | tf_op | source)
XLA Modules:
  0.0 482.2 jit_solution(17351027987387334736)
XLA Ops:
  3.6 5.1 %collective-permute-start.7 = (bf16[2,5,32,256]{3,2,1,0:T(8,128)(2,1)}, bf16[2,5,32,256]{3,2,1,0:T(8,128)(2,1)}, u32[]{:S(2)}, u32[]{:S(2)}) collective-permute-start(bf16[2,5,32,256]{3,2,1,0:T(8,128)(2,1)} %get-tuple-element.223), channel_id=1, source_target_pairs={{0,6},{2,4},{4,2},{6,0},{1,7},{3,5},{5,3},{7,1},{8,14},{10,12},{12... | collective-permute-start | bytes 491528 | tf_op jit(solution)/shard_map/ppermute | solution.py:49
  14.8 20.3 %collective-permute-done.6 = bf16[2,5,32,256]{3,2,1,0:T(8,128)(2,1)} collective-permute-done((bf16[2,5,32,256]{3,2,1,0:T(8,128)(2,1)}, bf16[2,5,32,256]{3,2,1,0:T(8,128)(2,1)}, u32[]{:S(2)}, u32[]{:S(2)}) %collective-permute-start.6) | collective-permute-done | bytes 163872 | tf_op jit(solution)/shard_map/ppermute | solution.py:49
  37.1 4.9 %collective-permute-done.refs_1_.refs_2_.p1 = bf16[1024,256]{1,0:T(8,128)(2,1)S(1)} collective-permute-done((bf16[1024,256]{1,0:T(8,128)(2,1)S(1)}, bf16[1024,256]{1,0:T(8,128)(2,1)S(1)}, u32[]{:S(2)}, u32[]{:S(2)}) %collective-permute-start) | collective-permute-done | bytes 524320 | tf_op jit(solution)/shard_map/ppermute | solution.py:49
  49.2 9.5 %collective-permute-done.8 = bf16[1,4,2,5,32,256]{5,4,3,2,1,0:T(8,128)(2,1)S(1)} collective-permute-done((bf16[1,4,2,5,32,256]{5,4,3,2,1,0:T(8,128)(2,1)}, bf16[1,4,2,5,32,256]{5,4,3,2,1,0:T(8,128)(2,1)S(1)}, u32[]{:S(2)}, u32[]{:S(2)}) %collective-permute-start.8) | collective-permute-done | bytes 655392 | tf_op jit(solution)/shard_map/ppermute | solution.py:49
  59.8 9.2 %collective-permute-done.2.refs_2_.p3 = bf16[1024,256]{1,0:T(8,128)(2,1)S(1)} collective-permute-done((bf16[1024,256]{1,0:T(8,128)(2,1)}, bf16[1024,256]{1,0:T(8,128)(2,1)S(1)}, u32[]{:S(2)}, u32[]{:S(2)}) %collective-permute-start.2) | collective-permute-done | bytes 524320 | tf_op jit(solution)/shard_map/ppermute | solution.py:49
  81.0 3.1 collective-permute-start.10
  88.5 25.8 %collective-permute-done.4 = f32[2,5376]{1,0:T(2,128)} collective-permute-done((f32[2,5376]{1,0:T(2,128)S(1)}, f32[2,5376]{1,0:T(2,128)}, u32[]{:S(2)}, u32[]{:S(2)}) %collective-permute-start.4) | collective-permute-done | bytes 43040 | tf_op jit(solution)/shard_map/ppermute | solution.py:49
  130.6 5.8 %join_weights.1 = (bf16[1536,1024]{1,0:T(8,128)(2,1)}, bf16[1024,1024]{1,0:T(8,128)(2,1)}, bf16[1024,1024]{1,0:T(8,128)(2,1)}) custom-call(bf16[2,4,2,5,32,256]{5,4,3,2,1,0:T(8,128)(2,1)} %after.28.refs_0_, bf16[2,4,2,5,32,256]{5,4,3,2,1,0:T(8,128)(2,1)} %copy-done.4, bf16[2,4,2,5,32,256]{5,4,3,2,1,0:T(8,128)(2,1)} %after.30.refs_2_, ...), custom_call_target="tpu_custom_call" | custom-call | tf_op jit(solution)/shard_map/join_weights/pallas_call | solution.py:176
  136.4 7.2 %tok_norm.1 = (bf16[1024,1024]{1,0:T(8,128)(2,1)}, bf16[1024,1024]{1,0:T(8,128)(2,1)}) custom-call(s32[1]{0:T(128)} %bitcast.where, bf16[1024,256]{1,0:T(8,128)(2,1)} %copy-done.23, bf16[1024,256]{1,0:T(8,128)(2,1)} %copy-done.5, bf16[1024,256]{1,0:T(8,128)(2,1)} %copy-done.24, bf16[1024,256]{1,0:T(8,128)(2,1)} %copy-done.6, f32[1,1024]{1,0:T(1,128)} %after.29.gain_ref), custom_call_target="tpu_custom_call" | custom-call | tf_op jit(solution)/shard_map/tok_norm/pallas_call | solution.py:104
  143.6 7.7 %convolution_convert_fusion.1._.tok_ref.refs_2_ = bf16[1024,1536]{1,0:T(8,128)(2,1)} fusion(bf16[1024,1024]{1,0:T(8,128)(2,1)} %get-tuple-element.100.xt_ref, bf16[1536,1024]{1,0:T(8,128)(2,1)} %get-tuple-element.101.w_ref), kind=kOutput, calls=%fused_computation.1 | convolution fusion | flops 3222798336 | bytes 8388608 | tf_op jit(solution)/shard_map/dot_general | solution.py:40
  151.3 5.5 %mem_norm.1 = (bf16[1152,1024]{1,0:T(8,128)(2,1)}, bf16[1024,1024]{1,0:T(8,128)(2,1)}) custom-call(bf16[1024,256]{1,0:T(8,128)(2,1)} %after.31.p0, bf16[1024,256]{1,0:T(8,128)(2,1)} %collective-permute-done.16.p1, bf16[1024,256]{1,0:T(8,128)(2,1)} %copy-done.1, bf16[1024,256]{1,0:T(8,128)(2,1)} %collective-permute-done.17.p3, f32[1,1024]{1,0:T(1,128)} %bitcast.221, ...), custom_call_target="tpu_custom_call" | custom-call | tf_op jit(solution)/shard_map/mem_norm/pallas_call | solution.py:141
  156.8 5.7 %convolution_convert_fusion.mem_ref.refs_1_ = bf16[1152,1024]{1,0:T(8,128)(2,1)} fusion(bf16[1152,1024]{1,0:T(8,128)(2,1)} %get-tuple-element.102.xm_ref, bf16[1024,1024]{1,0:T(8,128)(2,1)S(1)} %copy-done.22), kind=kOutput, calls=%fused_computation | convolution fusion | flops 2417098752 | bytes 6815744 | tf_op jit(solution)/shard_map/dot_general | solution.py:40
  166.9 25.3 %attention_forward.1 = (bf16[1024,512]{1,0:T(8,128)(2,1)}, f32[4,1,1024]{2,1,0:T(1,128)}) custom-call(bf16[1024,1536]{1,0:T(8,128)(2,1)} %convolution_convert_fusion.1._.tok_ref.refs_2_, bf16[1152,1024]{1,0:T(8,128)(2,1)} %convolution_convert_fusion.mem_ref.refs_1_, f32[2,1024]{1,0:T(2,128)} %stack.93.row_ref, f32[1024,3]{1,0:T(8,128)} %copy.85.col_ref), custom_call_target="tpu_custom_call" | custom-call | flops 24999999488 | bytes 25000000 | tf_op jit(solution)/shard_map/attention_forward/pallas_call | solution.py:253
  200.1 11.9 %reconstruction.1 = (f32[4,128,1024]{2,1,0:T(8,128)}, f32[640,1024]{1,0:T(8,128)}) custom-call(bf16[1024,1536]{1,0:T(8,128)(2,1)} %convolution_convert_fusion.1._.tok_ref.refs_2_, bf16[1152,1024]{1,0:T(8,128)(2,1)} %convolution_convert_fusion.mem_ref.refs_1_, bf16[512,1024]{1,0:T(8,128)(2,1)} %copy-done.20, ...), custom_call_target="tpu_custom_call" | custom-call | flops 10000000000 | bytes 10000000 | tf_op jit(solution)/shard_map/reconstruction/pallas_call | solution.py:307
  212.8 5.7 %residual_mid.1 = (f32[512,1024]{1,0:T(8,128)}, bf16[512,1024]{1,0:T(8,128)(2,1)}) custom-call(bf16[1024,1024]{1,0:T(8,128)(2,1)} %get-tuple-element.99.raw_ref, bf16[1024,512]{1,0:T(8,128)(2,1)} %get-tuple-element.104.own_ref.o_ref, bf16[512,512]{1,0:T(8,128)(2,1)} %copy-done.27, bf16[1024,1024]{1,0:T(8,128)(2,1)} %get-tuple-element.105.w_ref, ...), custom_call_target="tpu_custom_call" | custom-call | flops 2147483648 | bytes 2147483 | tf_op jit(solution)/shard_map/residual_mid/pallas_call | solution.py:440
  218.6 4.0 collective-permute-done.27.refs_8_
  225.1 43.5 %feed_forward.1 = (f32[512,1024]{1,0:T(8,128)}, bf16[512,1024]{1,0:T(8,128)(2,1)}, f32[512,1024]{1,0:T(8,128)}, bf16[512,1024]{1,0:T(8,128)(2,1)}, bf16[2,4,256,...) custom-call(bf16[512,1024]{1,0:T(8,128)(2,1)} %get-tuple-element.108, ...), custom_call_target="tpu_custom_call" | custom-call | flops 25769803776 | bytes 25769804 | tf_op jit(solution)/shard_map/feed_forward/pallas_call | solution.py:545
  272.5 7.9 %mid_back.1 = (f32[512,1024]{1,0:T(8,128)}, bf16[512,1024]{1,0:T(8,128)(2,1)}, bf16[512,512]{1,0:T(8,128)(2,1)}, bf16[512,512]{1,0:T(8,128)(2,1)}, f32[1,1024]{1,0:T(1,128)}) custom-call(f32[512,1024]{1,0:T(8,128)} %get-tuple-element.111.gx_ref, bf16[512,1024]{1,0:T(8,128)(2,1)} %copy-done.37, f32[512,1024]{1,0:T(8,128)} %get-tuple-element.107.mid_ref, ...), custom_call_target="tpu_custom_call" | custom-call | flops 1073741824 | bytes 1073741 | tf_op jit(solution)/shard_map/mid_back/pallas_call | solution.py:607
  285.9 4.9 %out_grad.1 = (bf16[2,4,2,32,1024]{4,3,2,1,0:T(8,128)(2,1)}, bf16[2,4,2,32,1024]{4,3,2,1,0:T(8,128)(2,1)}) custom-call(bf16[1024,512]{1,0:T(8,128)(2,1)} %get-tuple-element.104.own_ref.o_ref, bf16[512,512]{1,0:T(8,128)(2,1)} %copy-done.27, bf16[512,1024]{1,0:T(8,128)(2,1)} %get-tuple-element.113.g_ref), custom_call_target="tpu_custom_call" | custom-call | tf_op jit(solution)/shard_map/out_grad/pallas_call | solution.py:767
  290.8 4.1 out_sum.1
  309.6 36.9 %attention_backward.1 = (bf16[1024,1536]{1,0:T(8,128)(2,1)}, bf16[1152,1024]{1,0:T(8,128)(2,1)}) custom-call(bf16[1024,1536]{1,0:T(8,128)(2,1)} %convolution_convert_fusion.1._.tok_ref.refs_2_, bf16[1152,1024]{1,0:T(8,128)(2,1)} %convolution_convert_fusion.mem_ref.refs_1_, bf16[512,512]{1,0:T(8,128)(2,1)} %get-tuple-element.120.own_ref, ...), custom_call_target="tpu_custom_call" | custom-call | flops 35000000512 | bytes 35000000 | tf_op jit(solution)/shard_map/attention_backward/pallas_call | solution.py:387
  346.5 10.1 %tok_grad.1 = (f32[512,1024]{1,0:T(8,128)}, bf16[512,1024]{1,0:T(8,128)(2,1)}, f32[1,1024]{1,0:T(1,128)}) custom-call(bf16[1024,1536]{1,0:T(8,128)(2,1)} %get-tuple-element.127.g_ref.gt_ref, bf16[1536,1024]{1,0:T(8,128)(2,1)} %get-tuple-element.101.w_ref, bf16[1024,1024]{1,0:T(8,128)(2,1)} %get-tuple-element.99.raw_ref, bf16[512,256]{1,0:T(8,128)(2,1)} %copy-done.28, ...), custom_call_target="tpu_custom_call" | custom-call | tf_op jit(solution)/shard_map/tok_grad/pallas_call | solution.py:644
  358.1 4.1 merge.10
  364.1 10.6 %qkv_grad.1 = (bf16[2,4,3,32,1024]{4,3,2,1,0:T(8,128)(2,1)}, bf16[2,4,3,32,1024]{4,3,2,1,0:T(8,128)(2,1)}) custom-call(bf16[1024,1536]{1,0:T(8,128)(2,1)} %get-tuple-element.127.g_ref.gt_ref, bf16[1024,1024]{1,0:T(8,128)(2,1)} %get-tuple-element.100.xt_ref, bf16[1152,1024]{1,0:T(8,128)(2,1)} %get-tuple-element.131.gm_ref.g_ref, ...), custom_call_target="tpu_custom_call" | custom-call | tf_op jit(solution)/shard_map/qkv_grad/pallas_call | solution.py:741
  378.7 7.5 %mem_grad.1 = (f32[1,1024]{1,0:T(1,128)}, f32[3,1024]{1,0:T(4,128)}) custom-call(bf16[1152,1024]{1,0:T(8,128)(2,1)} %get-tuple-element.131.gm_ref.g_ref, bf16[1024,1024]{1,0:T(8,128)(2,1)} %get-tuple-element.103.w_ref, bf16[1024,1024]{1,0:T(8,128)(2,1)} %get-tuple-element.132.raw_ref, f32[1,1024]{1,0:T(1,128)} %bitcast.222, f32[3,1024]{1,0:T(4,128)} %bitcast.212, ...), custom_call_target="tpu_custom_call" | custom-call | tf_op jit(solution)/shard_map/mem_grad/pallas_call | solution.py:707
  386.2 5.1 %input_grad.1 = (bf16[512,256]{1,0:T(8,128)(2,1)}, bf16[512,256]{1,0:T(8,128)(2,1)}, bf16[512,256]{1,0:T(8,128)(2,1)}, bf16[512,256]{1,0:T(8,128)(2,1)}) custom-call(f32[512,1024]{1,0:T(8,128)} %get-tuple-element.128.keep_ref, bf16[512,1024]{1,0:T(8,128)(2,1)} %collective-permute-done.36.got_ref, bf16[1024,1024]{1,0:T(8,128)(2,1)} %get-tuple-element.99.raw_ref, ...), custom_call_target="tpu_custom_call" | custom-call | flops 20000000000 | bytes 20000000 | tf_op jit(solution)/shard_map/input_grad/pallas_call | solution.py:674
  399.0 3.2 merge.13
  403.5 7.5 %collective-permute-done.46 = bf16[2,2,256,512]{3,2,1,0:T(8,128)(2,1)S(1)} collective-permute-done((bf16[2,2,256,512]{3,2,1,0:T(8,128)(2,1)}, bf16[2,2,256,512]{3,2,1,0:T(8,128)(2,1)S(1)}, u32[]{:S(2)}, u32[]{:S(2)}) %collective-permute-start.46) | collective-permute-done | bytes 1048608 | tf_op jit(solution)/shard_map/ppermute | solution.py:49
  416.3 6.5 %collective-permute-done.42.refs_7_ = bf16[512,256]{1,0:T(8,128)(2,1)S(1)} collective-permute-done((bf16[512,256]{1,0:T(8,128)(2,1)}, bf16[512,256]{1,0:T(8,128)(2,1)S(1)}, u32[]{:S(2)}, u32[]{:S(2)}) %collective-permute-start.42) | collective-permute-done | bytes 262176 | tf_op jit(solution)/shard_map/ppermute | solution.py:49
  435.1 11.5 %collective-permute-done.53.refs_2_ = bf16[2,256,512]{2,1,0:T(8,128)(2,1)S(1)} collective-permute-done((bf16[2,256,512]{2,1,0:T(8,128)(2,1)}, bf16[2,256,512]{2,1,0:T(8,128)(2,1)S(1)}, u32[]{:S(2)}, u32[]{:S(2)}) %collective-permute-start.53) | collective-permute-done | bytes 524320 | tf_op jit(solution)/shard_map/ppermute | solution.py:49
  458.9 7.5 %collective-permute-done.49 = bf16[2,3,32,512]{3,2,1,0:T(8,128)(2,1)S(1)} collective-permute-done((bf16[2,3,32,512]{3,2,1,0:T(8,128)(2,1)}, bf16[2,3,32,512]{3,2,1,0:T(8,128)(2,1)S(1)}, u32[]{:S(2)}, u32[]{:S(2)}) %collective-permute-start.49) | collective-permute-done | bytes 196640 | tf_op jit(solution)/shard_map/ppermute | solution.py:49
  469.6 4.6 collective-permute-done.57
  (343 shorter events, 148.5 us)
Async XLA Ops:
  3.6 31.5 %collective-permute-start.7 = (bf16[2,5,32,256]{3,2,1,0:T(8,128)(2,1)}, bf16[2,5,32,256]{3,2,1,0:T(8,128)(2,1)}, u32[]{:S(2)}, u32[]{:S(2)}) collective-permute-start(bf16[2,5,32,256]{3,2,1,0:T(8,128)(2,1)} %get-tuple-element.223), channel_id=1, source_target_pairs={{0,6},{2,4},{4,2},{6,0},{1,7},{3,5},{5,3},{7,1},{8,14},{10,12},{12... | collective-permute-start | bytes 491528 | tf_op jit(solution)/shard_map/ppermute | solution.py:49
  8.7 26.4 %collective-permute-start.5 = (bf16[2,5,32,256]{3,2,1,0:T(8,128)(2,1)}, bf16[2,5,32,256]{3,2,1,0:T(8,128)(2,1)}, u32[]{:S(2)}, u32[]{:S(2)}) collective-permute-start(bf16[2,5,32,256]{3,2,1,0:T(8,128)(2,1)} %get-tuple-element.223), channel_id=1, source_target_pairs={{0,2},{2,0},{4,6},{6,4},{1,3},{3,1},{5,7},{7,5},{8,10},{10,8},{12,... | collective-permute-start | bytes 491528 | tf_op jit(solution)/shard_map/ppermute | solution.py:49
  8.7 26.4 %collective-permute-start.6 = (bf16[2,5,32,256]{3,2,1,0:T(8,128)(2,1)}, bf16[2,5,32,256]{3,2,1,0:T(8,128)(2,1)}, u32[]{:S(2)}, u32[]{:S(2)}) collective-permute-start(bf16[2,5,32,256]{3,2,1,0:T(8,128)(2,1)} %get-tuple-element.222), channel_id=1, source_target_pairs={{0,4},{2,6},{4,0},{6,2},{1,5},{3,7},{5,1},{7,3},{8,12},{10,14},{12... | collective-permute-start | bytes 491528 | tf_op jit(solution)/shard_map/ppermute | solution.py:49
  10.2 35.1 %collective-permute-start.1 = (bf16[1024,256]{1,0:T(8,128)(2,1)}, bf16[1024,256]{1,0:T(8,128)(2,1)S(1)}, u32[]{:S(2)}, u32[]{:S(2)}) collective-permute-start(bf16[1024,256]{1,0:T(8,128)(2,1)} %get-tuple-element.217), channel_id=1, source_target_pairs={{0,4},{2,6},{4,0},{6,2},{1,5},{3,7},{5,1},{7,3},{8,12},{10,14},{12... | collective-permute-start | bytes 1572872 | tf_op jit(solution)/shard_map/ppermute | solution.py:49
  12.5 29.5 %collective-permute-start = (bf16[1024,256]{1,0:T(8,128)(2,1)S(1)}, bf16[1024,256]{1,0:T(8,128)(2,1)S(1)}, u32[]{:S(2)}, u32[]{:S(2)}) collective-permute-start(bf16[1024,256]{1,0:T(8,128)(2,1)S(1)} %get-tuple-element.218.p0), channel_id=1, source_target_pairs={{0,2},{2,0},{4,6},{6,4},{1,3},{3,1},{5,7},{7,5},{8,10},{10,8},{12,... | collective-permute-start | bytes 1572872 | tf_op jit(solution)/shard_map/ppermute | solution.py:49
  46.1 25.4 %collective-permute-start.9 = (bf16[2,256,512]{2,1,0:T(8,128)(2,1)}, bf16[2,256,512]{2,1,0:T(8,128)(2,1)S(1)}, u32[]{:S(2)}, u32[]{:S(2)}) collective-permute-start(bf16[2,256,512]{2,1,0:T(8,128)(2,1)} %after.24.refs_0_), channel_id=1, source_target_pairs={{0,4},{2,6},{4,0},{6,2},{1,5},{3,7},{5,1},{7,3},{8,12},{10,14},{12... | collective-permute-start | bytes 1572872 | tf_op jit(solution)/shard_map/ppermute | solution.py:49
  72.3 42.8 %collective-permute-start.14 = (bf16[2,4,2,5,32,256]{5,4,3,2,1,0:T(8,128)(2,1)}, bf16[2,4,2,5,32,256]{5,4,3,2,1,0:T(8,128)(2,1)S(1)}, u32[]{:S(2)}, u32[]{:S(2)}) collective-permute-start(bf16[2,4,2,5,32,256]{5,4,3,2,1,0:T(8,128)(2,1)} %after.25.refs_0_), channel_id=1, source_target_pairs={{0,16},{8,24},{16,0},{24,8},{1,17},{9,25},{17,1},{25,9},{2,18},{10... | collective-permute-start | bytes 3932168 | tf_op jit(solution)/shard_map/ppermute | solution.py:49
  79.4 35.7 %collective-permute-start.11 = (bf16[2,256,512]{2,1,0:T(8,128)(2,1)}, bf16[2,256,512]{2,1,0:T(8,128)(2,1)S(1)}, u32[]{:S(2)}, u32[]{:S(2)}) collective-permute-start(bf16[2,256,512]{2,1,0:T(8,128)(2,1)} %after.27), channel_id=1, source_target_pairs={{0,2},{2,0},{4,6},{6,4},{1,3},{3,1},{5,7},{7,5},{8,10},{10,8},{12,... | collective-permute-start | bytes 1572872 | tf_op jit(solution)/shard_map/ppermute | solution.py:49
  81.0 34.1 %collective-permute-start.10 = (bf16[1024,256]{1,0:T(8,128)(2,1)}, bf16[1024,256]{1,0:T(8,128)(2,1)S(1)}, u32[]{:S(2)}, u32[]{:S(2)}) collective-permute-start(bf16[1024,256]{1,0:T(8,128)(2,1)} %after.26), channel_id=1, source_target_pairs={{0,4},{2,6},{4,0},{6,2},{1,5},{3,7},{5,1},{7,3},{8,12},{10,14},{12... | collective-permute-start | bytes 1572872 | tf_op jit(solution)/shard_map/ppermute | solution.py:49
  84.1 31.0 %collective-permute-start.12 = (bf16[2,256,512]{2,1,0:T(8,128)(2,1)S(1)}, bf16[2,256,512]{2,1,0:T(8,128)(2,1)S(1)}, u32[]{:S(2)}, u32[]{:S(2)}) collective-permute-start(bf16[2,256,512]{2,1,0:T(8,128)(2,1)S(1)} %copy-done.9), channel_id=1, source_target_pairs={{0,2},{2,0},{4,6},{6,4},{1,3},{3,1},{5,7},{7,5},{8,10},{10,8},{12,... | collective-permute-start | bytes 1572872 | tf_op jit(solution)/shard_map/ppermute | solution.py:49
  84.5 29.7 %collective-permute-start.4 = (f32[2,5376]{1,0:T(2,128)S(1)}, f32[2,5376]{1,0:T(2,128)}, u32[]{:S(2)}, u32[]{:S(2)}) collective-permute-start(f32[2,5376]{1,0:T(2,128)S(1)} %get-tuple-element.227), channel_id=1, source_target_pairs={{0,2},{2,0},{4,6},{6,4},{1,3},{3,1},{5,7},{7,5},{8,10},{10,8},{12,... | collective-permute-start | bytes 129032 | tf_op jit(solution)/shard_map/ppermute | solution.py:49
  121.9 29.4 %collective-permute-start.16 = (bf16[1024,256]{1,0:T(8,128)(2,1)}, bf16[1024,256]{1,0:T(8,128)(2,1)}, u32[]{:S(2)}, u32[]{:S(2)}) collective-permute-start(bf16[1024,256]{1,0:T(8,128)(2,1)} %after.31.p0), channel_id=1, source_target_pairs={{0,2},{2,0},{4,6},{6,4},{1,3},{3,1},{5,7},{7,5},{8,10},{10,8},{12,... | collective-permute-start | bytes 1572872 | tf_op jit(solution)/shard_map/ppermute | solution.py:49
  123.2 28.0 %collective-permute-start.17 = (bf16[1024,256]{1,0:T(8,128)(2,1)S(1)}, bf16[1024,256]{1,0:T(8,128)(2,1)}, u32[]{:S(2)}, u32[]{:S(2)}) collective-permute-start(bf16[1024,256]{1,0:T(8,128)(2,1)S(1)} %copy-done.2), channel_id=1, source_target_pairs={{0,2},{2,0},{4,6},{6,4},{1,3},{3,1},{5,7},{7,5},{8,10},{10,8},{12,... | collective-permute-start | bytes 1572872 | tf_op jit(solution)/shard_map/ppermute | solution.py:49
  127.6 67.9 %collective-permute-start.23 = (bf16[2,4,256,512]{3,2,1,0:T(8,128)(2,1)}, bf16[2,4,256,512]{3,2,1,0:T(8,128)(2,1)}, u32[]{:S(2)}, u32[]{:S(2)}) collective-permute-start(bf16[2,4,256,512]{3,2,1,0:T(8,128)(2,1)} %pad_maximum_fusion.refs_4_), channel_id=1, source_target_pairs={{0,1},{1,0},{2,3},{3,2},{4,5},{5,4},{6,7},{7,6},{8,9},{9,8},{10,11... | collective-permute-start | bytes 6291464 | tf_op jit(solution)/shard_map/ppermute | solution.py:49
  130.0 68.6 %collective-permute-start.22 = (bf16[2,4,256,512]{3,2,1,0:T(8,128)(2,1)}, bf16[2,4,256,512]{3,2,1,0:T(8,128)(2,1)}, u32[]{:S(2)}, u32[]{:S(2)}) collective-permute-start(bf16[2,4,256,512]{3,2,1,0:T(8,128)(2,1)} %pad_maximum_fusion.refs_4_), channel_id=1, source_target_pairs={{0,16},{8,24},{16,0},{24,8},{1,17},{9,25},{17,1},{25,9},{2,18},{10... | collective-permute-start | bytes 6291464 | tf_op jit(solution)/shard_map/ppermute | solution.py:49
  162.5 31.8 %collective-permute-start.19 = (bf16[512,256]{1,0:T(8,128)(2,1)}, bf16[512,256]{1,0:T(8,128)(2,1)S(1)}, u32[]{:S(2)}, u32[]{:S(2)}) collective-permute-start(bf16[512,256]{1,0:T(8,128)(2,1)} %after.33), channel_id=1, source_target_pairs={{0,2},{2,0},{4,6},{6,4},{1,3},{3,1},{5,7},{7,5},{8,10},{10,8},{12,... | collective-permute-start | bytes 786440 | tf_op jit(solution)/shard_map/ppermute | solution.py:49
  163.4 30.9 %collective-permute-start.20 = (bf16[512,256]{1,0:T(8,128)(2,1)S(1)}, bf16[512,256]{1,0:T(8,128)(2,1)S(1)}, u32[]{:S(2)}, u32[]{:S(2)}) collective-permute-start(bf16[512,256]{1,0:T(8,128)(2,1)S(1)} %copy-done.30), channel_id=1, source_target_pairs={{0,4},{2,6},{4,0},{6,2},{1,5},{3,7},{5,1},{7,3},{8,12},{10,14},{12... | collective-permute-start | bytes 786440 | tf_op jit(solution)/shard_map/ppermute | solution.py:49
  164.9 29.4 %collective-permute-start.21 = (bf16[512,256]{1,0:T(8,128)(2,1)S(1)}, bf16[512,256]{1,0:T(8,128)(2,1)S(1)}, u32[]{:S(2)}, u32[]{:S(2)}) collective-permute-start(bf16[512,256]{1,0:T(8,128)(2,1)S(1)} %copy-done.31), channel_id=1, source_target_pairs={{0,6},{2,4},{4,2},{6,0},{1,7},{3,5},{5,3},{7,1},{8,14},{10,12},{12... | collective-permute-start | bytes 786440 | tf_op jit(solution)/shard_map/ppermute | solution.py:49
  197.1 25.4 %collective-permute-start.27 = (bf16[4,256,512]{2,1,0:T(8,128)(2,1)S(1)}, bf16[4,256,512]{2,1,0:T(8,128)(2,1)}, u32[]{:S(2)}, u32[]{:S(2)}) collective-permute-start(bf16[4,256,512]{2,1,0:T(8,128)(2,1)S(1)} %slice_bitcast_fusion), channel_id=1, source_target_pairs={{0,16},{8,24},{16,0},{24,8},{1,17},{9,25},{17,1},{25,9},{2,18},{10... | collective-permute-start | bytes 3145736 | tf_op jit(solution)/shard_map/ppermute | solution.py:49
  200.0 25.1 %collective-permute-start.26 = (bf16[4,256,512]{2,1,0:T(8,128)(2,1)S(1)}, bf16[4,256,512]{2,1,0:T(8,128)(2,1)}, u32[]{:S(2)}, u32[]{:S(2)}) collective-permute-start(bf16[4,256,512]{2,1,0:T(8,128)(2,1)S(1)} %slice_bitcast_fusion.1), channel_id=1, source_target_pairs={{0,1},{1,0},{2,3},{3,2},{4,5},{5,4},{6,7},{7,6},{8,9},{9,8},{10,11... | collective-permute-start | bytes 3145736 | tf_op jit(solution)/shard_map/ppermute | solution.py:49
  269.2 29.0 %collective-permute-start.35 = (bf16[4,256,512]{2,1,0:T(8,128)(2,1)}, bf16[4,256,512]{2,1,0:T(8,128)(2,1)S(1)}, u32[]{:S(2)}, u32[]{:S(2)}) collective-permute-start(bf16[4,256,512]{2,1,0:T(8,128)(2,1)} %get-tuple-element.126), channel_id=1, source_target_pairs={{0,16},{8,24},{16,0},{24,8},{1,17},{9,25},{17,1},{25,9},{2,18},{10... | collective-permute-start | bytes 3145736 | tf_op jit(solution)/shard_map/ppermute | solution.py:49
  269.7 33.3 %collective-permute-start.34 = (bf16[4,256,512]{2,1,0:T(8,128)(2,1)}, bf16[4,256,512]{2,1,0:T(8,128)(2,1)S(1)}, u32[]{:S(2)}, u32[]{:S(2)}) collective-permute-start(bf16[4,256,512]{2,1,0:T(8,128)(2,1)} %get-tuple-element.124), channel_id=1, source_target_pairs={{0,1},{1,0},{2,3},{3,2},{4,5},{5,4},{6,7},{7,6},{8,9},{9,8},{10,11... | collective-permute-start | bytes 3145736 | tf_op jit(solution)/shard_map/ppermute | solution.py:49
  290.8 83.9 %collective-permute-start.37 = (bf16[2,4,2,32,1024]{4,3,2,1,0:T(8,128)(2,1)}, bf16[2,4,2,32,1024]{4,3,2,1,0:T(8,128)(2,1)}, u32[]{:S(2)}, u32[]{:S(2)}) collective-permute-start(bf16[2,4,2,32,1024]{4,3,2,1,0:T(8,128)(2,1)} %get-tuple-element.114.refs_0_), channel_id=1, source_target_pairs={{0,8},{8,0},{16,24},{24,16},{1,9},{9,1},{17,25},{25,17},{2,10},{10... | collective-permute-start | bytes 3145736 | tf_op jit(solution)/shard_map/ppermute | solution.py:49
  297.4 49.1 %collective-permute-start.32 = (bf16[512,256]{1,0:T(8,128)(2,1)}, bf16[512,256]{1,0:T(8,128)(2,1)}, u32[]{:S(2)}, u32[]{:S(2)}) collective-permute-start(bf16[512,256]{1,0:T(8,128)(2,1)} %after.38), channel_id=1, source_target_pairs={{0,4},{2,6},{4,0},{6,2},{1,5},{3,7},{5,1},{7,3},{8,12},{10,14},{12... | collective-permute-start | bytes 786440 | tf_op jit(solution)/shard_map/ppermute | solution.py:49
  298.1 48.4 %collective-permute-start.33 = (bf16[512,256]{1,0:T(8,128)(2,1)}, bf16[512,256]{1,0:T(8,128)(2,1)}, u32[]{:S(2)}, u32[]{:S(2)}) collective-permute-start(bf16[512,256]{1,0:T(8,128)(2,1)} %after.39), channel_id=1, source_target_pairs={{0,6},{2,4},{4,2},{6,0},{1,7},{3,5},{5,3},{7,1},{8,14},{10,12},{12... | collective-permute-start | bytes 786440 | tf_op jit(solution)/shard_map/ppermute | solution.py:49
  303.0 53.7 %collective-permute-start.39 = (bf16[2,4,256,512]{3,2,1,0:T(8,128)(2,1)}, bf16[2,4,256,512]{3,2,1,0:T(8,128)(2,1)S(1)}, u32[]{:S(2)}, u32[]{:S(2)}) collective-permute-start(bf16[2,4,256,512]{3,2,1,0:T(8,128)(2,1)} %fusion.5.refs_1_), channel_id=1, source_target_pairs={{0,1},{1,0},{2,3},{3,2},{4,5},{5,4},{6,7},{7,6},{8,9},{9,8},{10,11... | collective-permute-start | bytes 6291464 | tf_op jit(solution)/shard_map/ppermute | solution.py:49
  308.9 47.8 %collective-permute-start.38 = (bf16[2,4,256,512]{3,2,1,0:T(8,128)(2,1)}, bf16[2,4,256,512]{3,2,1,0:T(8,128)(2,1)}, u32[]{:S(2)}, u32[]{:S(2)}) collective-permute-start(bf16[2,4,256,512]{3,2,1,0:T(8,128)(2,1)} %fusion.3.refs_0_), channel_id=1, source_target_pairs={{0,16},{8,24},{16,0},{24,8},{1,17},{9,25},{17,1},{25,9},{2,18},{10... | collective-permute-start | bytes 6291464 | tf_op jit(solution)/shard_map/ppermute | solution.py:49
  356.7 29.6 %collective-permute-start.36 = (bf16[512,1024]{1,0:T(8,128)(2,1)}, bf16[512,1024]{1,0:T(8,128)(2,1)}, u32[]{:S(2)}, u32[]{:S(2)}) collective-permute-start(bf16[512,1024]{1,0:T(8,128)(2,1)} %get-tuple-element.129.refs_6_), channel_id=1, source_target_pairs={{0,2},{2,0},{4,6},{6,4},{1,3},{3,1},{5,7},{7,5},{8,10},{10,8},{12,... | collective-permute-start | bytes 3145736 | tf_op jit(solution)/shard_map/ppermute | solution.py:49
  362.1 48.9 %collective-permute-start.46 = (bf16[2,2,256,512]{3,2,1,0:T(8,128)(2,1)}, bf16[2,2,256,512]{3,2,1,0:T(8,128)(2,1)S(1)}, u32[]{:S(2)}, u32[]{:S(2)}) collective-permute-start(bf16[2,2,256,512]{3,2,1,0:T(8,128)(2,1)} %bitcast.188), channel_id=1, source_target_pairs={{0,2},{2,0},{4,6},{6,4},{1,3},{3,1},{5,7},{7,5},{8,10},{10,8},{12,... | collective-permute-start | bytes 3145736 | tf_op jit(solution)/shard_map/ppermute | solution.py:49
  391.3 24.9 %collective-permute-start.40 = (bf16[512,256]{1,0:T(8,128)(2,1)}, bf16[512,256]{1,0:T(8,128)(2,1)S(1)}, u32[]{:S(2)}, u32[]{:S(2)}) collective-permute-start(bf16[512,256]{1,0:T(8,128)(2,1)} %get-tuple-element.140), channel_id=1, source_target_pairs={{0,2},{2,0},{4,6},{6,4},{1,3},{3,1},{5,7},{7,5},{8,10},{10,8},{12,... | collective-permute-start | bytes 786440 | tf_op jit(solution)/shard_map/ppermute | solution.py:49
  393.8 28.9 %collective-permute-start.42 = (bf16[512,256]{1,0:T(8,128)(2,1)}, bf16[512,256]{1,0:T(8,128)(2,1)S(1)}, u32[]{:S(2)}, u32[]{:S(2)}) collective-permute-start(bf16[512,256]{1,0:T(8,128)(2,1)} %get-tuple-element.142), channel_id=1, source_target_pairs={{0,6},{2,4},{4,2},{6,0},{1,7},{3,5},{5,3},{7,1},{8,14},{10,12},{12... | collective-permute-start | bytes 786440 | tf_op jit(solution)/shard_map/ppermute | solution.py:49
  414.4 32.1 %collective-permute-start.53 = (bf16[2,256,512]{2,1,0:T(8,128)(2,1)}, bf16[2,256,512]{2,1,0:T(8,128)(2,1)S(1)}, u32[]{:S(2)}, u32[]{:S(2)}) collective-permute-start(bf16[2,256,512]{2,1,0:T(8,128)(2,1)} %get-tuple-element.149), channel_id=1, source_target_pairs={{0,4},{2,6},{4,0},{6,2},{1,5},{3,7},{5,1},{7,3},{8,12},{10,14},{12... | collective-permute-start | bytes 1572872 | tf_op jit(solution)/shard_map/ppermute | solution.py:49
  (91 other events, 774.4 us)
